TPU v7x, 256 devices: a whole 4x4x8 slice. The times are simulated.
256 devices in a mesh: tok: 32 (over x, y, core), blk: 8 (over z).
Axes of the slice: x: 4, y: 4, z: 8, core: 2. Of those that a mesh axis runs over, the one named last changes fastest.
Arguments:
- attn_out: bfloat16 [32768, 1536], P(('tok', 'blk')), may hold values from -6 to 6
- resid: bfloat16 [32768, 1536], P(('tok', 'blk')), may hold values from -6 to 6
- w_o: bfloat16 [1536, 1536], replicated, may hold values from -0.15625 to 0.15625
- norm1_gain: float32 [1536], replicated, may hold values from 0.1 to 1.9
- router_w: float32 [1536, 40], replicated, may hold values from -32 to 32
- route_slot: int32 [32768, 8], P(('tok', 'blk')), may hold values from 0 to 63, all different within a row; in each aligned block of 128 rows (0 to 127, 128 to 255, ...) at most 32 rows name the same one
- slot_expert: int32 [64], replicated, may hold values from 0 to 39, as said below
- keep: int32 [32768], P(('tok', 'blk')), may hold values 0 or 1
- w_gate: bfloat16 [64, 1536, 512], P('tok', 'blk'), may hold values from -0.15625 to 0.15625
- w_up: bfloat16 [64, 1536, 512], P('tok', 'blk'), may hold values from -0.15625 to 0.15625
- w_down: bfloat16 [64, 1536, 512], P('tok', 'blk'), may hold values from -0.25 to 0.25
- norm2_gain: float32 [1536], replicated, may hold values from 0.1 to 1.9
Outputs:
- layer_out: bfloat16 [32768, 1536], P(('tok', 'blk'))
Inputs may be any that keep to these rules, and one draw needn't show every extreme that they name: `route_slot`: each row names 8 different slots; among the 128 rows of one device (aligned blocks of rows), no slot is named more than 32 times, a bound that some block reaches. `slot_expert`: every expert is named by one slot or more.
All inputs are finite; a program needn't handle non-finite values. No bound on the sum of `keep` on one device may be relied on, other than what follows from the above.
Results may differ from a plain program's by a relative error of at most 0.0099.
Values may be sent and summed in bfloat16 or wider, within the bound.
No kernel may reach another device: no remote copies, remote signals or barrier semaphores. Data moves between devices by JAX's collectives and lax.ppermute only.
A program may use at most 128 MiB of HBM per device.

v0:
```python
import functools

import jax
import jax.numpy as jnp
from jax import lax
from jax.experimental import pallas as pl
from jax.experimental.pallas import tpu as pltpu
from jax.sharding import Mesh
from jax.sharding import PartitionSpec as P

EPS = 1e-05
D = 1536
FF = 512
TOP = 8
SLOTS = 64
ROWS = 128
CAP = 32
BLOCKS = 16
LOCAL = 4
CHUNK = D // 8
GROUP = 2 * CHUNK
F32 = jnp.float32
BF16 = jnp.bfloat16
MIB = 1024 * 1024


def params(mib, *semantics):
    return pltpu.CompilerParams(
        dimension_semantics=semantics or None, vmem_limit_bytes=mib * MIB
    )


PLANS = (("x", "y", 1, 3), ("x", "y", 3, 1), ("y", "x", 1, 3), ("y", "x", 3, 1))


def block_at(plan, x, y, j):
    big, small, first, other = plan
    bit = lambda n: (j >> n) & 1
    low = bit(0) * other ^ bit(1) * first
    high = bit(2) * other ^ bit(3) * first
    if big == "x":
        return 4 * (x ^ high) + (y ^ low)
    return 4 * (x ^ low) + (y ^ high)


def each(count, unroll, step):
    def run(i, carry):
        step(i)
        return carry

    lax.fori_loop(0, count, run, 0, unroll=unroll)


def links(turn):
    return [(i, i ^ turn) for i in range(4)]


def entry_kernel(
    attn_ref, resid_ref, wo_ref, gain_ref, router_ref, route_ref, expert_ref, keep_ref,
    hidden_ref, rows_ref,
):
    step = pl.program_id(0)
    width = wo_ref.shape[1]
    cols = pl.ds(step * width, width)
    hidden_ref[:, cols] = resid_ref[...].astype(F32) + jnp.dot(
        attn_ref[...], wo_ref[...], preferred_element_type=F32
    )

    @pl.when(step == pl.num_programs(0) - 1)
    def _():
        values = hidden_ref[...]
        mean_sq = jnp.mean(values * values, axis=-1, keepdims=True)
        normed = (values * lax.rsqrt(mean_sq + EPS) * gain_ref[...]).astype(BF16)
        logits = lax.dot_general(
            router_ref[...], normed.astype(F32), (((1,), (1,)), ((), ())),
            precision=lax.Precision.HIGHEST, preferred_element_type=F32,
        )
        experts = logits.shape[0]
        pick = lax.broadcasted_iota(jnp.int32, (experts, SLOTS), 0) == expert_ref[...]
        by_slot = lax.dot_general(
            pick.astype(F32), logits, (((0,), (0,)), ((), ())),
            precision=lax.Precision.HIGHEST, preferred_element_type=F32,
        )
        slot = lax.broadcasted_iota(jnp.int32, (SLOTS, ROWS), 0)
        named = slot == route_ref[0:1]
        for k in range(1, TOP):
            named = named | (slot == route_ref[k : k + 1])
        top = jnp.max(jnp.where(named, by_slot, -jnp.inf), axis=0, keepdims=True)
        grown = jnp.where(named, jnp.exp(jnp.where(named, by_slot - top, 0.0)), 0.0)
        probs = grown / jnp.sum(grown, axis=0, keepdims=True)
        live = jnp.where(keep_ref[...] > 0, probs, 0.0).reshape(BLOCKS, LOCAL, ROWS)
        for group in range(LOCAL):
            rows_ref[group, :ROWS] = normed[:, group * GROUP : (group + 1) * GROUP]
            rest = live[:, group]
            for n in range(3):
                part = rest.astype(BF16)
                rows_ref[group, ROWS:, n * ROWS : (n + 1) * ROWS] = part
                rest = rest - part.astype(F32)


def entry(attn_out, resid, w_o, gain, router_w, route_slot, slot_expert, keep):
    steps = 6
    width = D // steps
    whole = lambda shape: pl.BlockSpec(shape, lambda i: (0,) * len(shape))
    return pl.pallas_call(
        entry_kernel,
        grid=(steps,),
        in_specs=[
            whole((ROWS, D)),
            pl.BlockSpec((ROWS, width), lambda i: (0, i)),
            pl.BlockSpec((D, width), lambda i: (0, i)),
            whole(gain.shape),
            whole(router_w.shape),
            whole(route_slot.shape),
            whole(slot_expert.shape),
            whole(keep.shape),
        ],
        out_specs=[whole((ROWS, D)), whole((LOCAL, ROWS + BLOCKS, GROUP))],
        out_shape=[
            jax.ShapeDtypeStruct((ROWS, D), F32),
            jax.ShapeDtypeStruct((LOCAL, ROWS + BLOCKS, GROUP), BF16),
        ],
        compiler_params=params(16, "arbitrary"),
        name="entry",
    )(attn_out, resid, w_o, gain, router_w, route_slot, slot_expert, keep)


def compact_kernel(place_ref, *refs):
    row_refs = refs[:8]
    packed_ref, spread_ref, scale_ref, pick_ref, weight_ref = refs[8:]
    x, y = place_ref[0], place_ref[1]
    half = BLOCKS // 2
    earlier = (
        lax.broadcasted_iota(jnp.int32, (ROWS, ROWS), 0)
        < lax.broadcasted_iota(jnp.int32, (ROWS, ROWS), 1)
    ).astype(BF16)
    rank = lax.broadcasted_iota(jnp.int32, (CAP, ROWS), 0).astype(F32)
    mine = lax.broadcasted_iota(jnp.int32, (BLOCKS, GROUP), 0) == 4 * x + y

    def fetch(ref, group, start, i):
        b = block_at(PLANS[group], x, y, start + i)
        parts = jnp.where(mine, ref[i, ROWS:].astype(F32), 0.0)
        parts = jnp.sum(parts, axis=0, keepdims=True)
        weight_ref[b, group : group + 1] = (
            parts[:, :ROWS] + parts[:, ROWS : 2 * ROWS] + parts[:, 2 * ROWS :]
        )

    def choose(b):
        weight = weight_ref[b]
        hit = weight > 0.0
        place = jnp.dot(hit.astype(BF16), earlier, preferred_element_type=F32)
        place = jnp.where(hit, place, -1.0)
        picks = [rank == place[s : s + 1] for s in range(LOCAL)]
        for s in range(LOCAL):
            scale_ref[s, b] = jnp.sum(
                jnp.where(picks[s], weight[s : s + 1], 0.0), axis=1, keepdims=True
            )
        pick = jnp.concatenate([p.astype(F32) for p in picks], axis=0)
        spread_ref[b] = jnp.transpose(pick).astype(BF16)
        pick_ref[b] = pick.astype(BF16)

    def pack(ref, group, start, i):
        b = block_at(PLANS[group], x, y, start + i)
        packed = jnp.dot(pick_ref[b], ref[i, :ROWS], preferred_element_type=F32).astype(BF16)
        packed_ref[:, b, :, group * GROUP : (group + 1) * GROUP] = packed.reshape(
            LOCAL, CAP, GROUP
        )

    for n, ref in enumerate(row_refs):
        each(half, 2, functools.partial(fetch, ref, n // 2, n % 2 * half))
    each(BLOCKS, 2, choose)
    for n, ref in enumerate(row_refs):
        each(half, 2, functools.partial(pack, ref, n // 2, n % 2 * half))


def compact(place, rows):
    vmem = pl.BlockSpec(memory_space=pltpu.VMEM)
    return pl.pallas_call(
        compact_kernel,
        in_specs=[pl.BlockSpec(memory_space=pltpu.SMEM)] + [vmem] * len(rows),
        out_specs=[vmem] * 3,
        out_shape=[
            jax.ShapeDtypeStruct((LOCAL, BLOCKS, CAP, D), BF16),
            jax.ShapeDtypeStruct((BLOCKS, ROWS, LOCAL * CAP), BF16),
            jax.ShapeDtypeStruct((LOCAL, BLOCKS, CAP, 1), F32),
        ],
        scratch_shapes=[
            pltpu.VMEM((BLOCKS, LOCAL * CAP, ROWS), BF16),
            pltpu.VMEM((BLOCKS, LOCAL, ROWS), F32),
        ],
        compiler_params=params(24),
        name="compact",
    )(place, *rows)


def hidden_units_kernel(packed_ref, gate_ref, up_ref, act_ref):
    rows = packed_ref[0].reshape(BLOCKS * CAP, D)
    width = 256

    def run(i):
        cols = pl.ds(pl.multiple_of(i * width, width), width)
        w_gate = gate_ref[0, :, 0, 0, :, cols].reshape(D, width)
        w_up = up_ref[0, :, 0, 0, :, cols].reshape(D, width)
        gate = jnp.dot(rows, w_gate, preferred_element_type=F32)
        up = jnp.dot(rows, w_up, preferred_element_type=F32)
        act_ref[0, :, cols] = (gate / (1.0 + jnp.exp(-gate)) * up).astype(BF16)

    each(FF // width, 1, run)


def hidden_units(packed, weights):
    def block(which):
        return pl.BlockSpec((1, 8, 1, 1, CHUNK, FF), lambda s: (s // 2, 0, which, s % 2, 0, 0))

    return pl.pallas_call(
        hidden_units_kernel,
        grid=(LOCAL,),
        in_specs=[pl.BlockSpec((1, BLOCKS, CAP, D), lambda s: (s, 0, 0, 0)), block(0), block(1)],
        out_specs=pl.BlockSpec((1, BLOCKS * CAP, FF), lambda s: (s, 0, 0)),
        out_shape=jax.ShapeDtypeStruct((LOCAL, BLOCKS * CAP, FF), BF16),
        compiler_params=params(24, "arbitrary"),
        name="hidden_units",
    )(packed, weights, weights)


def spread_kernel(plan, place_ref, act_ref, scale_ref, spread_ref, *refs):
    down_refs, (send_ref, keep_ref, part_ref) = refs[:-3], refs[-3:]
    x, y, core = place_ref[0], place_ref[1], place_ref[2]
    half = BLOCKS // 2
    for flip in range(2):
        for q in range(2):
            if len(down_refs) == 4:
                pieces = [down_refs[flip][q], down_refs[2 + flip][q]]
            else:
                pieces = [down_refs[0][2 * flip + q], down_refs[1][2 * (1 - flip) + q]]
            slot = 2 * (core ^ flip) + q
            part = lax.dot_general(
                act_ref[slot], jnp.concatenate(pieces), (((1,), (1,)), ((), ())),
                preferred_element_type=F32,
            )
            scale = scale_ref[slot].reshape(BLOCKS * CAP, 1)
            part_ref[:, slot] = (part * scale).astype(BF16).reshape(BLOCKS, CAP, GROUP)

    def back(out_ref, start, i):
        b = block_at(plan, x, y, start + i)
        rows = part_ref[b].reshape(LOCAL * CAP, GROUP)
        out_ref[i] = jnp.dot(spread_ref[b], rows, preferred_element_type=F32).astype(BF16)

    each(half, 2, functools.partial(back, keep_ref, 0))
    each(half, 2, functools.partial(back, send_ref, half))


def spread_rows(place, act, scale, spread, down, group):
    half = BLOCKS // 2
    vmem = pl.BlockSpec(memory_space=pltpu.VMEM)
    return pl.pallas_call(
        functools.partial(spread_kernel, PLANS[group]),
        in_specs=[pl.BlockSpec(memory_space=pltpu.SMEM)] + [vmem] * (3 + len(down)),
        out_specs=[vmem, vmem],
        scratch_shapes=[pltpu.VMEM((BLOCKS, LOCAL, CAP, GROUP), BF16)],
        out_shape=[jax.ShapeDtypeStruct((half, ROWS, GROUP), BF16)] * 2,
        compiler_params=params(16),
        name="spread",
    )(place, act, scale, spread, *down)


def closing_kernel(place_ref, hidden_ref, gain_ref, *refs):
    parts, (out_ref, moe_ref) = refs[:-2], refs[-2:]
    core, z = place_ref[2], place_ref[3]
    step = 1 - 2 * core
    each_group = len(parts) // LOCAL
    for g in range(LOCAL):
        total = sum(ref[...].astype(F32) for ref in parts[g * each_group : (g + 1) * each_group])
        ends = (z, z + 4) if g == 0 else (z - g * step, z + g * step)
        for n, end in enumerate(ends):
            moe_ref[end & 7] = total[:, n * CHUNK : (n + 1) * CHUNK]
    moe = jnp.concatenate([moe_ref[i] for i in range(8)], axis=1)
    mixed = hidden_ref[...] + moe
    mean_sq = jnp.mean(mixed * mixed, axis=-1, keepdims=True)
    out_ref[...] = (mixed * lax.rsqrt(mean_sq + EPS) * gain_ref[...]).astype(BF16)


def closing(place, hidden, gain, parts):
    vmem = pl.BlockSpec(memory_space=pltpu.VMEM)
    return pl.pallas_call(
        closing_kernel,
        in_specs=[pl.BlockSpec(memory_space=pltpu.SMEM)] + [vmem] * (2 + len(parts)),
        out_specs=vmem,
        out_shape=jax.ShapeDtypeStruct((ROWS, D), BF16),
        scratch_shapes=[pltpu.VMEM((8, ROWS, CHUNK), F32)],
        compiler_params=params(8),
        name="closing",
    )(place, hidden, gain, *parts)


def behind(value, *earlier):
    return lax.optimization_barrier((value, *earlier))[0]


def spread_out(rows, own):
    axes = ("core", "blk")
    swap = [(8 * c + z, 8 * (1 - c) + z) for c in range(2) for z in range(8)]
    hop = [(z, (z + 1) % 8) for z in range(8)] + [(8 + z, 8 + (z - 1) % 8) for z in range(8)]
    held = [rows[group][None] for group in range(LOCAL)]
    block, blocks = None, []
    for step in range(4):
        got = []
        for group, (big, small, first, other) in enumerate(PLANS):
            axis = small if step < 2 else big
            turn = first if step % 2 else other
            got.append(lax.ppermute(held[group], axis, links(turn)))
        if step == 0:
            twin = lax.ppermute(behind(own, rows), axes, swap)
            block = jnp.concatenate([own, twin])
        if step < 3:
            held = [jnp.concatenate(both) for both in zip(held, got)]
            block = lax.ppermute(behind(block, *held), axes, hop)
            blocks.append(block)
    last = lax.ppermute(behind(block[:2], *got), axes, hop)
    *pairs, twin_last = [
        lax.ppermute(behind(block, *got), axes, swap) for block in (*blocks, last)
    ]
    downs = [(own, twin, last, twin_last), *zip(blocks, pairs)]
    return [half for both in zip(held, got) for half in both], downs


def add(a, b):
    return (a.astype(F32) + b.astype(F32)).astype(BF16)


def body(
    attn_out, resid, w_o, norm1_gain, router_w, route_slot, slot_expert, keep,
    w_gate, w_up, w_down, norm2_gain,
):
    joined = jnp.stack([w_gate, w_up])
    weights = lax.all_gather(joined, ("core", "blk"), axis=0, tiled=False)
    weights = weights.reshape(2, 8, 2, 2, CHUNK, FF)
    weights = pltpu.with_memory_space_constraint(weights, pltpu.HBM)

    hidden, outgoing = entry(
        attn_out, resid, w_o, norm1_gain.reshape(1, D), router_w.T, route_slot.T,
        slot_expert.reshape(1, SLOTS), keep.reshape(1, ROWS),
    )
    place = jnp.stack([lax.axis_index(name) for name in ("x", "y", "core", "blk")])
    place = place.astype(jnp.int32)
    rows, downs = spread_out(outgoing, w_down)
    packed, spread, scale = compact(place, rows)
    act = hidden_units(packed, weights)

    parts = []
    for group, (big, small, first, other) in enumerate(PLANS):
        send, kept = spread_rows(place, act, scale, spread, downs[group], group)
        got = lax.ppermute(send, big, links(first))
        send, kept = add(kept[4:], got[4:]), add(kept[:4], got[:4])
        got = lax.ppermute(send, big, links(other))
        sums = [add(kept[i], got[i]) for i in range(4)]
        turns = (other, first, first ^ other)
        parts += [sums[0]] + [
            lax.ppermute(sums[i + 1], small, links(turn)) for i, turn in enumerate(turns)
        ]
    return closing(place, hidden, norm2_gain.reshape(1, D), parts)


def solution(mesh):
    fine = Mesh(mesh.devices.reshape(4, 4, 2, 8), ("x", "y", "core", "blk"))
    rows = P(("x", "y", "core", "blk"), None)
    slots = P(("x", "y", "core"), "blk", None)
    placed = (
        rows, rows, P(), P(), P(), rows, P(), P(("x", "y", "core", "blk")),
        slots, slots, slots, P(),
    )
    return jax.shard_map(body, mesh=fine, in_specs=placed, out_specs=rows, check_vma=False)
```

profile of v0, /device:TPU:6, one launch (start us, length us, event | category | flops | bytes accessed | tf_op | source)
XLA Modules:
  0.0 237.6 jit_solution(5208245284099281207)
XLA Ops:
  6.5 2.1 pad_maximum_fusion.4
  9.4 2.3 copy-done.2
  16.7 3.4 %entry.1 = (f32[128,1536]{1,0:T(8,128)S(1)}, bf16[4,144,384]{2,1,0:T(8,128)(2,1)S(1)}) custom-call(bf16[128,1536]{1,0:T(8,128)(2,1)S(1)} %copy-done.21, bf16[128,1536]{1,0:T(8,128)(2,1)S(1)} %copy-done.22, bf16[1536,1536]{1,0:T(8,128)(2,1)S(1)} %copy-done.2, f32[1,1536]{1,0:T(1,128)S(1)} %reshape.79.gain_ref, f32[40,1536]{1,0:T(8,128)S(1)} %bitcast.43, ...), custom_call_target="tpu_custom_call" | custom-call | tf_op jit(solution)/shard_map/entry/pallas_call | solution.py:105
  23.2 2.2 collective-permute-start
  25.4 2.4 collective-permute-done.8
  34.6 2.2 collective-permute-start.5
  36.7 3.1 %collective-permute-done.13 = bf16[2,144,384]{2,1,0:T(8,128)(2,1)S(1)} collective-permute-done((bf16[2,144,384]{2,1,0:T(8,128)(2,1)S(1)}, bf16[2,144,384]{2,1,0:T(8,128)(2,1)S(1)}, u32[]{:S(2)}, u32[]{:S(2)}) %collective-permute-start.13) | collective-permute-done | bytes 221216 | tf_op jit(solution)/shard_map/ppermute | solution.py:311
  41.1 2.3 collective-permute-start.10
  45.0 17.1 %collective-permute-done.17.refs_0_ = bf16[4,192,512]{2,1,0:T(8,128)(2,1)} collective-permute-done((bf16[4,192,512]{2,1,0:T(8,128)(2,1)S(1)}, bf16[4,192,512]{2,1,0:T(8,128)(2,1)}, u32[]{:S(2)}, u32[]{:S(2)}) %collective-permute-start.17) | collective-permute-done | bytes 786464 | tf_op jit(solution)/shard_map/ppermute | solution.py:317
  64.3 2.3 collective-permute-start.15
  68.5 7.8 %collective-permute-done.2 = bf16[4,144,384]{2,1,0:T(8,128)(2,1)S(1)} collective-permute-done((bf16[4,144,384]{2,1,0:T(8,128)(2,1)S(1)}, bf16[4,144,384]{2,1,0:T(8,128)(2,1)S(1)}, u32[]{:S(2)}, u32[]{:S(2)}) %collective-permute-start.2) | collective-permute-done | bytes 442400 | tf_op jit(solution)/shard_map/ppermute | solution.py:311
  77.4 15.0 %collective-permute-done.18.refs_0_ = bf16[4,192,512]{2,1,0:T(8,128)(2,1)} collective-permute-done((bf16[4,192,512]{2,1,0:T(8,128)(2,1)}, bf16[4,192,512]{2,1,0:T(8,128)(2,1)}, u32[]{:S(2)}, u32[]{:S(2)}) %collective-permute-start.18) | collective-permute-done | bytes 786464 | tf_op jit(solution)/shard_map/ppermute | solution.py:317
  98.1 13.3 %collective-permute-done.19.refs_0_ = bf16[4,192,512]{2,1,0:T(8,128)(2,1)} collective-permute-done((bf16[4,192,512]{2,1,0:T(8,128)(2,1)}, bf16[4,192,512]{2,1,0:T(8,128)(2,1)}, u32[]{:S(2)}, u32[]{:S(2)}) %collective-permute-start.19) | collective-permute-done | bytes 786464 | tf_op jit(solution)/shard_map/ppermute | solution.py:317
  119.0 9.7 %compact.1 = (bf16[4,16,32,1536]{3,2,1,0:T(8,128)(2,1)S(1)}, bf16[16,128,128]{2,1,0:T(8,128)(2,1)S(1)}, f32[4,16,32,1]{3,2,1,0:T(8,128)S(1)}) custom-call(s32[4]{0:T(128)S(1)} %pad_add_fusion.place_ref, bf16[8,144,384]{2,1,0:T(8,128)(2,1)S(1)} %copy-done.6, bf16[8,144,384]{2,1,0:T(8,128)(2,1)S(1)} %copy-done.18, bf16[8,144,384]{2,1,0:T(8,128)(2,1)S(1)} %copy-done.4, ...), custom_call_target="tpu_custom_call" | custom-call | tf_op jit(solution)/shard_map/compact/pallas_call | solution.py:178
  128.8 2.6 %copy-done = bf16[4,16,32,1536]{3,2,1,0:T(8,128)(2,1)} copy-done((bf16[4,16,32,1536]{3,2,1,0:T(8,128)(2,1)}, bf16[4,16,32,1536]{3,2,1,0:T(8,128)(2,1)S(1)}, u32[]{:S(2)}) %copy-start) | copy-done | bytes 6291480
  132.5 2.8 %copy-done.1 = bf16[4,16,32,1536]{3,2,1,0:T(8,128)(2,1)S(1)} copy-done((bf16[4,16,32,1536]{3,2,1,0:T(8,128)(2,1)S(1)}, bf16[4,16,32,1536]{3,2,1,0:T(8,128)(2,1)}, u32[]{:S(2)}) %copy-start.1) | copy-done | bytes 6291480
  135.3 10.5 %hidden_units.1.act_ref = bf16[4,512,512]{2,1,0:T(8,128)(2,1)S(1)} custom-call(bf16[4,16,32,1536]{3,2,1,0:T(8,128)(2,1)S(1)} %copy-done.1, bf16[2,8,2,2,192,512]{5,4,3,2,1,0:T(8,128)(2,1)} %bitcast.47, bf16[2,8,2,2,192,512]{5,4,3,2,1,0:T(8,128)(2,1)} %bitcast.48), custom_call_target="tpu_custom_call" | custom-call | tf_op jit(solution)/shard_map/hidden_units/pallas_call | solution.py:215
  145.8 4.2 %spread.7 = (bf16[8,128,384]{2,1,0:T(8,128)(2,1)S(1)}, bf16[8,128,384]{2,1,0:T(8,128)(2,1)S(1)}) custom-call(s32[4]{0:T(128)S(1)} %pad_add_fusion.place_ref, bf16[4,512,512]{2,1,0:T(8,128)(2,1)S(1)} %hidden_units.1.act_ref, f32[4,16,32,1]{3,2,1,0:T(8,128)S(1)} %get-tuple-element.30.scale_ref, bf16[16,128,128]{2,1,0:T(8,128)(2,1)S(1)} %get-tuple-element.31.spread_ref, ...), custom_call_target="tpu_custom_call" | custom-call | tf_op jit(solution)/shard_map/spread/pallas_call | solution.py:256
  150.0 2.8 %collective-permute-start.40 = (bf16[8,128,384]{2,1,0:T(8,128)(2,1)S(1)}, bf16[8,128,384]{2,1,0:T(8,128)(2,1)S(1)}, u32[]{:S(2)}, u32[]{:S(2)}) collective-permute-start(bf16[8,128,384]{2,1,0:T(8,128)(2,1)S(1)} %get-tuple-element.48), channel_id=1, source_target_pairs={{0,48},{16,32},{32,16},{48,0},{1,49},{17,33},{33,17},{49,1},{2,50}... | collective-permute-start | bytes 2359304 | tf_op jit(solution)/shard_map/ppermute | solution.py:353
  152.9 4.2 %spread.6 = (bf16[8,128,384]{2,1,0:T(8,128)(2,1)S(1)}, bf16[8,128,384]{2,1,0:T(8,128)(2,1)S(1)}) custom-call(s32[4]{0:T(128)S(1)} %pad_add_fusion.place_ref, bf16[4,512,512]{2,1,0:T(8,128)(2,1)S(1)} %hidden_units.1.act_ref, f32[4,16,32,1]{3,2,1,0:T(8,128)S(1)} %get-tuple-element.30.scale_ref, bf16[16,128,128]{2,1,0:T(8,128)(2,1)S(1)} %get-tuple-element.31.spread_ref, ...), custom_call_target="tpu_custom_call" | custom-call | tf_op jit(solution)/shard_map/spread/pallas_call | solution.py:256
  158.5 4.2 %spread.5 = (bf16[8,128,384]{2,1,0:T(8,128)(2,1)S(1)}, bf16[8,128,384]{2,1,0:T(8,128)(2,1)S(1)}) custom-call(s32[4]{0:T(128)S(1)} %pad_add_fusion.place_ref, bf16[4,512,512]{2,1,0:T(8,128)(2,1)S(1)} %hidden_units.1.act_ref, f32[4,16,32,1]{3,2,1,0:T(8,128)S(1)} %get-tuple-element.30.scale_ref, bf16[16,128,128]{2,1,0:T(8,128)(2,1)S(1)} %get-tuple-element.31.spread_ref, ...), custom_call_target="tpu_custom_call" | custom-call | tf_op jit(solution)/shard_map/spread/pallas_call | solution.py:256
  162.7 9.7 %collective-permute-start.28 = (bf16[8,128,384]{2,1,0:T(8,128)(2,1)S(1)}, bf16[8,128,384]{2,1,0:T(8,128)(2,1)S(1)}, u32[]{:S(2)}, u32[]{:S(2)}) collective-permute-start(bf16[8,128,384]{2,1,0:T(8,128)(2,1)S(1)} %get-tuple-element.42), channel_id=1, source_target_pairs={{0,192},{64,128},{128,64},{192,0},{1,193},{65,129},{129,65},{193,1... | collective-permute-start | bytes 2359304 | tf_op jit(solution)/shard_map/ppermute | solution.py:353
  172.5 3.4 %spread.4 = (bf16[8,128,384]{2,1,0:T(8,128)(2,1)S(1)}, bf16[8,128,384]{2,1,0:T(8,128)(2,1)S(1)}) custom-call(s32[4]{0:T(128)S(1)} %pad_add_fusion.place_ref, bf16[4,512,512]{2,1,0:T(8,128)(2,1)S(1)} %hidden_units.1.act_ref, f32[4,16,32,1]{3,2,1,0:T(8,128)S(1)} %get-tuple-element.30.scale_ref, bf16[16,128,128]{2,1,0:T(8,128)(2,1)S(1)} %get-tuple-element.31.spread_ref, ...), custom_call_target="tpu_custom_call" | custom-call | tf_op jit(solution)/shard_map/spread/pallas_call | solution.py:256
  179.6 13.0 %collective-permute-done.28 = bf16[8,128,384]{2,1,0:T(8,128)(2,1)S(1)} collective-permute-done((bf16[8,128,384]{2,1,0:T(8,128)(2,1)S(1)}, bf16[8,128,384]{2,1,0:T(8,128)(2,1)S(1)}, u32[]{:S(2)}, u32[]{:S(2)}) %collective-permute-start.28) | collective-permute-done | bytes 786464 | tf_op jit(solution)/shard_map/ppermute | solution.py:353
  192.9 2.7 %collective-permute-done.22 = bf16[8,128,384]{2,1,0:T(8,128)(2,1)S(1)} collective-permute-done((bf16[8,128,384]{2,1,0:T(8,128)(2,1)S(1)}, bf16[8,128,384]{2,1,0:T(8,128)(2,1)S(1)}, u32[]{:S(2)}, u32[]{:S(2)}) %collective-permute-start.22) | collective-permute-done | bytes 786464 | tf_op jit(solution)/shard_map/ppermute | solution.py:353
  195.8 3.6 %collective-permute-start.23 = (bf16[4,128,384]{2,1,0:T(8,128)(2,1)S(1)}, bf16[4,128,384]{2,1,0:T(8,128)(2,1)S(1)}, u32[]{:S(2)}, u32[]{:S(2)}) collective-permute-start(bf16[4,128,384]{2,1,0:T(8,128)(2,1)S(1)} %get-tuple-element.56), channel_id=1, source_target_pairs={{0,192},{64,128},{128,64},{192,0},{1,193},{65,129},{129,65},{193,1... | collective-permute-start | bytes 1179656 | tf_op jit(solution)/shard_map/ppermute | solution.py:355
  200.2 3.5 %collective-permute-start.44 = (bf16[128,384]{1,0:T(8,128)(2,1)S(1)}, bf16[128,384]{1,0:T(8,128)(2,1)S(1)}, u32[]{:S(2)}, u32[]{:S(2)}) collective-permute-start(bf16[128,384]{1,0:T(8,128)(2,1)S(1)} %get-tuple-element.57), channel_id=1, source_target_pairs={{0,128},{64,192},{128,0},{192,64},{1,129},{65,193},{129,1},{193,65... | collective-permute-start | bytes 294920 | tf_op jit(solution)/shard_map/ppermute | solution.py:359
  204.9 2.6 %collective-permute-start.36 = (bf16[128,384]{1,0:T(8,128)(2,1)S(1)}, bf16[128,384]{1,0:T(8,128)(2,1)S(1)}, u32[]{:S(2)}, u32[]{:S(2)}) collective-permute-start(bf16[128,384]{1,0:T(8,128)(2,1)S(1)} %get-tuple-element.63), channel_id=1, source_target_pairs={{0,192},{64,128},{128,64},{192,0},{1,193},{65,129},{129,65},{193,1... | collective-permute-start | bytes 294920 | tf_op jit(solution)/shard_map/ppermute | solution.py:359
  207.6 3.2 %collective-permute-done.23 = bf16[4,128,384]{2,1,0:T(8,128)(2,1)S(1)} collective-permute-done((bf16[4,128,384]{2,1,0:T(8,128)(2,1)S(1)}, bf16[4,128,384]{2,1,0:T(8,128)(2,1)S(1)}, u32[]{:S(2)}, u32[]{:S(2)}) %collective-permute-start.23) | collective-permute-done | bytes 393248 | tf_op jit(solution)/shard_map/ppermute | solution.py:355
  210.8 5.2 %collective-permute-start.38 = (bf16[128,384]{1,0:T(8,128)(2,1)S(1)}, bf16[128,384]{1,0:T(8,128)(2,1)S(1)}, u32[]{:S(2)}, u32[]{:S(2)}) collective-permute-start(bf16[128,384]{1,0:T(8,128)(2,1)S(1)} %get-tuple-element.61), channel_id=1, source_target_pairs={{0,128},{64,192},{128,0},{192,64},{1,129},{65,193},{129,1},{193,65... | collective-permute-start | bytes 294920 | tf_op jit(solution)/shard_map/ppermute | solution.py:359
  222.0 3.0 %collective-permute-start.26 = (bf16[128,384]{1,0:T(8,128)(2,1)S(1)}, bf16[128,384]{1,0:T(8,128)(2,1)S(1)}, u32[]{:S(2)}, u32[]{:S(2)}) collective-permute-start(bf16[128,384]{1,0:T(8,128)(2,1)S(1)} %get-tuple-element.69), channel_id=1, source_target_pairs={{0,32},{16,48},{32,0},{48,16},{1,33},{17,49},{33,1},{49,17},{2,34}... | collective-permute-start | bytes 294920 | tf_op jit(solution)/shard_map/ppermute | solution.py:359
  226.1 2.5 %collective-permute-done.26.refs_3_ = bf16[128,384]{1,0:T(8,128)(2,1)S(1)} collective-permute-done((bf16[128,384]{1,0:T(8,128)(2,1)S(1)}, bf16[128,384]{1,0:T(8,128)(2,1)S(1)}, u32[]{:S(2)}, u32[]{:S(2)}) %collective-permute-start.26) | collective-permute-done | bytes 98336 | tf_op jit(solution)/shard_map/ppermute | solution.py:359
  (152 shorter events, 54.7 us)
Async XLA Ops:
  6.5 125.9 %all-gather.3.cloned.1.call-start = ((), (), s32[]{:S(2)}) async-start(), calls=%async_computation | async-start | bytes 13369344 | tf_op jit(solution)/shard_map/all_gather | solution.py:336
  29.3 32.8 %collective-permute-start.17 = (bf16[4,192,512]{2,1,0:T(8,128)(2,1)S(1)}, bf16[4,192,512]{2,1,0:T(8,128)(2,1)}, u32[]{:S(2)}, u32[]{:S(2)}) collective-permute-start(bf16[4,192,512]{2,1,0:T(8,128)(2,1)S(1)} %pad_maximum_fusion.5), channel_id=1, source_target_pairs={{0,1},{1,2},{2,3},{3,4},{4,5},{5,6},{6,7},{7,0},{8,15},{9,8},{10,9... | collective-permute-start | bytes 2359304 | tf_op jit(solution)/shard_map/ppermute | solution.py:317
  34.6 9.2 %collective-permute-start.5 = (bf16[2,144,384]{2,1,0:T(8,128)(2,1)S(1)}, bf16[2,144,384]{2,1,0:T(8,128)(2,1)S(1)}, u32[]{:S(2)}, u32[]{:S(2)}) collective-permute-start(bf16[2,144,384]{2,1,0:T(8,128)(2,1)S(1)} %pad_maximum_fusion.11), channel_id=1, source_target_pairs={{0,48},{16,32},{32,16},{48,0},{1,49},{17,33},{33,17},{49,1},{2,50}... | collective-permute-start | bytes 663560 | tf_op jit(solution)/shard_map/ppermute | solution.py:311
  39.9 24.3 %collective-permute-start.14 = (bf16[4,144,384]{2,1,0:T(8,128)(2,1)S(1)}, bf16[4,144,384]{2,1,0:T(8,128)(2,1)S(1)}, u32[]{:S(2)}, u32[]{:S(2)}) collective-permute-start(bf16[4,144,384]{2,1,0:T(8,128)(2,1)S(1)} %pad_maximum_fusion.9), channel_id=1, source_target_pairs={{0,16},{16,0},{32,48},{48,32},{1,17},{17,1},{33,49},{49,33},{2,18}... | collective-permute-start | bytes 1327112 | tf_op jit(solution)/shard_map/ppermute | solution.py:311
  41.1 25.5 %collective-permute-start.10 = (bf16[4,144,384]{2,1,0:T(8,128)(2,1)S(1)}, bf16[4,144,384]{2,1,0:T(8,128)(2,1)S(1)}, u32[]{:S(2)}, u32[]{:S(2)}) collective-permute-start(bf16[4,144,384]{2,1,0:T(8,128)(2,1)S(1)} %pad_maximum_fusion.8), channel_id=1, source_target_pairs={{0,48},{16,32},{32,16},{48,0},{1,49},{17,33},{33,17},{49,1},{2,50}... | collective-permute-start | bytes 1327112 | tf_op jit(solution)/shard_map/ppermute | solution.py:311
  43.8 23.2 %collective-permute-start.6 = (bf16[4,144,384]{2,1,0:T(8,128)(2,1)S(1)}, bf16[4,144,384]{2,1,0:T(8,128)(2,1)S(1)}, u32[]{:S(2)}, u32[]{:S(2)}) collective-permute-start(bf16[4,144,384]{2,1,0:T(8,128)(2,1)S(1)} %pad_maximum_fusion.7), channel_id=1, source_target_pairs={{0,64},{64,0},{128,192},{192,128},{1,65},{65,1},{129,193},{193,129... | collective-permute-start | bytes 1327112 | tf_op jit(solution)/shard_map/ppermute | solution.py:311
  62.1 30.3 %collective-permute-start.18 = (bf16[4,192,512]{2,1,0:T(8,128)(2,1)}, bf16[4,192,512]{2,1,0:T(8,128)(2,1)}, u32[]{:S(2)}, u32[]{:S(2)}) collective-permute-start(bf16[4,192,512]{2,1,0:T(8,128)(2,1)} %collective-permute-done.17.refs_0_), channel_id=1, source_target_pairs={{0,1},{1,2},{2,3},{3,4},{4,5},{5,6},{6,7},{7,0},{8,15},{9,8},{10,9... | collective-permute-start | bytes 2359304 | tf_op jit(solution)/shard_map/ppermute | solution.py:317
  62.1 14.2 %collective-permute-start.2 = (bf16[4,144,384]{2,1,0:T(8,128)(2,1)S(1)}, bf16[4,144,384]{2,1,0:T(8,128)(2,1)S(1)}, u32[]{:S(2)}, u32[]{:S(2)}) collective-permute-start(bf16[4,144,384]{2,1,0:T(8,128)(2,1)S(1)} %pad_maximum_fusion.6), channel_id=1, source_target_pairs={{0,192},{64,128},{128,64},{192,0},{1,193},{65,129},{129,65},{193,1... | collective-permute-start | bytes 1327112 | tf_op jit(solution)/shard_map/ppermute | solution.py:311
  64.3 28.1 %collective-permute-start.15 = (bf16[8,144,384]{2,1,0:T(8,128)(2,1)S(1)}, bf16[8,144,384]{2,1,0:T(8,128)(2,1)S(1)}, u32[]{:S(2)}, u32[]{:S(2)}) collective-permute-start(bf16[8,144,384]{2,1,0:T(8,128)(2,1)S(1)} %pad_maximum_fusion.3.refs_6_), channel_id=1, source_target_pairs={{0,48},{16,32},{32,16},{48,0},{1,49},{17,33},{33,17},{49,1},{2,50}... | collective-permute-start | bytes 2654216 | tf_op jit(solution)/shard_map/ppermute | solution.py:311
  66.7 26.7 %collective-permute-start.11 = (bf16[8,144,384]{2,1,0:T(8,128)(2,1)S(1)}, bf16[8,144,384]{2,1,0:T(8,128)(2,1)S(1)}, u32[]{:S(2)}, u32[]{:S(2)}) collective-permute-start(bf16[8,144,384]{2,1,0:T(8,128)(2,1)S(1)} %pad_maximum_fusion.2.refs_4_), channel_id=1, source_target_pairs={{0,16},{16,0},{32,48},{48,32},{1,17},{17,1},{33,49},{49,33},{2,18}... | collective-permute-start | bytes 2654216 | tf_op jit(solution)/shard_map/ppermute | solution.py:311
  67.2 27.5 %collective-permute-start.7 = (bf16[8,144,384]{2,1,0:T(8,128)(2,1)S(1)}, bf16[8,144,384]{2,1,0:T(8,128)(2,1)S(1)}, u32[]{:S(2)}, u32[]{:S(2)}) collective-permute-start(bf16[8,144,384]{2,1,0:T(8,128)(2,1)S(1)} %pad_maximum_fusion.1.refs_2_), channel_id=1, source_target_pairs={{0,192},{64,128},{128,64},{192,0},{1,193},{65,129},{129,65},{193,1... | collective-permute-start | bytes 2654216 | tf_op jit(solution)/shard_map/ppermute | solution.py:311
  76.4 20.7 %collective-permute-start.3 = (bf16[8,144,384]{2,1,0:T(8,128)(2,1)S(1)}, bf16[8,144,384]{2,1,0:T(8,128)(2,1)S(1)}, u32[]{:S(2)}, u32[]{:S(2)}) collective-permute-start(bf16[8,144,384]{2,1,0:T(8,128)(2,1)S(1)} %pad_maximum_fusion.refs_0_), channel_id=1, source_target_pairs={{0,64},{64,0},{128,192},{192,128},{1,65},{65,1},{129,193},{193,129... | collective-permute-start | bytes 2654216 | tf_op jit(solution)/shard_map/ppermute | solution.py:311
  92.4 19.0 %collective-permute-start.19 = (bf16[4,192,512]{2,1,0:T(8,128)(2,1)}, bf16[4,192,512]{2,1,0:T(8,128)(2,1)}, u32[]{:S(2)}, u32[]{:S(2)}) collective-permute-start(bf16[4,192,512]{2,1,0:T(8,128)(2,1)} %collective-permute-done.18.refs_0_), channel_id=1, source_target_pairs={{0,1},{1,2},{2,3},{3,4},{4,5},{5,6},{6,7},{7,0},{8,15},{9,8},{10,9... | collective-permute-start | bytes 2359304 | tf_op jit(solution)/shard_map/ppermute | solution.py:317
  111.4 34.3 %collective-permute-start.39 = (bf16[4,192,512]{2,1,0:T(8,128)(2,1)}, bf16[4,192,512]{2,1,0:T(8,128)(2,1)}, u32[]{:S(2)}, u32[]{:S(2)}) collective-permute-start(bf16[4,192,512]{2,1,0:T(8,128)(2,1)} %collective-permute-done.19.refs_0_), channel_id=1, source_target_pairs={{0,8},{1,9},{2,10},{3,11},{4,12},{5,13},{6,14},{7,15},{8,0},{9,1},... | collective-permute-start | bytes 2359304 | tf_op jit(solution)/shard_map/ppermute | solution.py:321
  111.4 41.4 %collective-permute-start.33 = (bf16[4,192,512]{2,1,0:T(8,128)(2,1)}, bf16[4,192,512]{2,1,0:T(8,128)(2,1)}, u32[]{:S(2)}, u32[]{:S(2)}) collective-permute-start(bf16[4,192,512]{2,1,0:T(8,128)(2,1)} %collective-permute-done.18.refs_0_), channel_id=1, source_target_pairs={{0,8},{1,9},{2,10},{3,11},{4,12},{5,13},{6,14},{7,15},{8,0},{9,1},... | collective-permute-start | bytes 2359304 | tf_op jit(solution)/shard_map/ppermute | solution.py:321
  112.0 46.6 %collective-permute-start.27 = (bf16[4,192,512]{2,1,0:T(8,128)(2,1)}, bf16[4,192,512]{2,1,0:T(8,128)(2,1)}, u32[]{:S(2)}, u32[]{:S(2)}) collective-permute-start(bf16[4,192,512]{2,1,0:T(8,128)(2,1)} %collective-permute-done.17.refs_0_), channel_id=1, source_target_pairs={{0,8},{1,9},{2,10},{3,11},{4,12},{5,13},{6,14},{7,15},{8,0},{9,1},... | collective-permute-start | bytes 2359304 | tf_op jit(solution)/shard_map/ppermute | solution.py:321
  132.4 25.0 %collective-permute-start.20 = (bf16[2,192,512]{2,1,0:T(8,128)(2,1)S(1)}, bf16[2,192,512]{2,1,0:T(8,128)(2,1)S(1)}, u32[]{:S(2)}, u32[]{:S(2)}) collective-permute-start(bf16[2,192,512]{2,1,0:T(8,128)(2,1)S(1)} %slice.212), channel_id=1, source_target_pairs={{0,1},{1,2},{2,3},{3,4},{4,5},{5,6},{6,7},{7,0},{8,15},{9,8},{10,9... | collective-permute-start | bytes 1179656 | tf_op jit(solution)/shard_map/ppermute | solution.py:319
  150.0 26.8 %collective-permute-start.40 = (bf16[8,128,384]{2,1,0:T(8,128)(2,1)S(1)}, bf16[8,128,384]{2,1,0:T(8,128)(2,1)S(1)}, u32[]{:S(2)}, u32[]{:S(2)}) collective-permute-start(bf16[8,128,384]{2,1,0:T(8,128)(2,1)S(1)} %get-tuple-element.48), channel_id=1, source_target_pairs={{0,48},{16,32},{32,16},{48,0},{1,49},{17,33},{33,17},{49,1},{2,50}... | collective-permute-start | bytes 2359304 | tf_op jit(solution)/shard_map/ppermute | solution.py:353
  157.1 21.7 %collective-permute-start.34 = (bf16[8,128,384]{2,1,0:T(8,128)(2,1)S(1)}, bf16[8,128,384]{2,1,0:T(8,128)(2,1)S(1)}, u32[]{:S(2)}, u32[]{:S(2)}) collective-permute-start(bf16[8,128,384]{2,1,0:T(8,128)(2,1)S(1)} %get-tuple-element.45), channel_id=1, source_target_pairs={{0,16},{16,0},{32,48},{48,32},{1,17},{17,1},{33,49},{49,33},{2,18}... | collective-permute-start | bytes 2359304 | tf_op jit(solution)/shard_map/ppermute | solution.py:353
  157.4 15.1 %collective-permute-start.21 = (bf16[2,192,512]{2,1,0:T(8,128)(2,1)S(1)}, bf16[2,192,512]{2,1,0:T(8,128)(2,1)S(1)}, u32[]{:S(2)}, u32[]{:S(2)}) collective-permute-start(bf16[2,192,512]{2,1,0:T(8,128)(2,1)S(1)} %collective-permute-done.20.refs_2_), channel_id=1, source_target_pairs={{0,8},{1,9},{2,10},{3,11},{4,12},{5,13},{6,14},{7,15},{8,0},{9,1},... | collective-permute-start | bytes 1179656 | tf_op jit(solution)/shard_map/ppermute | solution.py:321
  162.7 29.8 %collective-permute-start.28 = (bf16[8,128,384]{2,1,0:T(8,128)(2,1)S(1)}, bf16[8,128,384]{2,1,0:T(8,128)(2,1)S(1)}, u32[]{:S(2)}, u32[]{:S(2)}) collective-permute-start(bf16[8,128,384]{2,1,0:T(8,128)(2,1)S(1)} %get-tuple-element.42), channel_id=1, source_target_pairs={{0,192},{64,128},{128,64},{192,0},{1,193},{65,129},{129,65},{193,1... | collective-permute-start | bytes 2359304 | tf_op jit(solution)/shard_map/ppermute | solution.py:353
  175.9 19.7 %collective-permute-start.22 = (bf16[8,128,384]{2,1,0:T(8,128)(2,1)S(1)}, bf16[8,128,384]{2,1,0:T(8,128)(2,1)S(1)}, u32[]{:S(2)}, u32[]{:S(2)}) collective-permute-start(bf16[8,128,384]{2,1,0:T(8,128)(2,1)S(1)} %get-tuple-element.39), channel_id=1, source_target_pairs={{0,64},{64,0},{128,192},{192,128},{1,65},{65,1},{129,193},{193,129... | collective-permute-start | bytes 2359304 | tf_op jit(solution)/shard_map/ppermute | solution.py:353
  177.1 22.3 %collective-permute-start.41 = (bf16[4,128,384]{2,1,0:T(8,128)(2,1)S(1)}, bf16[4,128,384]{2,1,0:T(8,128)(2,1)S(1)}, u32[]{:S(2)}, u32[]{:S(2)}) collective-permute-start(bf16[4,128,384]{2,1,0:T(8,128)(2,1)S(1)} %get-tuple-element.50), channel_id=1, source_target_pairs={{0,16},{16,0},{32,48},{48,32},{1,17},{17,1},{33,49},{49,33},{2,18}... | collective-permute-start | bytes 1179656 | tf_op jit(solution)/shard_map/ppermute | solution.py:355
  179.0 21.1 %collective-permute-start.35 = (bf16[4,128,384]{2,1,0:T(8,128)(2,1)S(1)}, bf16[4,128,384]{2,1,0:T(8,128)(2,1)S(1)}, u32[]{:S(2)}, u32[]{:S(2)}) collective-permute-start(bf16[4,128,384]{2,1,0:T(8,128)(2,1)S(1)} %get-tuple-element.52), channel_id=1, source_target_pairs={{0,48},{16,32},{32,16},{48,0},{1,49},{17,33},{33,17},{49,1},{2,50}... | collective-permute-start | bytes 1179656 | tf_op jit(solution)/shard_map/ppermute | solution.py:355
  192.8 12.1 %collective-permute-start.29 = (bf16[4,128,384]{2,1,0:T(8,128)(2,1)S(1)}, bf16[4,128,384]{2,1,0:T(8,128)(2,1)S(1)}, u32[]{:S(2)}, u32[]{:S(2)}) collective-permute-start(bf16[4,128,384]{2,1,0:T(8,128)(2,1)S(1)} %get-tuple-element.54), channel_id=1, source_target_pairs={{0,64},{64,0},{128,192},{192,128},{1,65},{65,1},{129,193},{193,129... | collective-permute-start | bytes 1179656 | tf_op jit(solution)/shard_map/ppermute | solution.py:355
  195.8 15.0 %collective-permute-start.23 = (bf16[4,128,384]{2,1,0:T(8,128)(2,1)S(1)}, bf16[4,128,384]{2,1,0:T(8,128)(2,1)S(1)}, u32[]{:S(2)}, u32[]{:S(2)}) collective-permute-start(bf16[4,128,384]{2,1,0:T(8,128)(2,1)S(1)} %get-tuple-element.56), channel_id=1, source_target_pairs={{0,192},{64,128},{128,64},{192,0},{1,193},{65,129},{129,65},{193,1... | collective-permute-start | bytes 1179656 | tf_op jit(solution)/shard_map/ppermute | solution.py:355
  199.5 11.3 %collective-permute-start.42 = (bf16[128,384]{1,0:T(8,128)(2,1)S(1)}, bf16[128,384]{1,0:T(8,128)(2,1)S(1)}, u32[]{:S(2)}, u32[]{:S(2)}) collective-permute-start(bf16[128,384]{1,0:T(8,128)(2,1)S(1)} %get-tuple-element.59), channel_id=1, source_target_pairs={{0,64},{64,0},{128,192},{192,128},{1,65},{65,1},{129,193},{193,129... | collective-permute-start | bytes 294920 | tf_op jit(solution)/shard_map/ppermute | solution.py:359
  199.6 16.4 %collective-permute-start.43 = (bf16[128,384]{1,0:T(8,128)(2,1)S(1)}, bf16[128,384]{1,0:T(8,128)(2,1)S(1)}, u32[]{:S(2)}, u32[]{:S(2)}) collective-permute-start(bf16[128,384]{1,0:T(8,128)(2,1)S(1)} %get-tuple-element.58), channel_id=1, source_target_pairs={{0,192},{64,128},{128,64},{192,0},{1,193},{65,129},{129,65},{193,1... | collective-permute-start | bytes 294920 | tf_op jit(solution)/shard_map/ppermute | solution.py:359
  200.2 17.5 %collective-permute-start.44 = (bf16[128,384]{1,0:T(8,128)(2,1)S(1)}, bf16[128,384]{1,0:T(8,128)(2,1)S(1)}, u32[]{:S(2)}, u32[]{:S(2)}) collective-permute-start(bf16[128,384]{1,0:T(8,128)(2,1)S(1)} %get-tuple-element.57), channel_id=1, source_target_pairs={{0,128},{64,192},{128,0},{192,64},{1,129},{65,193},{129,1},{193,65... | collective-permute-start | bytes 294920 | tf_op jit(solution)/shard_map/ppermute | solution.py:359
  204.9 13.3 %collective-permute-start.36 = (bf16[128,384]{1,0:T(8,128)(2,1)S(1)}, bf16[128,384]{1,0:T(8,128)(2,1)S(1)}, u32[]{:S(2)}, u32[]{:S(2)}) collective-permute-start(bf16[128,384]{1,0:T(8,128)(2,1)S(1)} %get-tuple-element.63), channel_id=1, source_target_pairs={{0,192},{64,128},{128,64},{192,0},{1,193},{65,129},{129,65},{193,1... | collective-permute-start | bytes 294920 | tf_op jit(solution)/shard_map/ppermute | solution.py:359
  210.8 9.5 %collective-permute-start.37 = (bf16[128,384]{1,0:T(8,128)(2,1)S(1)}, bf16[128,384]{1,0:T(8,128)(2,1)S(1)}, u32[]{:S(2)}, u32[]{:S(2)}) collective-permute-start(bf16[128,384]{1,0:T(8,128)(2,1)S(1)} %get-tuple-element.62), channel_id=1, source_target_pairs={{0,64},{64,0},{128,192},{192,128},{1,65},{65,1},{129,193},{193,129... | collective-permute-start | bytes 294920 | tf_op jit(solution)/shard_map/ppermute | solution.py:359
  210.8 10.4 %collective-permute-start.38 = (bf16[128,384]{1,0:T(8,128)(2,1)S(1)}, bf16[128,384]{1,0:T(8,128)(2,1)S(1)}, u32[]{:S(2)}, u32[]{:S(2)}) collective-permute-start(bf16[128,384]{1,0:T(8,128)(2,1)S(1)} %get-tuple-element.61), channel_id=1, source_target_pairs={{0,128},{64,192},{128,0},{192,64},{1,129},{65,193},{129,1},{193,65... | collective-permute-start | bytes 294920 | tf_op jit(solution)/shard_map/ppermute | solution.py:359
  (42 other events, 383.8 us)
Sparse Core Ops, SparseCore 0:
  9.2 98.5 all-gather.2
where the time goes:
time: 242 us; the launch traced here: 238 us
  waiting for transfers between devices  87.3 us (36%)
  starting transfers between devices  64.3 us (27%)
  Pallas kernels  41.6 us (17%)
  local copies, waits for them, and re-layouts  26.1 us (11%)
  between operations  14 us (6%)
  other arithmetic  4.37 us (2%)
    ppermute x3, waiting for transfers between devices, spread_out(): block = lax.ppermute(behind(block, *held), axes, hop)  45.4 us
    unnamed x56, local copies, waits for them, and re-layouts  24.3 us
    ppermute x12, starting transfers between devices, body(): lax.ppermute(sums[i + 1], small, links(turn))  20.8 us
    ppermute x16, starting transfers between devices, spread_out(): got.append(lax.ppermute(held[group], axis, links(turn)))  20 us
    ppermute x16, waiting for transfers between devices, spread_out(): got.append(lax.ppermute(held[group], axis, links(turn)))  18.2 us
    pallas_call x4, Pallas kernels, spread_rows(): pl.pallas_call(functools.partial(spread_kernel, PLANS[group]), in_specs=[...  16.1 us
    ppermute x4, waiting for transfers between devices, body(): got = lax.ppermute(send, big, links(first))  15.7 us
    ppermute x4, starting transfers between devices, body(): got = lax.ppermute(send, big, links(first))  13.8 us
  transfers between devices with their start and end apart: 46, of which 18 were waited for; matrix products, arithmetic and copies ran while one was open for 2% of the time, Pallas kernels for 17%

commit v1 on v0

--- a/solution.py
+++ b/solution.py
@@ -195,133 +195,107 @@
 
 def hidden_units_kernel(packed_ref, gate_ref, up_ref, act_ref):
     rows = packed_ref[0].reshape(BLOCKS * CAP, D)
+    width = act_ref.shape[-1]
+    gate = jnp.dot(rows, gate_ref[...].reshape(D, width), preferred_element_type=F32)
+    up = jnp.dot(rows, up_ref[...].reshape(D, width), preferred_element_type=F32)
+    act = (gate / (1.0 + jnp.exp(-gate)) * up).astype(BF16)
+    act_ref[0] = act.reshape(BLOCKS, CAP, width)
+
+
+def hidden_units(packed, weights):
     width = 256
 
-    def run(i):
-        cols = pl.ds(pl.multiple_of(i * width, width), width)
-        w_gate = gate_ref[0, :, 0, 0, :, cols].reshape(D, width)
-        w_up = up_ref[0, :, 0, 0, :, cols].reshape(D, width)
-        gate = jnp.dot(rows, w_gate, preferred_element_type=F32)
-        up = jnp.dot(rows, w_up, preferred_element_type=F32)
-        act_ref[0, :, cols] = (gate / (1.0 + jnp.exp(-gate)) * up).astype(BF16)
-
-    each(FF // width, 1, run)
-
-
-def hidden_units(packed, weights):
     def block(which):
-        return pl.BlockSpec((1, 8, 1, 1, CHUNK, FF), lambda s: (s // 2, 0, which, s % 2, 0, 0))
+        return pl.BlockSpec(
+            (1, 8, 1, 1, CHUNK, width), lambda s, f: (s // 2, 0, which, s % 2, 0, f)
+        )
 
     return pl.pallas_call(
         hidden_units_kernel,
-        grid=(LOCAL,),
-        in_specs=[pl.BlockSpec((1, BLOCKS, CAP, D), lambda s: (s, 0, 0, 0)), block(0), block(1)],
-        out_specs=pl.BlockSpec((1, BLOCKS * CAP, FF), lambda s: (s, 0, 0)),
-        out_shape=jax.ShapeDtypeStruct((LOCAL, BLOCKS * CAP, FF), BF16),
-        compiler_params=params(24, "arbitrary"),
+        grid=(LOCAL, FF // width),
+        in_specs=[pl.BlockSpec((1, BLOCKS, CAP, D), lambda s, f: (s, 0, 0, 0)), block(0), block(1)],
+        out_specs=pl.BlockSpec((1, BLOCKS, CAP, width), lambda s, f: (s, 0, 0, f)),
+        out_shape=jax.ShapeDtypeStruct((LOCAL, BLOCKS, CAP, FF), BF16),
+        compiler_params=params(24, "arbitrary", "arbitrary"),
         name="hidden_units",
     )(packed, weights, weights)
 
 
-def spread_kernel(plan, place_ref, act_ref, scale_ref, spread_ref, *refs):
-    down_refs, (send_ref, keep_ref, part_ref) = refs[:-3], refs[-3:]
-    x, y, core = place_ref[0], place_ref[1], place_ref[2]
+def spread_kernel(plan, start, place_ref, act_ref, down_ref, scale_ref, spread_ref, out_ref, part_ref):
+    x, y = place_ref[0], place_ref[1]
     half = BLOCKS // 2
-    for flip in range(2):
-        for q in range(2):
-            if len(down_refs) == 4:
-                pieces = [down_refs[flip][q], down_refs[2 + flip][q]]
-            else:
-                pieces = [down_refs[0][2 * flip + q], down_refs[1][2 * (1 - flip) + q]]
-            slot = 2 * (core ^ flip) + q
-            part = lax.dot_general(
-                act_ref[slot], jnp.concatenate(pieces), (((1,), (1,)), ((), ())),
-                preferred_element_type=F32,
-            )
-            scale = scale_ref[slot].reshape(BLOCKS * CAP, 1)
-            part_ref[:, slot] = (part * scale).astype(BF16).reshape(BLOCKS, CAP, GROUP)
-
-    def back(out_ref, start, i):
+    order = [block_at(plan, x, y, start + i) for i in range(half)]
+    for s in range(LOCAL):
+        rows = jnp.concatenate([act_ref[s, b] for b in order])
+        scale = jnp.concatenate([scale_ref[s, b] for b in order])
+        down = down_ref[s // 2, :, 0, s % 2].reshape(GROUP, FF)
+        part = lax.dot_general(
+            rows, down, (((1,), (1,)), ((), ())), preferred_element_type=F32
+        )
+        part_ref[:, s] = (part * scale).astype(BF16).reshape(half, CAP, GROUP)
+
+    def back(i):
         b = block_at(plan, x, y, start + i)
-        rows = part_ref[b].reshape(LOCAL * CAP, GROUP)
+        rows = part_ref[i].reshape(LOCAL * CAP, GROUP)
         out_ref[i] = jnp.dot(spread_ref[b], rows, preferred_element_type=F32).astype(BF16)
 
-    each(half, 2, functools.partial(back, keep_ref, 0))
-    each(half, 2, functools.partial(back, send_ref, half))
-
-
-def spread_rows(place, act, scale, spread, down, group):
+    each(half, 4, back)
+
+
+def spread_rows(place, act, weights, scale, spread, group, start):
     half = BLOCKS // 2
-    vmem = pl.BlockSpec(memory_space=pltpu.VMEM)
-    return pl.pallas_call(
-        functools.partial(spread_kernel, PLANS[group]),
-        in_specs=[pl.BlockSpec(memory_space=pltpu.SMEM)] + [vmem] * (3 + len(down)),
-        out_specs=[vmem, vmem],
-        scratch_shapes=[pltpu.VMEM((BLOCKS, LOCAL, CAP, GROUP), BF16)],
-        out_shape=[jax.ShapeDtypeStruct((half, ROWS, GROUP), BF16)] * 2,
-        compiler_params=params(16),
+    whole = lambda array: pl.BlockSpec(array.shape, lambda i, o: (0,) * array.ndim)
+    return pl.pallas_call(
+        functools.partial(spread_kernel, PLANS[group], start),
+        grid_spec=pltpu.PrefetchScalarGridSpec(
+            num_scalar_prefetch=1,
+            grid=(1,),
+            in_specs=[
+                whole(act),
+                pl.BlockSpec((2, 2, 1, 2, CHUNK, FF), lambda i, o: (0, group, 2, 0, 0, 0)),
+                whole(scale),
+                whole(spread),
+            ],
+            out_specs=pl.BlockSpec((half, ROWS, GROUP), lambda i, o: (0, 0, 0)),
+            scratch_shapes=[pltpu.VMEM((half, LOCAL, CAP, GROUP), BF16)],
+        ),
+        out_shape=jax.ShapeDtypeStruct((half, ROWS, GROUP), BF16),
+        compiler_params=params(16, "arbitrary"),
         name="spread",
-    )(place, act, scale, spread, *down)
-
-
-def closing_kernel(place_ref, hidden_ref, gain_ref, *refs):
-    parts, (out_ref, moe_ref) = refs[:-2], refs[-2:]
-    core, z = place_ref[2], place_ref[3]
-    step = 1 - 2 * core
-    each_group = len(parts) // LOCAL
-    for g in range(LOCAL):
-        total = sum(ref[...].astype(F32) for ref in parts[g * each_group : (g + 1) * each_group])
-        ends = (z, z + 4) if g == 0 else (z - g * step, z + g * step)
-        for n, end in enumerate(ends):
-            moe_ref[end & 7] = total[:, n * CHUNK : (n + 1) * CHUNK]
-    moe = jnp.concatenate([moe_ref[i] for i in range(8)], axis=1)
+    )(place, act, weights, scale, spread)
+
+
+def closing_kernel(hidden_ref, gain_ref, *refs):
+    pairs, out_ref = refs[:-1], refs[-1]
+    moe = jnp.concatenate(
+        [
+            pairs[2 * g][...].astype(F32) + pairs[2 * g + 1][...].astype(F32)
+            for g in range(LOCAL)
+        ],
+        axis=1,
+    )
     mixed = hidden_ref[...] + moe
     mean_sq = jnp.mean(mixed * mixed, axis=-1, keepdims=True)
     out_ref[...] = (mixed * lax.rsqrt(mean_sq + EPS) * gain_ref[...]).astype(BF16)
 
 
-def closing(place, hidden, gain, parts):
-    vmem = pl.BlockSpec(memory_space=pltpu.VMEM)
+def closing(hidden, gain, pairs):
     return pl.pallas_call(
         closing_kernel,
-        in_specs=[pl.BlockSpec(memory_space=pltpu.SMEM)] + [vmem] * (2 + len(parts)),
-        out_specs=vmem,
         out_shape=jax.ShapeDtypeStruct((ROWS, D), BF16),
-        scratch_shapes=[pltpu.VMEM((8, ROWS, CHUNK), F32)],
         compiler_params=params(8),
         name="closing",
-    )(place, hidden, gain, *parts)
-
-
-def behind(value, *earlier):
-    return lax.optimization_barrier((value, *earlier))[0]
-
-
-def spread_out(rows, own):
-    axes = ("core", "blk")
-    swap = [(8 * c + z, 8 * (1 - c) + z) for c in range(2) for z in range(8)]
-    hop = [(z, (z + 1) % 8) for z in range(8)] + [(8 + z, 8 + (z - 1) % 8) for z in range(8)]
-    held = [rows[group][None] for group in range(LOCAL)]
-    block, blocks = None, []
-    for step in range(4):
-        got = []
-        for group, (big, small, first, other) in enumerate(PLANS):
-            axis = small if step < 2 else big
-            turn = first if step % 2 else other
-            got.append(lax.ppermute(held[group], axis, links(turn)))
-        if step == 0:
-            twin = lax.ppermute(behind(own, rows), axes, swap)
-            block = jnp.concatenate([own, twin])
-        if step < 3:
-            held = [jnp.concatenate(both) for both in zip(held, got)]
-            block = lax.ppermute(behind(block, *held), axes, hop)
-            blocks.append(block)
-    last = lax.ppermute(behind(block[:2], *got), axes, hop)
-    *pairs, twin_last = [
-        lax.ppermute(behind(block, *got), axes, swap) for block in (*blocks, last)
-    ]
-    downs = [(own, twin, last, twin_last), *zip(blocks, pairs)]
-    return [half for both in zip(held, got) for half in both], downs
+    )(hidden, gain, *pairs)
+
+
+def spread_out(rows):
+    halves = []
+    for group, (big, small, first, other) in enumerate(PLANS):
+        held = rows[group][None]
+        for axis, turn in ((small, other), (small, first), (big, other)):
+            held = jnp.concatenate([held, lax.ppermute(held, axis, links(turn))])
+        halves += [held, lax.ppermute(held, big, links(first))]
+    return halves
 
 
 def add(a, b):
@@ -332,33 +306,37 @@
     attn_out, resid, w_o, norm1_gain, router_w, route_slot, slot_expert, keep,
     w_gate, w_up, w_down, norm2_gain,
 ):
-    joined = jnp.stack([w_gate, w_up])
+    joined = jnp.stack([w_gate, w_up, w_down])
     weights = lax.all_gather(joined, ("core", "blk"), axis=0, tiled=False)
-    weights = weights.reshape(2, 8, 2, 2, CHUNK, FF)
+    weights = weights.reshape(2, 8, 3, 2, CHUNK, FF)
     weights = pltpu.with_memory_space_constraint(weights, pltpu.HBM)
 
     hidden, outgoing = entry(
         attn_out, resid, w_o, norm1_gain.reshape(1, D), router_w.T, route_slot.T,
         slot_expert.reshape(1, SLOTS), keep.reshape(1, ROWS),
     )
-    place = jnp.stack([lax.axis_index(name) for name in ("x", "y", "core", "blk")])
-    place = place.astype(jnp.int32)
-    rows, downs = spread_out(outgoing, w_down)
-    packed, spread, scale = compact(place, rows)
+    place = jnp.stack([lax.axis_index(name) for name in ("x", "y")]).astype(jnp.int32)
+    packed, spread, scale = compact(place, spread_out(outgoing))
+    packed = pltpu.with_memory_space_constraint(packed, pltpu.HBM)
     act = hidden_units(packed, weights)
 
-    parts = []
-    for group, (big, small, first, other) in enumerate(PLANS):
-        send, kept = spread_rows(place, act, scale, spread, downs[group], group)
+    halves = []
+    for start in (BLOCKS // 2, 0):
+        done = [half for group in halves for half in group]
+        act = lax.optimization_barrier((act, *done))[0]
+        halves.append(
+            [spread_rows(place, act, weights, scale, spread, g, start) for g in range(LOCAL)]
+        )
+    pairs = []
+    for send, kept, (big, small, first, other) in zip(*halves, PLANS):
         got = lax.ppermute(send, big, links(first))
         send, kept = add(kept[4:], got[4:]), add(kept[:4], got[:4])
         got = lax.ppermute(send, big, links(other))
-        sums = [add(kept[i], got[i]) for i in range(4)]
-        turns = (other, first, first ^ other)
-        parts += [sums[0]] + [
-            lax.ppermute(sums[i + 1], small, links(turn)) for i, turn in enumerate(turns)
-        ]
-    return closing(place, hidden, norm2_gain.reshape(1, D), parts)
+        send, kept = add(kept[2:], got[2:]), add(kept[:2], got[:2])
+        got = lax.ppermute(send, small, links(first))
+        send, kept = add(kept[1], got[1]), add(kept[0], got[0])
+        pairs += [kept, lax.ppermute(send, small, links(other))]
+    return closing(hidden, norm2_gain.reshape(1, D), pairs)
 
 
 def solution(mesh):

time: 242 us -> 213 us (0.88); the launches traced: 238 us -> 212 us
  starting transfers between devices: 64.3 us -> 42.5 us
  local copies, waits for them, and re-layouts: 26.1 us -> 7.4 us
  Pallas kernels: 41.6 us -> 54.1 us
    all_gather x1, waiting for transfers between devices: 0.02 us -> 28.7 us  [body(): weights = lax.all_gather(joined, ('core', 'blk'), axis=0, tiled=False)]
    ppermute x37 -> x24, waiting for transfers between devices: 67.2 us -> 38.9 us  [the longest x12 19.9 us: spread_out(): held = jnp.concatenate([held, lax.ppermute(held, axis, links(turn))])]
    unnamed x56 -> x28, local copies, waits for them, and re-layouts: 24.3 us -> 7.34 us
    ppermute x37 -> x24, starting transfers between devices: 44.5 us -> 31 us  [the longest x12 17.8 us: spread_out(): held = jnp.concatenate([held, lax.ppermute(held, axis, links(turn))])]
    pallas_call x6 -> x10, Pallas kernels: 28.5 us -> 39.2 us  [the longest x8 25.5 us: spread_rows(): pl.pallas_call(functools.partial(spread_kernel, PLANS[group], start), gri...]
    ppermute x4, starting transfers between devices: 13.8 us -> 4.72 us  [body(): got = lax.ppermute(send, big, links(first))]
  transfers between devices with their start and end apart: 46 -> 33, of which waited for: 18 -> 14; matrix products, arithmetic and copies ran while one was open for 2% -> 2% of each run, Pallas kernels for 17% -> 18%
where the time goes in v1:
time: 213 us; the launch traced here: 212 us
  waiting for transfers between devices  89.1 us (42%)
  Pallas kernels  54.1 us (25%)
  starting transfers between devices  42.5 us (20%)
  between operations  13.7 us (6%)
  local copies, waits for them, and re-layouts  7.4 us (3%)
  other arithmetic  5.67 us (3%)
    all_gather x1, waiting for transfers between devices, body(): weights = lax.all_gather(joined, ('core', 'blk'), axis=0, tiled=False)  28.7 us
    pallas_call x8, Pallas kernels, spread_rows(): pl.pallas_call(functools.partial(spread_kernel, PLANS[group], start), gri...  25.5 us
    ppermute x12, waiting for transfers between devices, spread_out(): held = jnp.concatenate([held, lax.ppermute(held, axis, links(turn))])  19.9 us
    ppermute x12, starting transfers between devices, spread_out(): held = jnp.concatenate([held, lax.ppermute(held, axis, links(turn))])  17.8 us
    ppermute x4, waiting for transfers between devices, body(): got = lax.ppermute(send, big, links(first))  15.1 us
    ppermute x4, waiting for transfers between devices, spread_out(): halves += [held, lax.ppermute(held, big, links(first))]  13.8 us
    pallas_call x1, Pallas kernels, hidden_units(): pl.pallas_call(hidden_units_kernel, grid=(LOCAL, FF // width), in_specs=[...  12.7 us
    pallas_call x1, Pallas kernels, compact(): pl.pallas_call(compact_kernel, in_specs=[pl.BlockSpec(memory_space=pltpu....  11.5 us
  transfers between devices with their start and end apart: 33, of which 14 were waited for; matrix products, arithmetic and copies ran while one was open for 2% of the time, Pallas kernels for 18%

profile of v1, /device:TPU:6, one launch (start us, length us, event | category | flops | bytes accessed | tf_op | source)
XLA Modules:
  0.0 212.5 jit_solution(10959426034190155802)
XLA Ops:
  6.5 2.4 %pad_maximum_fusion = bf16[3,2,192,512]{3,2,1,0:T(8,128)(2,1)} fusion(bf16[1,2,192,512]{3,2,1,0:T(8,128)(2,1)} %bitcast.40, bf16[1,2,192,512]{3,2,1,0:T(8,128)(2,1)} %bitcast.41, bf16[1,2,192,512]{3,2,1,0:T(8,128)(2,1)} %bitcast.42), kind=kLoop, calls=%fused_computation | loop fusion | flops 1179648 | bytes 2359296 | tf_op jit(solution)/shard_map/stack | solution.py:309
  10.1 2.3 %copy-done.1 = bf16[1536,1536]{1,0:T(8,128)(2,1)S(1)} copy-done((bf16[1536,1536]{1,0:T(8,128)(2,1)S(1)}, bf16[1536,1536]{1,0:T(8,128)(2,1)}, u32[]{:S(2)}) %copy-start.1) | copy-done | bytes 4718616
  12.4 3.4 %entry.1 = (f32[128,1536]{1,0:T(8,128)S(1)}, bf16[4,144,384]{2,1,0:T(8,128)(2,1)S(1)}) custom-call(bf16[128,1536]{1,0:T(8,128)(2,1)S(1)} %copy-done.6, bf16[128,1536]{1,0:T(8,128)(2,1)S(1)} %copy-done.7, bf16[1536,1536]{1,0:T(8,128)(2,1)S(1)} %copy-done.1, f32[1,1536]{1,0:T(1,128)S(1)} %reshape.47.gain_ref, f32[40,1536]{1,0:T(8,128)S(1)} %bitcast.26, ...), custom_call_target="tpu_custom_call" | custom-call | tf_op jit(solution)/shard_map/entry/pallas_call | solution.py:105
  19.5 2.2 %collective-permute-start = (bf16[1,144,384]{2,1,0:T(8,128)(2,1)S(1)}, bf16[1,144,384]{2,1,0:T(8,128)(2,1)S(1)}, u32[]{:S(2)}, u32[]{:S(2)}) collective-permute-start(bf16[1,144,384]{2,1,0:T(8,128)(2,1)S(1)} %get-tuple-element.36), channel_id=1, source_target_pairs={{0,48},{16,32},{32,16},{48,0},{1,49},{17,33},{33,17},{49,1},{2,50}... | collective-permute-start | bytes 331784 | tf_op jit(solution)/shard_map/ppermute | solution.py:296
  21.8 2.2 %collective-permute-start.13 = (bf16[2,144,384]{2,1,0:T(8,128)(2,1)S(1)}, bf16[2,144,384]{2,1,0:T(8,128)(2,1)S(1)}, u32[]{:S(2)}, u32[]{:S(2)}) collective-permute-start(bf16[2,144,384]{2,1,0:T(8,128)(2,1)S(1)} %pad_maximum_fusion.12), channel_id=1, source_target_pairs={{0,192},{64,128},{128,64},{192,0},{1,193},{65,129},{129,65},{193,1... | collective-permute-start | bytes 663560 | tf_op jit(solution)/shard_map/ppermute | solution.py:296
  24.1 1.9 collective-permute-start.5
  26.1 3.0 %collective-permute-done.13 = bf16[2,144,384]{2,1,0:T(8,128)(2,1)S(1)} collective-permute-done((bf16[2,144,384]{2,1,0:T(8,128)(2,1)S(1)}, bf16[2,144,384]{2,1,0:T(8,128)(2,1)S(1)}, u32[]{:S(2)}, u32[]{:S(2)}) %collective-permute-start.13) | collective-permute-done | bytes 221216 | tf_op jit(solution)/shard_map/ppermute | solution.py:296
  31.5 2.4 %collective-permute-start.10 = (bf16[4,144,384]{2,1,0:T(8,128)(2,1)S(1)}, bf16[4,144,384]{2,1,0:T(8,128)(2,1)S(1)}, u32[]{:S(2)}, u32[]{:S(2)}) collective-permute-start(bf16[4,144,384]{2,1,0:T(8,128)(2,1)S(1)} %pad_maximum_fusion.7), channel_id=1, source_target_pairs={{0,48},{16,32},{32,16},{48,0},{1,49},{17,33},{33,17},{49,1},{2,50}... | collective-permute-start | bytes 1327112 | tf_op jit(solution)/shard_map/ppermute | solution.py:296
  34.8 9.0 %collective-permute-done.1 = bf16[2,144,384]{2,1,0:T(8,128)(2,1)S(1)} collective-permute-done((bf16[2,144,384]{2,1,0:T(8,128)(2,1)S(1)}, bf16[2,144,384]{2,1,0:T(8,128)(2,1)S(1)}, u32[]{:S(2)}, u32[]{:S(2)}) %collective-permute-start.1) | collective-permute-done | bytes 221216 | tf_op jit(solution)/shard_map/ppermute | solution.py:296
  43.9 2.3 %collective-permute-start.2 = (bf16[4,144,384]{2,1,0:T(8,128)(2,1)S(1)}, bf16[4,144,384]{2,1,0:T(8,128)(2,1)S(1)}, u32[]{:S(2)}, u32[]{:S(2)}) collective-permute-start(bf16[4,144,384]{2,1,0:T(8,128)(2,1)S(1)} %pad_maximum_fusion.5), channel_id=1, source_target_pairs={{0,192},{64,128},{128,64},{192,0},{1,193},{65,129},{129,65},{193,1... | collective-permute-start | bytes 1327112 | tf_op jit(solution)/shard_map/ppermute | solution.py:296
  47.9 2.7 %collective-permute-start.7 = (bf16[8,144,384]{2,1,0:T(8,128)(2,1)S(1)}, bf16[8,144,384]{2,1,0:T(8,128)(2,1)}, u32[]{:S(2)}, u32[]{:S(2)}) collective-permute-start(bf16[8,144,384]{2,1,0:T(8,128)(2,1)S(1)} %pad_maximum_fusion.2.refs_2_), channel_id=1, source_target_pairs={{0,192},{64,128},{128,64},{192,0},{1,193},{65,129},{129,65},{193,1... | collective-permute-start | bytes 2654216 | tf_op jit(solution)/shard_map/ppermute | solution.py:297
  50.6 7.8 %collective-permute-done.2 = bf16[4,144,384]{2,1,0:T(8,128)(2,1)S(1)} collective-permute-done((bf16[4,144,384]{2,1,0:T(8,128)(2,1)S(1)}, bf16[4,144,384]{2,1,0:T(8,128)(2,1)S(1)}, u32[]{:S(2)}, u32[]{:S(2)}) %collective-permute-start.2) | collective-permute-done | bytes 442400 | tf_op jit(solution)/shard_map/ppermute | solution.py:296
  59.5 6.6 %collective-permute-done.15.refs_7_ = bf16[8,144,384]{2,1,0:T(8,128)(2,1)} collective-permute-done((bf16[8,144,384]{2,1,0:T(8,128)(2,1)S(1)}, bf16[8,144,384]{2,1,0:T(8,128)(2,1)}, u32[]{:S(2)}, u32[]{:S(2)}) %collective-permute-start.15) | collective-permute-done | bytes 884768 | tf_op jit(solution)/shard_map/ppermute | solution.py:297
  66.1 7.2 %collective-permute-done.7.refs_3_ = bf16[8,144,384]{2,1,0:T(8,128)(2,1)} collective-permute-done((bf16[8,144,384]{2,1,0:T(8,128)(2,1)S(1)}, bf16[8,144,384]{2,1,0:T(8,128)(2,1)}, u32[]{:S(2)}, u32[]{:S(2)}) %collective-permute-start.7) | collective-permute-done | bytes 884768 | tf_op jit(solution)/shard_map/ppermute | solution.py:297
  74.5 11.5 %compact.1 = (bf16[4,16,32,1536]{3,2,1,0:T(8,128)(2,1)S(1)}, bf16[16,128,128]{2,1,0:T(8,128)(2,1)S(1)}, f32[4,16,32,1]{3,2,1,0:T(8,128)S(1)}) custom-call(s32[2]{0:T(128)S(1)} %pad_add_fusion.place_ref, bf16[8,144,384]{2,1,0:T(8,128)(2,1)} %pad_maximum_fusion.1.refs_0_, bf16[8,144,384]{2,1,0:T(8,128)(2,1)} %collective-permute-done.3.refs_1_, ...), custom_call_target="tpu_custom_call" | custom-call | tf_op jit(solution)/shard_map/compact/pallas_call | solution.py:178
  86.1 2.7 %copy-done = bf16[4,16,32,1536]{3,2,1,0:T(8,128)(2,1)} copy-done((bf16[4,16,32,1536]{3,2,1,0:T(8,128)(2,1)}, bf16[4,16,32,1536]{3,2,1,0:T(8,128)(2,1)S(1)}, u32[]{:S(2)}) %copy-start) | copy-done | bytes 6291480
  88.7 28.7 %all-gather.3.cloned.1.call-done = bf16[48,2,192,512]{3,2,1,0:T(8,128)(2,1)} async-done(((bf16[3,2,192,512]{3,2,1,0:T(8,128)(2,1)}), bf16[48,2,192,512]{3,2,1,0:T(8,128)(2,1)}) %all-gather.3.cloned.1.call-update) | async-done | bytes 18874384 | tf_op jit(solution)/shard_map/all_gather | solution.py:310
  117.4 12.7 %hidden_units.1.act_ref = bf16[4,16,32,512]{3,2,1,0:T(8,128)(2,1)S(1)} custom-call(bf16[4,16,32,1536]{3,2,1,0:T(8,128)(2,1)} %copy-done, bf16[2,8,3,2,192,512]{5,4,3,2,1,0:T(8,128)(2,1)} %bitcast.30, bf16[2,8,3,2,192,512]{5,4,3,2,1,0:T(8,128)(2,1)} %bitcast.31), custom_call_target="tpu_custom_call" | custom-call | tf_op jit(solution)/shard_map/hidden_units/pallas_call | solution.py:213
  130.1 3.2 %spread.11 = bf16[8,128,384]{2,1,0:T(8,128)(2,1)S(1)} custom-call(s32[2]{0:T(128)S(1)} %pad_add_fusion.place_ref, bf16[4,16,32,512]{3,2,1,0:T(8,128)(2,1)S(1)} %hidden_units.1.act_ref, bf16[2,8,3,2,192,512]{5,4,3,2,1,0:T(8,128)(2,1)} %bitcast.32, f32[4,16,32,1]{3,2,1,0:T(8,128)S(1)} %get-tuple-element.14.scale_ref, ...), custom_call_target="tpu_custom_call" | custom-call | tf_op jit(solution)/shard_map/spread/pallas_call | solution.py:248
  133.3 2.8 %collective-permute-start.28 = (bf16[8,128,384]{2,1,0:T(8,128)(2,1)S(1)}, bf16[8,128,384]{2,1,0:T(8,128)(2,1)S(1)}, u32[]{:S(2)}, u32[]{:S(2)}) collective-permute-start(bf16[8,128,384]{2,1,0:T(8,128)(2,1)S(1)} %spread.11), channel_id=1, source_target_pairs={{0,48},{16,32},{32,16},{48,0},{1,49},{17,33},{33,17},{49,1},{2,50}... | collective-permute-start | bytes 2359304 | tf_op jit(solution)/shard_map/ppermute | solution.py:332
  136.2 3.2 %spread.10 = bf16[8,128,384]{2,1,0:T(8,128)(2,1)S(1)} custom-call(s32[2]{0:T(128)S(1)} %pad_add_fusion.place_ref, bf16[4,16,32,512]{3,2,1,0:T(8,128)(2,1)S(1)} %hidden_units.1.act_ref, bf16[2,8,3,2,192,512]{5,4,3,2,1,0:T(8,128)(2,1)} %bitcast.33, f32[4,16,32,1]{3,2,1,0:T(8,128)S(1)} %get-tuple-element.14.scale_ref, ...), custom_call_target="tpu_custom_call" | custom-call | tf_op jit(solution)/shard_map/spread/pallas_call | solution.py:248
  139.7 3.2 %spread.9 = bf16[8,128,384]{2,1,0:T(8,128)(2,1)S(1)} custom-call(s32[2]{0:T(128)S(1)} %pad_add_fusion.place_ref, bf16[4,16,32,512]{3,2,1,0:T(8,128)(2,1)S(1)} %hidden_units.1.act_ref, bf16[2,8,3,2,192,512]{5,4,3,2,1,0:T(8,128)(2,1)} %bitcast.34, f32[4,16,32,1]{3,2,1,0:T(8,128)S(1)} %get-tuple-element.14.scale_ref, ...), custom_call_target="tpu_custom_call" | custom-call | tf_op jit(solution)/shard_map/spread/pallas_call | solution.py:248
  143.5 3.2 %spread.8 = bf16[8,128,384]{2,1,0:T(8,128)(2,1)S(1)} custom-call(s32[2]{0:T(128)S(1)} %pad_add_fusion.place_ref, bf16[4,16,32,512]{3,2,1,0:T(8,128)(2,1)S(1)} %hidden_units.1.act_ref, bf16[2,8,3,2,192,512]{5,4,3,2,1,0:T(8,128)(2,1)} %bitcast.35, f32[4,16,32,1]{3,2,1,0:T(8,128)S(1)} %get-tuple-element.14.scale_ref, ...), custom_call_target="tpu_custom_call" | custom-call | tf_op jit(solution)/shard_map/spread/pallas_call | solution.py:248
  146.7 3.2 %spread.15 = bf16[8,128,384]{2,1,0:T(8,128)(2,1)S(1)} custom-call(s32[2]{0:T(128)S(1)} %pad_add_fusion.place_ref, bf16[4,16,32,512]{3,2,1,0:T(8,128)(2,1)S(1)} %hidden_units.1.act_ref, bf16[2,8,3,2,192,512]{5,4,3,2,1,0:T(8,128)(2,1)} %bitcast.36, f32[4,16,32,1]{3,2,1,0:T(8,128)S(1)} %get-tuple-element.14.scale_ref, ...), custom_call_target="tpu_custom_call" | custom-call | tf_op jit(solution)/shard_map/spread/pallas_call | solution.py:248
  149.9 3.2 %spread.14 = bf16[8,128,384]{2,1,0:T(8,128)(2,1)S(1)} custom-call(s32[2]{0:T(128)S(1)} %pad_add_fusion.place_ref, bf16[4,16,32,512]{3,2,1,0:T(8,128)(2,1)S(1)} %hidden_units.1.act_ref, bf16[2,8,3,2,192,512]{5,4,3,2,1,0:T(8,128)(2,1)} %bitcast.37, f32[4,16,32,1]{3,2,1,0:T(8,128)S(1)} %get-tuple-element.14.scale_ref, ...), custom_call_target="tpu_custom_call" | custom-call | tf_op jit(solution)/shard_map/spread/pallas_call | solution.py:248
  153.1 3.2 %spread.13 = bf16[8,128,384]{2,1,0:T(8,128)(2,1)S(1)} custom-call(s32[2]{0:T(128)S(1)} %pad_add_fusion.place_ref, bf16[4,16,32,512]{3,2,1,0:T(8,128)(2,1)S(1)} %hidden_units.1.act_ref, bf16[2,8,3,2,192,512]{5,4,3,2,1,0:T(8,128)(2,1)} %bitcast.38, f32[4,16,32,1]{3,2,1,0:T(8,128)S(1)} %get-tuple-element.14.scale_ref, ...), custom_call_target="tpu_custom_call" | custom-call | tf_op jit(solution)/shard_map/spread/pallas_call | solution.py:248
  156.3 3.2 %spread.12 = bf16[8,128,384]{2,1,0:T(8,128)(2,1)S(1)} custom-call(s32[2]{0:T(128)S(1)} %pad_add_fusion.place_ref, bf16[4,16,32,512]{3,2,1,0:T(8,128)(2,1)S(1)} %hidden_units.1.act_ref, bf16[2,8,3,2,192,512]{5,4,3,2,1,0:T(8,128)(2,1)} %bitcast.39, f32[4,16,32,1]{3,2,1,0:T(8,128)S(1)} %get-tuple-element.14.scale_ref, ...), custom_call_target="tpu_custom_call" | custom-call | tf_op jit(solution)/shard_map/spread/pallas_call | solution.py:248
  165.0 15.0 %collective-permute-done.16 = bf16[8,128,384]{2,1,0:T(8,128)(2,1)S(1)} collective-permute-done((bf16[8,128,384]{2,1,0:T(8,128)(2,1)S(1)}, bf16[8,128,384]{2,1,0:T(8,128)(2,1)S(1)}, u32[]{:S(2)}, u32[]{:S(2)}) %collective-permute-start.16) | collective-permute-done | bytes 786464 | tf_op jit(solution)/shard_map/ppermute | solution.py:332
  180.3 2.8 %collective-permute-start.17 = (bf16[4,128,384]{2,1,0:T(8,128)(2,1)S(1)}, bf16[4,128,384]{2,1,0:T(8,128)(2,1)S(1)}, u32[]{:S(2)}, u32[]{:S(2)}) collective-permute-start(bf16[4,128,384]{2,1,0:T(8,128)(2,1)S(1)} %get-tuple-element.24), channel_id=1, source_target_pairs={{0,192},{64,128},{128,64},{192,0},{1,193},{65,129},{129,65},{193,1... | collective-permute-start | bytes 1179656 | tf_op jit(solution)/shard_map/ppermute | solution.py:334
  184.0 4.5 %collective-permute-done.21 = bf16[4,128,384]{2,1,0:T(8,128)(2,1)S(1)} collective-permute-done((bf16[4,128,384]{2,1,0:T(8,128)(2,1)S(1)}, bf16[4,128,384]{2,1,0:T(8,128)(2,1)S(1)}, u32[]{:S(2)}, u32[]{:S(2)}) %collective-permute-start.21) | collective-permute-done | bytes 393248 | tf_op jit(solution)/shard_map/ppermute | solution.py:334
  194.0 2.7 %collective-permute-start.27 = (bf16[128,384]{1,0:T(8,128)(2,1)S(1)}, bf16[128,384]{1,0:T(8,128)(2,1)S(1)}, u32[]{:S(2)}, u32[]{:S(2)}) collective-permute-start(bf16[128,384]{1,0:T(8,128)(2,1)S(1)} %get-tuple-element.39), channel_id=1, source_target_pairs={{0,192},{64,128},{128,64},{192,0},{1,193},{65,129},{129,65},{193,1... | collective-permute-start | bytes 294920 | tf_op jit(solution)/shard_map/ppermute | solution.py:338
  201.5 3.1 %collective-permute-done.19.refs_1_ = bf16[128,384]{1,0:T(8,128)(2,1)S(1)} collective-permute-done((bf16[128,384]{1,0:T(8,128)(2,1)S(1)}, bf16[128,384]{1,0:T(8,128)(2,1)S(1)}, u32[]{:S(2)}, u32[]{:S(2)}) %collective-permute-start.19) | collective-permute-done | bytes 98336 | tf_op jit(solution)/shard_map/ppermute | solution.py:338
  (104 shorter events, 31.2 us)
Async XLA Ops:
  6.5 110.9 %all-gather.3.cloned.1.call-start = ((), (), s32[]{:S(2)}) async-start(), calls=%async_computation | async-start | bytes 20054016 | tf_op jit(solution)/shard_map/all_gather | solution.py:310
  15.9 5.8 %collective-permute-start.12 = (bf16[1,144,384]{2,1,0:T(8,128)(2,1)S(1)}, bf16[1,144,384]{2,1,0:T(8,128)(2,1)S(1)}, u32[]{:S(2)}, u32[]{:S(2)}) collective-permute-start(bf16[1,144,384]{2,1,0:T(8,128)(2,1)S(1)} %get-tuple-element.33), channel_id=1, source_target_pairs={{0,64},{64,0},{128,192},{192,128},{1,65},{65,1},{129,193},{193,129... | collective-permute-start | bytes 331784 | tf_op jit(solution)/shard_map/ppermute | solution.py:296
  16.8 7.1 %collective-permute-start.8 = (bf16[1,144,384]{2,1,0:T(8,128)(2,1)S(1)}, bf16[1,144,384]{2,1,0:T(8,128)(2,1)S(1)}, u32[]{:S(2)}, u32[]{:S(2)}) collective-permute-start(bf16[1,144,384]{2,1,0:T(8,128)(2,1)S(1)} %get-tuple-element.34), channel_id=1, source_target_pairs={{0,192},{64,128},{128,64},{192,0},{1,193},{65,129},{129,65},{193,1... | collective-permute-start | bytes 331784 | tf_op jit(solution)/shard_map/ppermute | solution.py:296
  18.3 5.8 %collective-permute-start.4 = (bf16[1,144,384]{2,1,0:T(8,128)(2,1)S(1)}, bf16[1,144,384]{2,1,0:T(8,128)(2,1)S(1)}, u32[]{:S(2)}, u32[]{:S(2)}) collective-permute-start(bf16[1,144,384]{2,1,0:T(8,128)(2,1)S(1)} %get-tuple-element.35), channel_id=1, source_target_pairs={{0,16},{16,0},{32,48},{48,32},{1,17},{17,1},{33,49},{49,33},{2,18}... | collective-permute-start | bytes 331784 | tf_op jit(solution)/shard_map/ppermute | solution.py:296
  19.5 10.6 %collective-permute-start = (bf16[1,144,384]{2,1,0:T(8,128)(2,1)S(1)}, bf16[1,144,384]{2,1,0:T(8,128)(2,1)S(1)}, u32[]{:S(2)}, u32[]{:S(2)}) collective-permute-start(bf16[1,144,384]{2,1,0:T(8,128)(2,1)S(1)} %get-tuple-element.36), channel_id=1, source_target_pairs={{0,48},{16,32},{32,16},{48,0},{1,49},{17,33},{33,17},{49,1},{2,50}... | collective-permute-start | bytes 331784 | tf_op jit(solution)/shard_map/ppermute | solution.py:296
  21.8 7.3 %collective-permute-start.13 = (bf16[2,144,384]{2,1,0:T(8,128)(2,1)S(1)}, bf16[2,144,384]{2,1,0:T(8,128)(2,1)S(1)}, u32[]{:S(2)}, u32[]{:S(2)}) collective-permute-start(bf16[2,144,384]{2,1,0:T(8,128)(2,1)S(1)} %pad_maximum_fusion.12), channel_id=1, source_target_pairs={{0,192},{64,128},{128,64},{192,0},{1,193},{65,129},{129,65},{193,1... | collective-permute-start | bytes 663560 | tf_op jit(solution)/shard_map/ppermute | solution.py:296
  24.0 7.4 %collective-permute-start.9 = (bf16[2,144,384]{2,1,0:T(8,128)(2,1)S(1)}, bf16[2,144,384]{2,1,0:T(8,128)(2,1)S(1)}, u32[]{:S(2)}, u32[]{:S(2)}) collective-permute-start(bf16[2,144,384]{2,1,0:T(8,128)(2,1)S(1)} %pad_maximum_fusion.11), channel_id=1, source_target_pairs={{0,64},{64,0},{128,192},{192,128},{1,65},{65,1},{129,193},{193,129... | collective-permute-start | bytes 663560 | tf_op jit(solution)/shard_map/ppermute | solution.py:296
  24.1 9.8 %collective-permute-start.5 = (bf16[2,144,384]{2,1,0:T(8,128)(2,1)S(1)}, bf16[2,144,384]{2,1,0:T(8,128)(2,1)S(1)}, u32[]{:S(2)}, u32[]{:S(2)}) collective-permute-start(bf16[2,144,384]{2,1,0:T(8,128)(2,1)S(1)} %pad_maximum_fusion.10), channel_id=1, source_target_pairs={{0,48},{16,32},{32,16},{48,0},{1,49},{17,33},{33,17},{49,1},{2,50}... | collective-permute-start | bytes 663560 | tf_op jit(solution)/shard_map/ppermute | solution.py:296
  29.2 17.0 %collective-permute-start.14 = (bf16[4,144,384]{2,1,0:T(8,128)(2,1)S(1)}, bf16[4,144,384]{2,1,0:T(8,128)(2,1)S(1)}, u32[]{:S(2)}, u32[]{:S(2)}) collective-permute-start(bf16[4,144,384]{2,1,0:T(8,128)(2,1)S(1)} %pad_maximum_fusion.8), channel_id=1, source_target_pairs={{0,16},{16,0},{32,48},{48,32},{1,17},{17,1},{33,49},{49,33},{2,18}... | collective-permute-start | bytes 1327112 | tf_op jit(solution)/shard_map/ppermute | solution.py:296
  30.2 13.7 %collective-permute-start.1 = (bf16[2,144,384]{2,1,0:T(8,128)(2,1)S(1)}, bf16[2,144,384]{2,1,0:T(8,128)(2,1)S(1)}, u32[]{:S(2)}, u32[]{:S(2)}) collective-permute-start(bf16[2,144,384]{2,1,0:T(8,128)(2,1)S(1)} %pad_maximum_fusion.9), channel_id=1, source_target_pairs={{0,16},{16,0},{32,48},{48,32},{1,17},{17,1},{33,49},{49,33},{2,18}... | collective-permute-start | bytes 663560 | tf_op jit(solution)/shard_map/ppermute | solution.py:296
  31.5 15.9 %collective-permute-start.10 = (bf16[4,144,384]{2,1,0:T(8,128)(2,1)S(1)}, bf16[4,144,384]{2,1,0:T(8,128)(2,1)S(1)}, u32[]{:S(2)}, u32[]{:S(2)}) collective-permute-start(bf16[4,144,384]{2,1,0:T(8,128)(2,1)S(1)} %pad_maximum_fusion.7), channel_id=1, source_target_pairs={{0,48},{16,32},{32,16},{48,0},{1,49},{17,33},{33,17},{49,1},{2,50}... | collective-permute-start | bytes 1327112 | tf_op jit(solution)/shard_map/ppermute | solution.py:296
  34.0 13.8 %collective-permute-start.6 = (bf16[4,144,384]{2,1,0:T(8,128)(2,1)S(1)}, bf16[4,144,384]{2,1,0:T(8,128)(2,1)S(1)}, u32[]{:S(2)}, u32[]{:S(2)}) collective-permute-start(bf16[4,144,384]{2,1,0:T(8,128)(2,1)S(1)} %pad_maximum_fusion.6), channel_id=1, source_target_pairs={{0,64},{64,0},{128,192},{192,128},{1,65},{65,1},{129,193},{193,129... | collective-permute-start | bytes 1327112 | tf_op jit(solution)/shard_map/ppermute | solution.py:296
  43.9 14.4 %collective-permute-start.2 = (bf16[4,144,384]{2,1,0:T(8,128)(2,1)S(1)}, bf16[4,144,384]{2,1,0:T(8,128)(2,1)S(1)}, u32[]{:S(2)}, u32[]{:S(2)}) collective-permute-start(bf16[4,144,384]{2,1,0:T(8,128)(2,1)S(1)} %pad_maximum_fusion.5), channel_id=1, source_target_pairs={{0,192},{64,128},{128,64},{192,0},{1,193},{65,129},{129,65},{193,1... | collective-permute-start | bytes 1327112 | tf_op jit(solution)/shard_map/ppermute | solution.py:296
  46.3 19.8 %collective-permute-start.15 = (bf16[8,144,384]{2,1,0:T(8,128)(2,1)S(1)}, bf16[8,144,384]{2,1,0:T(8,128)(2,1)}, u32[]{:S(2)}, u32[]{:S(2)}) collective-permute-start(bf16[8,144,384]{2,1,0:T(8,128)(2,1)S(1)} %pad_maximum_fusion.4.refs_6_), channel_id=1, source_target_pairs={{0,48},{16,32},{32,16},{48,0},{1,49},{17,33},{33,17},{49,1},{2,50}... | collective-permute-start | bytes 2654216 | tf_op jit(solution)/shard_map/ppermute | solution.py:297
  47.5 18.6 %collective-permute-start.11 = (bf16[8,144,384]{2,1,0:T(8,128)(2,1)S(1)}, bf16[8,144,384]{2,1,0:T(8,128)(2,1)}, u32[]{:S(2)}, u32[]{:S(2)}) collective-permute-start(bf16[8,144,384]{2,1,0:T(8,128)(2,1)S(1)} %pad_maximum_fusion.3.refs_4_), channel_id=1, source_target_pairs={{0,16},{16,0},{32,48},{48,32},{1,17},{17,1},{33,49},{49,33},{2,18}... | collective-permute-start | bytes 2654216 | tf_op jit(solution)/shard_map/ppermute | solution.py:297
  47.9 25.4 %collective-permute-start.7 = (bf16[8,144,384]{2,1,0:T(8,128)(2,1)S(1)}, bf16[8,144,384]{2,1,0:T(8,128)(2,1)}, u32[]{:S(2)}, u32[]{:S(2)}) collective-permute-start(bf16[8,144,384]{2,1,0:T(8,128)(2,1)S(1)} %pad_maximum_fusion.2.refs_2_), channel_id=1, source_target_pairs={{0,192},{64,128},{128,64},{192,0},{1,193},{65,129},{129,65},{193,1... | collective-permute-start | bytes 2654216 | tf_op jit(solution)/shard_map/ppermute | solution.py:297
  59.4 13.9 %collective-permute-start.3 = (bf16[8,144,384]{2,1,0:T(8,128)(2,1)}, bf16[8,144,384]{2,1,0:T(8,128)(2,1)}, u32[]{:S(2)}, u32[]{:S(2)}) collective-permute-start(bf16[8,144,384]{2,1,0:T(8,128)(2,1)} %pad_maximum_fusion.1.refs_0_), channel_id=1, source_target_pairs={{0,64},{64,0},{128,192},{192,128},{1,65},{65,1},{129,193},{193,129... | collective-permute-start | bytes 2654216 | tf_op jit(solution)/shard_map/ppermute | solution.py:297
  133.3 27.1 %collective-permute-start.28 = (bf16[8,128,384]{2,1,0:T(8,128)(2,1)S(1)}, bf16[8,128,384]{2,1,0:T(8,128)(2,1)S(1)}, u32[]{:S(2)}, u32[]{:S(2)}) collective-permute-start(bf16[8,128,384]{2,1,0:T(8,128)(2,1)S(1)} %spread.11), channel_id=1, source_target_pairs={{0,48},{16,32},{32,16},{48,0},{1,49},{17,33},{33,17},{49,1},{2,50}... | collective-permute-start | bytes 2359304 | tf_op jit(solution)/shard_map/ppermute | solution.py:332
  139.4 23.2 %collective-permute-start.24 = (bf16[8,128,384]{2,1,0:T(8,128)(2,1)S(1)}, bf16[8,128,384]{2,1,0:T(8,128)(2,1)S(1)}, u32[]{:S(2)}, u32[]{:S(2)}) collective-permute-start(bf16[8,128,384]{2,1,0:T(8,128)(2,1)S(1)} %spread.10), channel_id=1, source_target_pairs={{0,16},{16,0},{32,48},{48,32},{1,17},{17,1},{33,49},{49,33},{2,18}... | collective-permute-start | bytes 2359304 | tf_op jit(solution)/shard_map/ppermute | solution.py:332
  142.9 20.4 %collective-permute-start.20 = (bf16[8,128,384]{2,1,0:T(8,128)(2,1)S(1)}, bf16[8,128,384]{2,1,0:T(8,128)(2,1)S(1)}, u32[]{:S(2)}, u32[]{:S(2)}) collective-permute-start(bf16[8,128,384]{2,1,0:T(8,128)(2,1)S(1)} %spread.9), channel_id=1, source_target_pairs={{0,192},{64,128},{128,64},{192,0},{1,193},{65,129},{129,65},{193,1... | collective-permute-start | bytes 2359304 | tf_op jit(solution)/shard_map/ppermute | solution.py:332
  159.5 20.6 %collective-permute-start.16 = (bf16[8,128,384]{2,1,0:T(8,128)(2,1)S(1)}, bf16[8,128,384]{2,1,0:T(8,128)(2,1)S(1)}, u32[]{:S(2)}, u32[]{:S(2)}) collective-permute-start(bf16[8,128,384]{2,1,0:T(8,128)(2,1)S(1)} %spread.8), channel_id=1, source_target_pairs={{0,64},{64,0},{128,192},{192,128},{1,65},{65,1},{129,193},{193,129... | collective-permute-start | bytes 2359304 | tf_op jit(solution)/shard_map/ppermute | solution.py:332
  160.6 22.4 %collective-permute-start.29 = (bf16[4,128,384]{2,1,0:T(8,128)(2,1)S(1)}, bf16[4,128,384]{2,1,0:T(8,128)(2,1)S(1)}, u32[]{:S(2)}, u32[]{:S(2)}) collective-permute-start(bf16[4,128,384]{2,1,0:T(8,128)(2,1)S(1)} %get-tuple-element.18), channel_id=1, source_target_pairs={{0,16},{16,0},{32,48},{48,32},{1,17},{17,1},{33,49},{49,33},{2,18}... | collective-permute-start | bytes 1179656 | tf_op jit(solution)/shard_map/ppermute | solution.py:334
  162.7 21.1 %collective-permute-start.25 = (bf16[4,128,384]{2,1,0:T(8,128)(2,1)S(1)}, bf16[4,128,384]{2,1,0:T(8,128)(2,1)S(1)}, u32[]{:S(2)}, u32[]{:S(2)}) collective-permute-start(bf16[4,128,384]{2,1,0:T(8,128)(2,1)S(1)} %get-tuple-element.20), channel_id=1, source_target_pairs={{0,48},{16,32},{32,16},{48,0},{1,49},{17,33},{33,17},{49,1},{2,50}... | collective-permute-start | bytes 1179656 | tf_op jit(solution)/shard_map/ppermute | solution.py:334
  163.6 24.9 %collective-permute-start.21 = (bf16[4,128,384]{2,1,0:T(8,128)(2,1)S(1)}, bf16[4,128,384]{2,1,0:T(8,128)(2,1)S(1)}, u32[]{:S(2)}, u32[]{:S(2)}) collective-permute-start(bf16[4,128,384]{2,1,0:T(8,128)(2,1)S(1)} %get-tuple-element.22), channel_id=1, source_target_pairs={{0,64},{64,0},{128,192},{192,128},{1,65},{65,1},{129,193},{193,129... | collective-permute-start | bytes 1179656 | tf_op jit(solution)/shard_map/ppermute | solution.py:334
  180.3 11.4 %collective-permute-start.17 = (bf16[4,128,384]{2,1,0:T(8,128)(2,1)S(1)}, bf16[4,128,384]{2,1,0:T(8,128)(2,1)S(1)}, u32[]{:S(2)}, u32[]{:S(2)}) collective-permute-start(bf16[4,128,384]{2,1,0:T(8,128)(2,1)S(1)} %get-tuple-element.24), channel_id=1, source_target_pairs={{0,192},{64,128},{128,64},{192,0},{1,193},{65,129},{129,65},{193,1... | collective-permute-start | bytes 1179656 | tf_op jit(solution)/shard_map/ppermute | solution.py:334
  183.2 10.6 %collective-permute-start.30 = (bf16[2,128,384]{2,1,0:T(8,128)(2,1)S(1)}, bf16[2,128,384]{2,1,0:T(8,128)(2,1)S(1)}, u32[]{:S(2)}, u32[]{:S(2)}) collective-permute-start(bf16[2,128,384]{2,1,0:T(8,128)(2,1)S(1)} %get-tuple-element.26), channel_id=1, source_target_pairs={{0,192},{64,128},{128,64},{192,0},{1,193},{65,129},{129,65},{193,1... | collective-permute-start | bytes 589832 | tf_op jit(solution)/shard_map/ppermute | solution.py:336
  183.9 10.1 %collective-permute-start.26 = (bf16[2,128,384]{2,1,0:T(8,128)(2,1)S(1)}, bf16[2,128,384]{2,1,0:T(8,128)(2,1)S(1)}, u32[]{:S(2)}, u32[]{:S(2)}) collective-permute-start(bf16[2,128,384]{2,1,0:T(8,128)(2,1)S(1)} %get-tuple-element.28), channel_id=1, source_target_pairs={{0,64},{64,0},{128,192},{192,128},{1,65},{65,1},{129,193},{193,129... | collective-permute-start | bytes 589832 | tf_op jit(solution)/shard_map/ppermute | solution.py:336
  188.6 8.2 %collective-permute-start.22 = (bf16[2,128,384]{2,1,0:T(8,128)(2,1)S(1)}, bf16[2,128,384]{2,1,0:T(8,128)(2,1)S(1)}, u32[]{:S(2)}, u32[]{:S(2)}) collective-permute-start(bf16[2,128,384]{2,1,0:T(8,128)(2,1)S(1)} %get-tuple-element.30), channel_id=1, source_target_pairs={{0,48},{16,32},{32,16},{48,0},{1,49},{17,33},{33,17},{49,1},{2,50}... | collective-permute-start | bytes 589832 | tf_op jit(solution)/shard_map/ppermute | solution.py:336
  191.8 6.8 %collective-permute-start.18 = (bf16[2,128,384]{2,1,0:T(8,128)(2,1)S(1)}, bf16[2,128,384]{2,1,0:T(8,128)(2,1)S(1)}, u32[]{:S(2)}, u32[]{:S(2)}) collective-permute-start(bf16[2,128,384]{2,1,0:T(8,128)(2,1)S(1)} %get-tuple-element.32), channel_id=1, source_target_pairs={{0,16},{16,0},{32,48},{48,32},{1,17},{17,1},{33,49},{49,33},{2,18}... | collective-permute-start | bytes 589832 | tf_op jit(solution)/shard_map/ppermute | solution.py:336
  193.9 5.8 %collective-permute-start.31 = (bf16[128,384]{1,0:T(8,128)(2,1)S(1)}, bf16[128,384]{1,0:T(8,128)(2,1)S(1)}, u32[]{:S(2)}, u32[]{:S(2)}) collective-permute-start(bf16[128,384]{1,0:T(8,128)(2,1)S(1)} %get-tuple-element.37), channel_id=1, source_target_pairs={{0,64},{64,0},{128,192},{192,128},{1,65},{65,1},{129,193},{193,129... | collective-permute-start | bytes 294920 | tf_op jit(solution)/shard_map/ppermute | solution.py:338
  194.0 5.9 %collective-permute-start.27 = (bf16[128,384]{1,0:T(8,128)(2,1)S(1)}, bf16[128,384]{1,0:T(8,128)(2,1)S(1)}, u32[]{:S(2)}, u32[]{:S(2)}) collective-permute-start(bf16[128,384]{1,0:T(8,128)(2,1)S(1)} %get-tuple-element.39), channel_id=1, source_target_pairs={{0,192},{64,128},{128,64},{192,0},{1,193},{65,129},{129,65},{193,1... | collective-permute-start | bytes 294920 | tf_op jit(solution)/shard_map/ppermute | solution.py:338
  198.7 5.9 %collective-permute-start.19 = (bf16[128,384]{1,0:T(8,128)(2,1)S(1)}, bf16[128,384]{1,0:T(8,128)(2,1)S(1)}, u32[]{:S(2)}, u32[]{:S(2)}) collective-permute-start(bf16[128,384]{1,0:T(8,128)(2,1)S(1)} %get-tuple-element.43), channel_id=1, source_target_pairs={{0,48},{16,32},{32,16},{48,0},{1,49},{17,33},{33,17},{49,1},{2,50}... | collective-permute-start | bytes 294920 | tf_op jit(solution)/shard_map/ppermute | solution.py:338
  (15 other events, 73.9 us)
Sparse Core Ops, SparseCore 0:
  9.2 108.1 all-gather.2

commit v2 on v1

--- a/solution.py
+++ b/solution.py
@@ -203,7 +203,7 @@
 
 
 def hidden_units(packed, weights):
-    width = 256
+    width = FF
 
     def block(which):
         return pl.BlockSpec(
@@ -221,48 +221,58 @@
     )(packed, weights, weights)
 
 
-def spread_kernel(plan, start, place_ref, act_ref, down_ref, scale_ref, spread_ref, out_ref, part_ref):
+def spread_kernel(start, place_ref, act_ref, scale_ref, spread_ref, weights_ref, *refs):
+    out_refs, (down_ref, part_ref, sems) = refs[:LOCAL], refs[LOCAL:]
     x, y = place_ref[0], place_ref[1]
     half = BLOCKS // 2
-    order = [block_at(plan, x, y, start + i) for i in range(half)]
-    for s in range(LOCAL):
-        rows = jnp.concatenate([act_ref[s, b] for b in order])
-        scale = jnp.concatenate([scale_ref[s, b] for b in order])
-        down = down_ref[s // 2, :, 0, s % 2].reshape(GROUP, FF)
-        part = lax.dot_general(
-            rows, down, (((1,), (1,)), ((), ())), preferred_element_type=F32
-        )
-        part_ref[:, s] = (part * scale).astype(BF16).reshape(half, CAP, GROUP)
-
-    def back(i):
-        b = block_at(plan, x, y, start + i)
-        rows = part_ref[i].reshape(LOCAL * CAP, GROUP)
-        out_ref[i] = jnp.dot(spread_ref[b], rows, preferred_element_type=F32).astype(BF16)
-
-    each(half, 4, back)
-
-
-def spread_rows(place, act, weights, scale, spread, group, start):
+    copies = [
+        pltpu.make_async_copy(
+            weights_ref.at[:, 2 * group : 2 * group + 2, 2], down_ref.at[group], sems.at[group]
+        )
+        for group in range(LOCAL)
+    ]
+    for copy in copies:
+        copy.start()
+    for group, plan in enumerate(PLANS):
+        order = [block_at(plan, x, y, start + i) for i in range(half)]
+        copies[group].wait()
+        for s in range(LOCAL):
+            rows = jnp.concatenate([act_ref[s, b] for b in order])
+            scale = jnp.concatenate([scale_ref[s, b] for b in order])
+            down = down_ref[group, s // 2, :, s % 2].reshape(GROUP, FF)
+            part = lax.dot_general(
+                rows, down, (((1,), (1,)), ((), ())), preferred_element_type=F32
+            )
+            part_ref[:, s] = (part * scale).astype(BF16).reshape(half, CAP, GROUP)
+
+        def back(i):
+            b = block_at(plan, x, y, start + i)
+            rows = part_ref[i].reshape(LOCAL * CAP, GROUP)
+            out = jnp.dot(spread_ref[b], rows, preferred_element_type=F32)
+            out_refs[group][i] = out.astype(BF16)
+
+        each(half, 4, back)
+
+
+def spread_rows(place, act, weights, scale, spread, start):
     half = BLOCKS // 2
-    whole = lambda array: pl.BlockSpec(array.shape, lambda i, o: (0,) * array.ndim)
-    return pl.pallas_call(
-        functools.partial(spread_kernel, PLANS[group], start),
-        grid_spec=pltpu.PrefetchScalarGridSpec(
-            num_scalar_prefetch=1,
-            grid=(1,),
-            in_specs=[
-                whole(act),
-                pl.BlockSpec((2, 2, 1, 2, CHUNK, FF), lambda i, o: (0, group, 2, 0, 0, 0)),
-                whole(scale),
-                whole(spread),
-            ],
-            out_specs=pl.BlockSpec((half, ROWS, GROUP), lambda i, o: (0, 0, 0)),
-            scratch_shapes=[pltpu.VMEM((half, LOCAL, CAP, GROUP), BF16)],
-        ),
-        out_shape=jax.ShapeDtypeStruct((half, ROWS, GROUP), BF16),
-        compiler_params=params(16, "arbitrary"),
+    vmem = pl.BlockSpec(memory_space=pltpu.VMEM)
+    return pl.pallas_call(
+        functools.partial(spread_kernel, start),
+        in_specs=[
+            pl.BlockSpec(memory_space=pltpu.SMEM), vmem, vmem, vmem,
+            pl.BlockSpec(memory_space=pltpu.HBM),
+        ],
+        out_specs=[vmem] * LOCAL,
+        out_shape=[jax.ShapeDtypeStruct((half, ROWS, GROUP), BF16)] * LOCAL,
+        scratch_shapes=[
+            pltpu.VMEM((LOCAL, 2, 2, 2, CHUNK, FF), BF16),
+            pltpu.VMEM((half, LOCAL, CAP, GROUP), BF16),
+            pltpu.SemaphoreType.DMA((LOCAL,)),
+        ],
+        compiler_params=params(24),
         name="spread",
-    )(place, act, weights, scale, spread)
+    )(place, act, scale, spread, weights)
 
 
 def closing_kernel(hidden_ref, gain_ref, *refs):
@@ -320,13 +330,9 @@
     packed = pltpu.with_memory_space_constraint(packed, pltpu.HBM)
     act = hidden_units(packed, weights)
 
-    halves = []
-    for start in (BLOCKS // 2, 0):
-        done = [half for group in halves for half in group]
-        act = lax.optimization_barrier((act, *done))[0]
-        halves.append(
-            [spread_rows(place, act, weights, scale, spread, g, start) for g in range(LOCAL)]
-        )
+    sends = spread_rows(place, act, weights, scale, spread, BLOCKS // 2)
+    act = lax.optimization_barrier((act, *sends))[0]
+    halves = [sends, spread_rows(place, act, weights, scale, spread, 0)]
     pairs = []
     for send, kept, (big, small, first, other) in zip(*halves, PLANS):
         got = lax.ppermute(send, big, links(first))

time: 213 us -> 195 us (0.915)
  Pallas kernels: 54.1 us -> 40.4 us
  starting transfers between devices: 42.5 us -> 38.6 us
    pallas_call x8 -> x2, Pallas kernels: 25.5 us -> 14.1 us  [spread_rows(): pl.pallas_call(functools.partial(spread_kernel, start), in_specs=[pl.Bloc...]
    ppermute x4, waiting for transfers between devices: 15.1 us -> 10.2 us  [body(): got = lax.ppermute(send, big, links(first))]
    ppermute x4, starting transfers between devices: 5.56 us -> 2.63 us  [body(): pairs += [kept, lax.ppermute(send, small, links(other))]]
    ppermute x4, waiting for transfers between devices: 0.26 us -> 2.87 us  [body(): got = lax.ppermute(send, small, links(first))]
    pallas_call x1, Pallas kernels: 12.7 us -> 10.4 us  [hidden_units(): pl.pallas_call(hidden_units_kernel, grid=(LOCAL, FF // width), in_specs=[...]
  transfers between devices with their start and end apart: 33 -> 33, of which waited for: 14 -> 16; matrix products, arithmetic and copies ran while one was open for 2% -> 2% of each run, Pallas kernels for 18% -> 11%
where the time goes in v2:
time: 195 us
  waiting for transfers between devices  89.1 us (46%)
  Pallas kernels  40.4 us (21%)
  starting transfers between devices  38.6 us (20%)
  between operations  13.7 us (7%)
  local copies, waits for them, and re-layouts  7.39 us (4%)
  other arithmetic  5.67 us (3%)
    all_gather x1, waiting for transfers between devices, body(): weights = lax.all_gather(joined, ('core', 'blk'), axis=0, tiled=False)  28.7 us
    ppermute x12, waiting for transfers between devices, spread_out(): held = jnp.concatenate([held, lax.ppermute(held, axis, links(turn))])  19.9 us
    ppermute x12, starting transfers between devices, spread_out(): held = jnp.concatenate([held, lax.ppermute(held, axis, links(turn))])  17.8 us
    pallas_call x2, Pallas kernels, spread_rows(): pl.pallas_call(functools.partial(spread_kernel, start), in_specs=[pl.Bloc...  14.1 us
    ppermute x4, waiting for transfers between devices, spread_out(): halves += [held, lax.ppermute(held, big, links(first))]  13.8 us
    pallas_call x1, Pallas kernels, compact(): pl.pallas_call(compact_kernel, in_specs=[pl.BlockSpec(memory_space=pltpu....  11.5 us
    pallas_call x1, Pallas kernels, hidden_units(): pl.pallas_call(hidden_units_kernel, grid=(LOCAL, FF // width), in_specs=[...  10.4 us
    ppermute x4, waiting for transfers between devices, body(): got = lax.ppermute(send, big, links(first))  10.2 us
  transfers between devices with their start and end apart: 33, of which 16 were waited for; matrix products, arithmetic and copies ran while one was open for 2% of the time, Pallas kernels for 11%

profile of v2, /device:TPU:6, one launch (start us, length us, event | category | flops | bytes accessed | tf_op | source)
XLA Modules:
  0.0 194.9 jit_solution(6111199794331080423)
XLA Ops:
  6.5 2.4 %pad_maximum_fusion = bf16[3,2,192,512]{3,2,1,0:T(8,128)(2,1)} fusion(bf16[1,2,192,512]{3,2,1,0:T(8,128)(2,1)} %bitcast.34, bf16[1,2,192,512]{3,2,1,0:T(8,128)(2,1)} %bitcast.35, bf16[1,2,192,512]{3,2,1,0:T(8,128)(2,1)} %bitcast.36), kind=kLoop, calls=%fused_computation | loop fusion | flops 1179648 | bytes 2359296 | tf_op jit(solution)/shard_map/stack | solution.py:319
  10.1 2.3 %copy-done.1 = bf16[1536,1536]{1,0:T(8,128)(2,1)S(1)} copy-done((bf16[1536,1536]{1,0:T(8,128)(2,1)S(1)}, bf16[1536,1536]{1,0:T(8,128)(2,1)}, u32[]{:S(2)}) %copy-start.1) | copy-done | bytes 4718616
  12.4 3.4 %entry.1 = (f32[128,1536]{1,0:T(8,128)S(1)}, bf16[4,144,384]{2,1,0:T(8,128)(2,1)S(1)}) custom-call(bf16[128,1536]{1,0:T(8,128)(2,1)S(1)} %copy-done.6, bf16[128,1536]{1,0:T(8,128)(2,1)S(1)} %copy-done.7, bf16[1536,1536]{1,0:T(8,128)(2,1)S(1)} %copy-done.1, f32[1,1536]{1,0:T(1,128)S(1)} %reshape.47.gain_ref, f32[40,1536]{1,0:T(8,128)S(1)} %bitcast.26, ...), custom_call_target="tpu_custom_call" | custom-call | tf_op jit(solution)/shard_map/entry/pallas_call | solution.py:105
  16.8 1.5 collective-permute-start.8
  19.5 2.2 %collective-permute-start = (bf16[1,144,384]{2,1,0:T(8,128)(2,1)S(1)}, bf16[1,144,384]{2,1,0:T(8,128)(2,1)S(1)}, u32[]{:S(2)}, u32[]{:S(2)}) collective-permute-start(bf16[1,144,384]{2,1,0:T(8,128)(2,1)S(1)} %get-tuple-element.52), channel_id=1, source_target_pairs={{0,48},{16,32},{32,16},{48,0},{1,49},{17,33},{33,17},{49,1},{2,50}... | collective-permute-start | bytes 331784 | tf_op jit(solution)/shard_map/ppermute | solution.py:306
  21.8 2.2 %collective-permute-start.13 = (bf16[2,144,384]{2,1,0:T(8,128)(2,1)S(1)}, bf16[2,144,384]{2,1,0:T(8,128)(2,1)S(1)}, u32[]{:S(2)}, u32[]{:S(2)}) collective-permute-start(bf16[2,144,384]{2,1,0:T(8,128)(2,1)S(1)} %pad_maximum_fusion.12), channel_id=1, source_target_pairs={{0,192},{64,128},{128,64},{192,0},{1,193},{65,129},{129,65},{193,1... | collective-permute-start | bytes 663560 | tf_op jit(solution)/shard_map/ppermute | solution.py:306
  24.1 1.9 collective-permute-start.5
  26.1 3.0 %collective-permute-done.13 = bf16[2,144,384]{2,1,0:T(8,128)(2,1)S(1)} collective-permute-done((bf16[2,144,384]{2,1,0:T(8,128)(2,1)S(1)}, bf16[2,144,384]{2,1,0:T(8,128)(2,1)S(1)}, u32[]{:S(2)}, u32[]{:S(2)}) %collective-permute-start.13) | collective-permute-done | bytes 221216 | tf_op jit(solution)/shard_map/ppermute | solution.py:306
  31.5 2.4 %collective-permute-start.10 = (bf16[4,144,384]{2,1,0:T(8,128)(2,1)S(1)}, bf16[4,144,384]{2,1,0:T(8,128)(2,1)S(1)}, u32[]{:S(2)}, u32[]{:S(2)}) collective-permute-start(bf16[4,144,384]{2,1,0:T(8,128)(2,1)S(1)} %pad_maximum_fusion.7), channel_id=1, source_target_pairs={{0,48},{16,32},{32,16},{48,0},{1,49},{17,33},{33,17},{49,1},{2,50}... | collective-permute-start | bytes 1327112 | tf_op jit(solution)/shard_map/ppermute | solution.py:306
  34.8 9.0 %collective-permute-done.1 = bf16[2,144,384]{2,1,0:T(8,128)(2,1)S(1)} collective-permute-done((bf16[2,144,384]{2,1,0:T(8,128)(2,1)S(1)}, bf16[2,144,384]{2,1,0:T(8,128)(2,1)S(1)}, u32[]{:S(2)}, u32[]{:S(2)}) %collective-permute-start.1) | collective-permute-done | bytes 221216 | tf_op jit(solution)/shard_map/ppermute | solution.py:306
  43.9 2.3 %collective-permute-start.2 = (bf16[4,144,384]{2,1,0:T(8,128)(2,1)S(1)}, bf16[4,144,384]{2,1,0:T(8,128)(2,1)S(1)}, u32[]{:S(2)}, u32[]{:S(2)}) collective-permute-start(bf16[4,144,384]{2,1,0:T(8,128)(2,1)S(1)} %pad_maximum_fusion.5), channel_id=1, source_target_pairs={{0,192},{64,128},{128,64},{192,0},{1,193},{65,129},{129,65},{193,1... | collective-permute-start | bytes 1327112 | tf_op jit(solution)/shard_map/ppermute | solution.py:306
  47.9 2.7 %collective-permute-start.7 = (bf16[8,144,384]{2,1,0:T(8,128)(2,1)S(1)}, bf16[8,144,384]{2,1,0:T(8,128)(2,1)}, u32[]{:S(2)}, u32[]{:S(2)}) collective-permute-start(bf16[8,144,384]{2,1,0:T(8,128)(2,1)S(1)} %pad_maximum_fusion.2.refs_2_), channel_id=1, source_target_pairs={{0,192},{64,128},{128,64},{192,0},{1,193},{65,129},{129,65},{193,1... | collective-permute-start | bytes 2654216 | tf_op jit(solution)/shard_map/ppermute | solution.py:307
  50.6 7.8 %collective-permute-done.2 = bf16[4,144,384]{2,1,0:T(8,128)(2,1)S(1)} collective-permute-done((bf16[4,144,384]{2,1,0:T(8,128)(2,1)S(1)}, bf16[4,144,384]{2,1,0:T(8,128)(2,1)S(1)}, u32[]{:S(2)}, u32[]{:S(2)}) %collective-permute-start.2) | collective-permute-done | bytes 442400 | tf_op jit(solution)/shard_map/ppermute | solution.py:306
  59.5 6.6 %collective-permute-done.15.refs_7_ = bf16[8,144,384]{2,1,0:T(8,128)(2,1)} collective-permute-done((bf16[8,144,384]{2,1,0:T(8,128)(2,1)S(1)}, bf16[8,144,384]{2,1,0:T(8,128)(2,1)}, u32[]{:S(2)}, u32[]{:S(2)}) %collective-permute-start.15) | collective-permute-done | bytes 884768 | tf_op jit(solution)/shard_map/ppermute | solution.py:307
  66.1 7.2 %collective-permute-done.7.refs_3_ = bf16[8,144,384]{2,1,0:T(8,128)(2,1)} collective-permute-done((bf16[8,144,384]{2,1,0:T(8,128)(2,1)S(1)}, bf16[8,144,384]{2,1,0:T(8,128)(2,1)}, u32[]{:S(2)}, u32[]{:S(2)}) %collective-permute-start.7) | collective-permute-done | bytes 884768 | tf_op jit(solution)/shard_map/ppermute | solution.py:307
  74.5 11.5 %compact.1 = (bf16[4,16,32,1536]{3,2,1,0:T(8,128)(2,1)S(1)}, bf16[16,128,128]{2,1,0:T(8,128)(2,1)S(1)}, f32[4,16,32,1]{3,2,1,0:T(8,128)S(1)}) custom-call(s32[2]{0:T(128)S(1)} %pad_add_fusion.place_ref, bf16[8,144,384]{2,1,0:T(8,128)(2,1)} %pad_maximum_fusion.1.refs_0_, bf16[8,144,384]{2,1,0:T(8,128)(2,1)} %collective-permute-done.3.refs_1_, ...), custom_call_target="tpu_custom_call" | custom-call | tf_op jit(solution)/shard_map/compact/pallas_call | solution.py:178
  86.1 2.7 %copy-done = bf16[4,16,32,1536]{3,2,1,0:T(8,128)(2,1)} copy-done((bf16[4,16,32,1536]{3,2,1,0:T(8,128)(2,1)}, bf16[4,16,32,1536]{3,2,1,0:T(8,128)(2,1)S(1)}, u32[]{:S(2)}) %copy-start) | copy-done | bytes 6291480
  88.7 28.7 %all-gather.3.cloned.1.call-done = bf16[48,2,192,512]{3,2,1,0:T(8,128)(2,1)} async-done(((bf16[3,2,192,512]{3,2,1,0:T(8,128)(2,1)}), bf16[48,2,192,512]{3,2,1,0:T(8,128)(2,1)}) %all-gather.3.cloned.1.call-update) | async-done | bytes 18874384 | tf_op jit(solution)/shard_map/all_gather | solution.py:320
  117.4 10.4 %hidden_units.1.act_ref = bf16[4,16,32,512]{3,2,1,0:T(8,128)(2,1)S(1)} custom-call(bf16[4,16,32,1536]{3,2,1,0:T(8,128)(2,1)} %copy-done, bf16[2,8,3,2,192,512]{5,4,3,2,1,0:T(8,128)(2,1)} %bitcast.30, bf16[2,8,3,2,192,512]{5,4,3,2,1,0:T(8,128)(2,1)} %bitcast.31), custom_call_target="tpu_custom_call" | custom-call | tf_op jit(solution)/shard_map/hidden_units/pallas_call | solution.py:213
  127.8 7.0 %spread.2 = (bf16[8,128,384]{2,1,0:T(8,128)(2,1)S(1)}, bf16[8,128,384]{2,1,0:T(8,128)(2,1)S(1)}, bf16[8,128,384]{2,1,0:T(8,128)(2,1)S(1)}, bf16[8,128,384]{2,1,0:T(8,128)(2,1)S(1)}) custom-call(s32[2]{0:T(128)S(1)} %pad_add_fusion.place_ref, bf16[4,16,32,512]{3,2,1,0:T(8,128)(2,1)S(1)} %hidden_units.1.act_ref, ...), custom_call_target="tpu_custom_call" | custom-call | tf_op jit(solution)/shard_map/spread/pallas_call | solution.py:260
  134.9 2.8 %collective-permute-start.28 = (bf16[8,128,384]{2,1,0:T(8,128)(2,1)S(1)}, bf16[8,128,384]{2,1,0:T(8,128)(2,1)S(1)}, u32[]{:S(2)}, u32[]{:S(2)}) collective-permute-start(bf16[8,128,384]{2,1,0:T(8,128)(2,1)S(1)} %get-tuple-element.27), channel_id=1, source_target_pairs={{0,48},{16,32},{32,16},{48,0},{1,49},{17,33},{33,17},{49,1},{2,50}... | collective-permute-start | bytes 2359304 | tf_op jit(solution)/shard_map/ppermute | solution.py:338
  139.4 7.0 %spread.3 = (bf16[8,128,384]{2,1,0:T(8,128)(2,1)S(1)}, bf16[8,128,384]{2,1,0:T(8,128)(2,1)S(1)}, bf16[8,128,384]{2,1,0:T(8,128)(2,1)S(1)}, bf16[8,128,384]{2,1,0:T(8,128)(2,1)S(1)}) custom-call(s32[2]{0:T(128)S(1)} %pad_add_fusion.place_ref, bf16[4,16,32,512]{3,2,1,0:T(8,128)(2,1)S(1)} %hidden_units.1.act_ref, ...), custom_call_target="tpu_custom_call" | custom-call | tf_op jit(solution)/shard_map/spread/pallas_call | solution.py:260
  146.4 9.5 %collective-permute-done.28 = bf16[8,128,384]{2,1,0:T(8,128)(2,1)S(1)} collective-permute-done((bf16[8,128,384]{2,1,0:T(8,128)(2,1)S(1)}, bf16[8,128,384]{2,1,0:T(8,128)(2,1)S(1)}, u32[]{:S(2)}, u32[]{:S(2)}) %collective-permute-start.28) | collective-permute-done | bytes 786464 | tf_op jit(solution)/shard_map/ppermute | solution.py:338
  157.4 2.1 %collective-permute-start.25 = (bf16[4,128,384]{2,1,0:T(8,128)(2,1)S(1)}, bf16[4,128,384]{2,1,0:T(8,128)(2,1)S(1)}, u32[]{:S(2)}, u32[]{:S(2)}) collective-permute-start(bf16[4,128,384]{2,1,0:T(8,128)(2,1)S(1)} %get-tuple-element.36), channel_id=1, source_target_pairs={{0,48},{16,32},{32,16},{48,0},{1,49},{17,33},{33,17},{49,1},{2,50}... | collective-permute-start | bytes 1179656 | tf_op jit(solution)/shard_map/ppermute | solution.py:340
  160.9 1.2 collective-permute-start.17
  162.1 4.6 %collective-permute-done.29 = bf16[4,128,384]{2,1,0:T(8,128)(2,1)S(1)} collective-permute-done((bf16[4,128,384]{2,1,0:T(8,128)(2,1)S(1)}, bf16[4,128,384]{2,1,0:T(8,128)(2,1)S(1)}, u32[]{:S(2)}, u32[]{:S(2)}) %collective-permute-start.29) | collective-permute-done | bytes 393248 | tf_op jit(solution)/shard_map/ppermute | solution.py:340
  167.4 1.6 collective-permute-done.25
  170.2 2.2 %collective-permute-start.22 = (bf16[2,128,384]{2,1,0:T(8,128)(2,1)S(1)}, bf16[2,128,384]{2,1,0:T(8,128)(2,1)S(1)}, u32[]{:S(2)}, u32[]{:S(2)}) collective-permute-start(bf16[2,128,384]{2,1,0:T(8,128)(2,1)S(1)} %get-tuple-element.46), channel_id=1, source_target_pairs={{0,48},{16,32},{32,16},{48,0},{1,49},{17,33},{33,17},{49,1},{2,50}... | collective-permute-start | bytes 589832 | tf_op jit(solution)/shard_map/ppermute | solution.py:342
  172.4 1.8 collective-permute-done.17
  176.5 1.2 collective-permute-start.27
  179.0 2.1 %collective-permute-done.18 = bf16[2,128,384]{2,1,0:T(8,128)(2,1)S(1)} collective-permute-done((bf16[2,128,384]{2,1,0:T(8,128)(2,1)S(1)}, bf16[2,128,384]{2,1,0:T(8,128)(2,1)S(1)}, u32[]{:S(2)}, u32[]{:S(2)}) %collective-permute-start.18) | collective-permute-done | bytes 196640 | tf_op jit(solution)/shard_map/ppermute | solution.py:342
  182.5 4.5 %collective-permute-done.19.refs_1_ = bf16[128,384]{1,0:T(8,128)(2,1)S(1)} collective-permute-done((bf16[128,384]{1,0:T(8,128)(2,1)S(1)}, bf16[128,384]{1,0:T(8,128)(2,1)S(1)}, u32[]{:S(2)}, u32[]{:S(2)}) %collective-permute-start.19) | collective-permute-done | bytes 98336 | tf_op jit(solution)/shard_map/ppermute | solution.py:344
  (98 shorter events, 23.3 us)
Async XLA Ops:
  6.5 110.9 %all-gather.3.cloned.1.call-start = ((), (), s32[]{:S(2)}) async-start(), calls=%async_computation | async-start | bytes 20054016 | tf_op jit(solution)/shard_map/all_gather | solution.py:320
  15.9 5.8 %collective-permute-start.12 = (bf16[1,144,384]{2,1,0:T(8,128)(2,1)S(1)}, bf16[1,144,384]{2,1,0:T(8,128)(2,1)S(1)}, u32[]{:S(2)}, u32[]{:S(2)}) collective-permute-start(bf16[1,144,384]{2,1,0:T(8,128)(2,1)S(1)} %get-tuple-element.49), channel_id=1, source_target_pairs={{0,64},{64,0},{128,192},{192,128},{1,65},{65,1},{129,193},{193,129... | collective-permute-start | bytes 331784 | tf_op jit(solution)/shard_map/ppermute | solution.py:306
  16.8 7.1 %collective-permute-start.8 = (bf16[1,144,384]{2,1,0:T(8,128)(2,1)S(1)}, bf16[1,144,384]{2,1,0:T(8,128)(2,1)S(1)}, u32[]{:S(2)}, u32[]{:S(2)}) collective-permute-start(bf16[1,144,384]{2,1,0:T(8,128)(2,1)S(1)} %get-tuple-element.50), channel_id=1, source_target_pairs={{0,192},{64,128},{128,64},{192,0},{1,193},{65,129},{129,65},{193,1... | collective-permute-start | bytes 331784 | tf_op jit(solution)/shard_map/ppermute | solution.py:306
  18.3 5.8 %collective-permute-start.4 = (bf16[1,144,384]{2,1,0:T(8,128)(2,1)S(1)}, bf16[1,144,384]{2,1,0:T(8,128)(2,1)S(1)}, u32[]{:S(2)}, u32[]{:S(2)}) collective-permute-start(bf16[1,144,384]{2,1,0:T(8,128)(2,1)S(1)} %get-tuple-element.51), channel_id=1, source_target_pairs={{0,16},{16,0},{32,48},{48,32},{1,17},{17,1},{33,49},{49,33},{2,18}... | collective-permute-start | bytes 331784 | tf_op jit(solution)/shard_map/ppermute | solution.py:306
  19.5 10.6 %collective-permute-start = (bf16[1,144,384]{2,1,0:T(8,128)(2,1)S(1)}, bf16[1,144,384]{2,1,0:T(8,128)(2,1)S(1)}, u32[]{:S(2)}, u32[]{:S(2)}) collective-permute-start(bf16[1,144,384]{2,1,0:T(8,128)(2,1)S(1)} %get-tuple-element.52), channel_id=1, source_target_pairs={{0,48},{16,32},{32,16},{48,0},{1,49},{17,33},{33,17},{49,1},{2,50}... | collective-permute-start | bytes 331784 | tf_op jit(solution)/shard_map/ppermute | solution.py:306
  21.8 7.3 %collective-permute-start.13 = (bf16[2,144,384]{2,1,0:T(8,128)(2,1)S(1)}, bf16[2,144,384]{2,1,0:T(8,128)(2,1)S(1)}, u32[]{:S(2)}, u32[]{:S(2)}) collective-permute-start(bf16[2,144,384]{2,1,0:T(8,128)(2,1)S(1)} %pad_maximum_fusion.12), channel_id=1, source_target_pairs={{0,192},{64,128},{128,64},{192,0},{1,193},{65,129},{129,65},{193,1... | collective-permute-start | bytes 663560 | tf_op jit(solution)/shard_map/ppermute | solution.py:306
  24.0 7.4 %collective-permute-start.9 = (bf16[2,144,384]{2,1,0:T(8,128)(2,1)S(1)}, bf16[2,144,384]{2,1,0:T(8,128)(2,1)S(1)}, u32[]{:S(2)}, u32[]{:S(2)}) collective-permute-start(bf16[2,144,384]{2,1,0:T(8,128)(2,1)S(1)} %pad_maximum_fusion.11), channel_id=1, source_target_pairs={{0,64},{64,0},{128,192},{192,128},{1,65},{65,1},{129,193},{193,129... | collective-permute-start | bytes 663560 | tf_op jit(solution)/shard_map/ppermute | solution.py:306
  24.1 9.8 %collective-permute-start.5 = (bf16[2,144,384]{2,1,0:T(8,128)(2,1)S(1)}, bf16[2,144,384]{2,1,0:T(8,128)(2,1)S(1)}, u32[]{:S(2)}, u32[]{:S(2)}) collective-permute-start(bf16[2,144,384]{2,1,0:T(8,128)(2,1)S(1)} %pad_maximum_fusion.10), channel_id=1, source_target_pairs={{0,48},{16,32},{32,16},{48,0},{1,49},{17,33},{33,17},{49,1},{2,50}... | collective-permute-start | bytes 663560 | tf_op jit(solution)/shard_map/ppermute | solution.py:306
  29.2 17.0 %collective-permute-start.14 = (bf16[4,144,384]{2,1,0:T(8,128)(2,1)S(1)}, bf16[4,144,384]{2,1,0:T(8,128)(2,1)S(1)}, u32[]{:S(2)}, u32[]{:S(2)}) collective-permute-start(bf16[4,144,384]{2,1,0:T(8,128)(2,1)S(1)} %pad_maximum_fusion.8), channel_id=1, source_target_pairs={{0,16},{16,0},{32,48},{48,32},{1,17},{17,1},{33,49},{49,33},{2,18}... | collective-permute-start | bytes 1327112 | tf_op jit(solution)/shard_map/ppermute | solution.py:306
  30.2 13.7 %collective-permute-start.1 = (bf16[2,144,384]{2,1,0:T(8,128)(2,1)S(1)}, bf16[2,144,384]{2,1,0:T(8,128)(2,1)S(1)}, u32[]{:S(2)}, u32[]{:S(2)}) collective-permute-start(bf16[2,144,384]{2,1,0:T(8,128)(2,1)S(1)} %pad_maximum_fusion.9), channel_id=1, source_target_pairs={{0,16},{16,0},{32,48},{48,32},{1,17},{17,1},{33,49},{49,33},{2,18}... | collective-permute-start | bytes 663560 | tf_op jit(solution)/shard_map/ppermute | solution.py:306
  31.5 15.9 %collective-permute-start.10 = (bf16[4,144,384]{2,1,0:T(8,128)(2,1)S(1)}, bf16[4,144,384]{2,1,0:T(8,128)(2,1)S(1)}, u32[]{:S(2)}, u32[]{:S(2)}) collective-permute-start(bf16[4,144,384]{2,1,0:T(8,128)(2,1)S(1)} %pad_maximum_fusion.7), channel_id=1, source_target_pairs={{0,48},{16,32},{32,16},{48,0},{1,49},{17,33},{33,17},{49,1},{2,50}... | collective-permute-start | bytes 1327112 | tf_op jit(solution)/shard_map/ppermute | solution.py:306
  33.9 13.8 %collective-permute-start.6 = (bf16[4,144,384]{2,1,0:T(8,128)(2,1)S(1)}, bf16[4,144,384]{2,1,0:T(8,128)(2,1)S(1)}, u32[]{:S(2)}, u32[]{:S(2)}) collective-permute-start(bf16[4,144,384]{2,1,0:T(8,128)(2,1)S(1)} %pad_maximum_fusion.6), channel_id=1, source_target_pairs={{0,64},{64,0},{128,192},{192,128},{1,65},{65,1},{129,193},{193,129... | collective-permute-start | bytes 1327112 | tf_op jit(solution)/shard_map/ppermute | solution.py:306
  43.9 14.4 %collective-permute-start.2 = (bf16[4,144,384]{2,1,0:T(8,128)(2,1)S(1)}, bf16[4,144,384]{2,1,0:T(8,128)(2,1)S(1)}, u32[]{:S(2)}, u32[]{:S(2)}) collective-permute-start(bf16[4,144,384]{2,1,0:T(8,128)(2,1)S(1)} %pad_maximum_fusion.5), channel_id=1, source_target_pairs={{0,192},{64,128},{128,64},{192,0},{1,193},{65,129},{129,65},{193,1... | collective-permute-start | bytes 1327112 | tf_op jit(solution)/shard_map/ppermute | solution.py:306
  46.3 19.8 %collective-permute-start.15 = (bf16[8,144,384]{2,1,0:T(8,128)(2,1)S(1)}, bf16[8,144,384]{2,1,0:T(8,128)(2,1)}, u32[]{:S(2)}, u32[]{:S(2)}) collective-permute-start(bf16[8,144,384]{2,1,0:T(8,128)(2,1)S(1)} %pad_maximum_fusion.4.refs_6_), channel_id=1, source_target_pairs={{0,48},{16,32},{32,16},{48,0},{1,49},{17,33},{33,17},{49,1},{2,50}... | collective-permute-start | bytes 2654216 | tf_op jit(solution)/shard_map/ppermute | solution.py:307
  47.5 18.6 %collective-permute-start.11 = (bf16[8,144,384]{2,1,0:T(8,128)(2,1)S(1)}, bf16[8,144,384]{2,1,0:T(8,128)(2,1)}, u32[]{:S(2)}, u32[]{:S(2)}) collective-permute-start(bf16[8,144,384]{2,1,0:T(8,128)(2,1)S(1)} %pad_maximum_fusion.3.refs_4_), channel_id=1, source_target_pairs={{0,16},{16,0},{32,48},{48,32},{1,17},{17,1},{33,49},{49,33},{2,18}... | collective-permute-start | bytes 2654216 | tf_op jit(solution)/shard_map/ppermute | solution.py:307
  47.9 25.4 %collective-permute-start.7 = (bf16[8,144,384]{2,1,0:T(8,128)(2,1)S(1)}, bf16[8,144,384]{2,1,0:T(8,128)(2,1)}, u32[]{:S(2)}, u32[]{:S(2)}) collective-permute-start(bf16[8,144,384]{2,1,0:T(8,128)(2,1)S(1)} %pad_maximum_fusion.2.refs_2_), channel_id=1, source_target_pairs={{0,192},{64,128},{128,64},{192,0},{1,193},{65,129},{129,65},{193,1... | collective-permute-start | bytes 2654216 | tf_op jit(solution)/shard_map/ppermute | solution.py:307
  59.5 13.9 %collective-permute-start.3 = (bf16[8,144,384]{2,1,0:T(8,128)(2,1)}, bf16[8,144,384]{2,1,0:T(8,128)(2,1)}, u32[]{:S(2)}, u32[]{:S(2)}) collective-permute-start(bf16[8,144,384]{2,1,0:T(8,128)(2,1)} %pad_maximum_fusion.1.refs_0_), channel_id=1, source_target_pairs={{0,64},{64,0},{128,192},{192,128},{1,65},{65,1},{129,193},{193,129... | collective-permute-start | bytes 2654216 | tf_op jit(solution)/shard_map/ppermute | solution.py:307
  134.9 21.0 %collective-permute-start.28 = (bf16[8,128,384]{2,1,0:T(8,128)(2,1)S(1)}, bf16[8,128,384]{2,1,0:T(8,128)(2,1)S(1)}, u32[]{:S(2)}, u32[]{:S(2)}) collective-permute-start(bf16[8,128,384]{2,1,0:T(8,128)(2,1)S(1)} %get-tuple-element.27), channel_id=1, source_target_pairs={{0,48},{16,32},{32,16},{48,0},{1,49},{17,33},{33,17},{49,1},{2,50}... | collective-permute-start | bytes 2359304 | tf_op jit(solution)/shard_map/ppermute | solution.py:338
  137.7 19.4 %collective-permute-start.24 = (bf16[8,128,384]{2,1,0:T(8,128)(2,1)S(1)}, bf16[8,128,384]{2,1,0:T(8,128)(2,1)S(1)}, u32[]{:S(2)}, u32[]{:S(2)}) collective-permute-start(bf16[8,128,384]{2,1,0:T(8,128)(2,1)S(1)} %get-tuple-element.26), channel_id=1, source_target_pairs={{0,16},{16,0},{32,48},{48,32},{1,17},{17,1},{33,49},{49,33},{2,18}... | collective-permute-start | bytes 2359304 | tf_op jit(solution)/shard_map/ppermute | solution.py:338
  138.0 21.5 %collective-permute-start.20 = (bf16[8,128,384]{2,1,0:T(8,128)(2,1)S(1)}, bf16[8,128,384]{2,1,0:T(8,128)(2,1)S(1)}, u32[]{:S(2)}, u32[]{:S(2)}) collective-permute-start(bf16[8,128,384]{2,1,0:T(8,128)(2,1)S(1)} %get-tuple-element.25), channel_id=1, source_target_pairs={{0,192},{64,128},{128,64},{192,0},{1,193},{65,129},{129,65},{193,1... | collective-permute-start | bytes 2359304 | tf_op jit(solution)/shard_map/ppermute | solution.py:338
  138.5 22.2 %collective-permute-start.16 = (bf16[8,128,384]{2,1,0:T(8,128)(2,1)S(1)}, bf16[8,128,384]{2,1,0:T(8,128)(2,1)S(1)}, u32[]{:S(2)}, u32[]{:S(2)}) collective-permute-start(bf16[8,128,384]{2,1,0:T(8,128)(2,1)S(1)} %get-tuple-element.24), channel_id=1, source_target_pairs={{0,64},{64,0},{128,192},{192,128},{1,65},{65,1},{129,193},{193,129... | collective-permute-start | bytes 2359304 | tf_op jit(solution)/shard_map/ppermute | solution.py:338
  156.1 10.6 %collective-permute-start.29 = (bf16[4,128,384]{2,1,0:T(8,128)(2,1)S(1)}, bf16[4,128,384]{2,1,0:T(8,128)(2,1)S(1)}, u32[]{:S(2)}, u32[]{:S(2)}) collective-permute-start(bf16[4,128,384]{2,1,0:T(8,128)(2,1)S(1)} %get-tuple-element.34), channel_id=1, source_target_pairs={{0,16},{16,0},{32,48},{48,32},{1,17},{17,1},{33,49},{49,33},{2,18}... | collective-permute-start | bytes 1179656 | tf_op jit(solution)/shard_map/ppermute | solution.py:340
  157.4 11.7 %collective-permute-start.25 = (bf16[4,128,384]{2,1,0:T(8,128)(2,1)S(1)}, bf16[4,128,384]{2,1,0:T(8,128)(2,1)S(1)}, u32[]{:S(2)}, u32[]{:S(2)}) collective-permute-start(bf16[4,128,384]{2,1,0:T(8,128)(2,1)S(1)} %get-tuple-element.36), channel_id=1, source_target_pairs={{0,48},{16,32},{32,16},{48,0},{1,49},{17,33},{33,17},{49,1},{2,50}... | collective-permute-start | bytes 1179656 | tf_op jit(solution)/shard_map/ppermute | solution.py:340
  159.7 10.4 %collective-permute-start.21 = (bf16[4,128,384]{2,1,0:T(8,128)(2,1)S(1)}, bf16[4,128,384]{2,1,0:T(8,128)(2,1)S(1)}, u32[]{:S(2)}, u32[]{:S(2)}) collective-permute-start(bf16[4,128,384]{2,1,0:T(8,128)(2,1)S(1)} %get-tuple-element.38), channel_id=1, source_target_pairs={{0,64},{64,0},{128,192},{192,128},{1,65},{65,1},{129,193},{193,129... | collective-permute-start | bytes 1179656 | tf_op jit(solution)/shard_map/ppermute | solution.py:340
  160.9 13.3 %collective-permute-start.17 = (bf16[4,128,384]{2,1,0:T(8,128)(2,1)S(1)}, bf16[4,128,384]{2,1,0:T(8,128)(2,1)S(1)}, u32[]{:S(2)}, u32[]{:S(2)}) collective-permute-start(bf16[4,128,384]{2,1,0:T(8,128)(2,1)S(1)} %get-tuple-element.40), channel_id=1, source_target_pairs={{0,192},{64,128},{128,64},{192,0},{1,193},{65,129},{129,65},{193,1... | collective-permute-start | bytes 1179656 | tf_op jit(solution)/shard_map/ppermute | solution.py:340
  166.8 9.5 %collective-permute-start.30 = (bf16[2,128,384]{2,1,0:T(8,128)(2,1)S(1)}, bf16[2,128,384]{2,1,0:T(8,128)(2,1)S(1)}, u32[]{:S(2)}, u32[]{:S(2)}) collective-permute-start(bf16[2,128,384]{2,1,0:T(8,128)(2,1)S(1)} %get-tuple-element.42), channel_id=1, source_target_pairs={{0,192},{64,128},{128,64},{192,0},{1,193},{65,129},{129,65},{193,1... | collective-permute-start | bytes 589832 | tf_op jit(solution)/shard_map/ppermute | solution.py:342
  169.1 7.3 %collective-permute-start.26 = (bf16[2,128,384]{2,1,0:T(8,128)(2,1)S(1)}, bf16[2,128,384]{2,1,0:T(8,128)(2,1)S(1)}, u32[]{:S(2)}, u32[]{:S(2)}) collective-permute-start(bf16[2,128,384]{2,1,0:T(8,128)(2,1)S(1)} %get-tuple-element.44), channel_id=1, source_target_pairs={{0,64},{64,0},{128,192},{192,128},{1,65},{65,1},{129,193},{193,129... | collective-permute-start | bytes 589832 | tf_op jit(solution)/shard_map/ppermute | solution.py:342
  170.2 7.6 %collective-permute-start.22 = (bf16[2,128,384]{2,1,0:T(8,128)(2,1)S(1)}, bf16[2,128,384]{2,1,0:T(8,128)(2,1)S(1)}, u32[]{:S(2)}, u32[]{:S(2)}) collective-permute-start(bf16[2,128,384]{2,1,0:T(8,128)(2,1)S(1)} %get-tuple-element.46), channel_id=1, source_target_pairs={{0,48},{16,32},{32,16},{48,0},{1,49},{17,33},{33,17},{49,1},{2,50}... | collective-permute-start | bytes 589832 | tf_op jit(solution)/shard_map/ppermute | solution.py:342
  174.3 6.8 %collective-permute-start.18 = (bf16[2,128,384]{2,1,0:T(8,128)(2,1)S(1)}, bf16[2,128,384]{2,1,0:T(8,128)(2,1)S(1)}, u32[]{:S(2)}, u32[]{:S(2)}) collective-permute-start(bf16[2,128,384]{2,1,0:T(8,128)(2,1)S(1)} %get-tuple-element.48), channel_id=1, source_target_pairs={{0,16},{16,0},{32,48},{48,32},{1,17},{17,1},{33,49},{49,33},{2,18}... | collective-permute-start | bytes 589832 | tf_op jit(solution)/shard_map/ppermute | solution.py:342
  176.3 4.9 %collective-permute-start.31 = (bf16[128,384]{1,0:T(8,128)(2,1)S(1)}, bf16[128,384]{1,0:T(8,128)(2,1)S(1)}, u32[]{:S(2)}, u32[]{:S(2)}) collective-permute-start(bf16[128,384]{1,0:T(8,128)(2,1)S(1)} %get-tuple-element.53), channel_id=1, source_target_pairs={{0,64},{64,0},{128,192},{192,128},{1,65},{65,1},{129,193},{193,129... | collective-permute-start | bytes 294920 | tf_op jit(solution)/shard_map/ppermute | solution.py:344
  176.5 5.9 %collective-permute-start.27 = (bf16[128,384]{1,0:T(8,128)(2,1)S(1)}, bf16[128,384]{1,0:T(8,128)(2,1)S(1)}, u32[]{:S(2)}, u32[]{:S(2)}) collective-permute-start(bf16[128,384]{1,0:T(8,128)(2,1)S(1)} %get-tuple-element.55), channel_id=1, source_target_pairs={{0,192},{64,128},{128,64},{192,0},{1,193},{65,129},{129,65},{193,1... | collective-permute-start | bytes 294920 | tf_op jit(solution)/shard_map/ppermute | solution.py:344
  181.1 5.9 %collective-permute-start.19 = (bf16[128,384]{1,0:T(8,128)(2,1)S(1)}, bf16[128,384]{1,0:T(8,128)(2,1)S(1)}, u32[]{:S(2)}, u32[]{:S(2)}) collective-permute-start(bf16[128,384]{1,0:T(8,128)(2,1)S(1)} %get-tuple-element.59), channel_id=1, source_target_pairs={{0,48},{16,32},{32,16},{48,0},{1,49},{17,33},{33,17},{49,1},{2,50}... | collective-permute-start | bytes 294920 | tf_op jit(solution)/shard_map/ppermute | solution.py:344
  (15 other events, 73.0 us)
Sparse Core Ops, SparseCore 0:
  9.2 108.1 all-gather.2

commit v3 on v1

v3 whole, which is shorter than its diff:
```python
import functools

import jax
import jax.numpy as jnp
from jax import lax
from jax.experimental import pallas as pl
from jax.experimental.pallas import tpu as pltpu
from jax.sharding import Mesh
from jax.sharding import PartitionSpec as P

EPS = 1e-05
D = 1536
FF = 512
TOP = 8
SLOTS = 64
ROWS = 128
CAP = 32
BLOCKS = 16
LOCAL = 4
CHUNK = D // 8
GROUPS = 2
GROUP = D // GROUPS
F32 = jnp.float32
BF16 = jnp.bfloat16
MIB = 1024 * 1024


def params(mib, *semantics):
    return pltpu.CompilerParams(
        dimension_semantics=semantics or None, vmem_limit_bytes=mib * MIB
    )


PLANS = ((1, 3), (3, 1))


def block_at(plan, place, j):
    first, other = plan
    x, y, core = place
    bit = lambda n: (j >> n) & 1
    low = bit(0) * other ^ bit(1) * first
    high = bit(2) * other ^ bit(3) * first
    along_x = jnp.where(core == 0, high, low)
    along_y = jnp.where(core == 0, low, high)
    return 4 * (x ^ along_x) + (y ^ along_y)


def place_of(place_ref):
    return place_ref[0], place_ref[1], place_ref[2]


def turned(rows, turn, large):
    pairs = []
    for x in range(4):
        for y in range(4):
            for core in range(2):
                along_x = large == (core == 0)
                to = (x ^ turn, y) if along_x else (x, y ^ turn)
                pairs.append((8 * x + 2 * y + core, 8 * to[0] + 2 * to[1] + core))
    return lax.ppermute(rows, ("x", "y", "core"), pairs)


def each(count, unroll, step):
    def run(i, carry):
        step(i)
        return carry

    lax.fori_loop(0, count, run, 0, unroll=unroll)


def entry_kernel(
    attn_ref, resid_ref, wo_ref, gain_ref, router_ref, route_ref, expert_ref, keep_ref,
    hidden_ref, rows_ref,
):
    step = pl.program_id(0)
    width = wo_ref.shape[1]
    cols = pl.ds(step * width, width)
    hidden_ref[:, cols] = resid_ref[...].astype(F32) + jnp.dot(
        attn_ref[...], wo_ref[...], preferred_element_type=F32
    )

    @pl.when(step == pl.num_programs(0) - 1)
    def _():
        values = hidden_ref[...]
        mean_sq = jnp.mean(values * values, axis=-1, keepdims=True)
        normed = (values * lax.rsqrt(mean_sq + EPS) * gain_ref[...]).astype(BF16)
        logits = lax.dot_general(
            router_ref[...], normed.astype(F32), (((1,), (1,)), ((), ())),
            precision=lax.Precision.HIGHEST, preferred_element_type=F32,
        )
        experts = logits.shape[0]
        pick = lax.broadcasted_iota(jnp.int32, (experts, SLOTS), 0) == expert_ref[...]
        by_slot = lax.dot_general(
            pick.astype(F32), logits, (((0,), (0,)), ((), ())),
            precision=lax.Precision.HIGHEST, preferred_element_type=F32,
        )
        slot = lax.broadcasted_iota(jnp.int32, (SLOTS, ROWS), 0)
        named = slot == route_ref[0:1]
        for k in range(1, TOP):
            named = named | (slot == route_ref[k : k + 1])
        top = jnp.max(jnp.where(named, by_slot, -jnp.inf), axis=0, keepdims=True)
        grown = jnp.where(named, jnp.exp(jnp.where(named, by_slot - top, 0.0)), 0.0)
        probs = grown / jnp.sum(grown, axis=0, keepdims=True)
        live = jnp.where(keep_ref[...] > 0, probs, 0.0).reshape(BLOCKS, LOCAL, ROWS)
        for group in range(GROUPS):
            rows_ref[group, :ROWS] = normed[:, group * GROUP : (group + 1) * GROUP]
        for s in range(LOCAL):
            rest = live[:, s]
            for n in range(3):
                part = rest.astype(BF16)
                at = (s % 2 * 3 + n) * ROWS
                rows_ref[s // 2, ROWS:, at : at + ROWS] = part
                rest = rest - part.astype(F32)


def entry(attn_out, resid, w_o, gain, router_w, route_slot, slot_expert, keep):
    steps = 6
    width = D // steps
    whole = lambda shape: pl.BlockSpec(shape, lambda i: (0,) * len(shape))
    return pl.pallas_call(
        entry_kernel,
        grid=(steps,),
        in_specs=[
            whole((ROWS, D)),
            pl.BlockSpec((ROWS, width), lambda i: (0, i)),
            pl.BlockSpec((D, width), lambda i: (0, i)),
            whole(gain.shape),
            whole(router_w.shape),
            whole(route_slot.shape),
            whole(slot_expert.shape),
            whole(keep.shape),
        ],
        out_specs=[whole((ROWS, D)), whole((GROUPS, ROWS + BLOCKS, GROUP))],
        out_shape=[
            jax.ShapeDtypeStruct((ROWS, D), F32),
            jax.ShapeDtypeStruct((GROUPS, ROWS + BLOCKS, GROUP), BF16),
        ],
        compiler_params=params(16, "arbitrary"),
        name="entry",
    )(attn_out, resid, w_o, gain, router_w, route_slot, slot_expert, keep)


def compact_kernel(place_ref, *refs):
    row_refs = refs[: 2 * GROUPS]
    packed_ref, spread_ref, scale_ref, pick_ref, weight_ref = refs[2 * GROUPS :]
    place_here = place_of(place_ref)
    half = BLOCKS // 2
    earlier = (
        lax.broadcasted_iota(jnp.int32, (ROWS, ROWS), 0)
        < lax.broadcasted_iota(jnp.int32, (ROWS, ROWS), 1)
    ).astype(BF16)
    rank = lax.broadcasted_iota(jnp.int32, (CAP, ROWS), 0).astype(F32)
    mine = lax.broadcasted_iota(jnp.int32, (BLOCKS, GROUP), 0) == 4 * place_here[0] + place_here[1]

    def fetch(ref, group, start, i):
        b = block_at(PLANS[group], place_here, start + i)
        parts = jnp.where(mine, ref[i, ROWS:].astype(F32), 0.0)
        parts = jnp.sum(parts, axis=0, keepdims=True)
        parts = [parts[:, n * ROWS : (n + 1) * ROWS] for n in range(6)]
        for n in range(2):
            s = 2 * group + n
            weight_ref[b, s : s + 1] = parts[3 * n] + parts[3 * n + 1] + parts[3 * n + 2]

    def choose(b):
        weight = weight_ref[b]
        hit = weight > 0.0
        place = jnp.dot(hit.astype(BF16), earlier, preferred_element_type=F32)
        place = jnp.where(hit, place, -1.0)
        picks = [rank == place[s : s + 1] for s in range(LOCAL)]
        for s in range(LOCAL):
            scale_ref[s, b] = jnp.sum(
                jnp.where(picks[s], weight[s : s + 1], 0.0), axis=1, keepdims=True
            )
        pick = jnp.concatenate([p.astype(F32) for p in picks], axis=0)
        spread_ref[b] = jnp.transpose(pick).astype(BF16)
        pick_ref[b] = pick.astype(BF16)

    def pack(ref, group, start, i):
        b = block_at(PLANS[group], place_here, start + i)
        packed = jnp.dot(pick_ref[b], ref[i, :ROWS], preferred_element_type=F32).astype(BF16)
        packed_ref[:, b, :, group * GROUP : (group + 1) * GROUP] = packed.reshape(
            LOCAL, CAP, GROUP
        )

    for n, ref in enumerate(row_refs):
        each(half, 2, functools.partial(fetch, ref, n // 2, n % 2 * half))
    each(BLOCKS, 2, choose)
    for n, ref in enumerate(row_refs):
        each(half, 2, functools.partial(pack, ref, n // 2, n % 2 * half))


def compact(place, rows):
    vmem = pl.BlockSpec(memory_space=pltpu.VMEM)
    return pl.pallas_call(
        compact_kernel,
        in_specs=[pl.BlockSpec(memory_space=pltpu.SMEM)] + [vmem] * len(rows),
        out_specs=[vmem] * 3,
        out_shape=[
            jax.ShapeDtypeStruct((LOCAL, BLOCKS, CAP, D), BF16),
            jax.ShapeDtypeStruct((BLOCKS, ROWS, LOCAL * CAP), BF16),
            jax.ShapeDtypeStruct((LOCAL, BLOCKS, CAP, 1), F32),
        ],
        scratch_shapes=[
            pltpu.VMEM((BLOCKS, LOCAL * CAP, ROWS), BF16),
            pltpu.VMEM((BLOCKS, LOCAL, ROWS), F32),
        ],
        compiler_params=params(24),
        name="compact",
    )(place, *rows)


def back_to_rows(plan, place, start, group, act_ref, down_ref, spread_ref, part_ref, out_ref):
    half = BLOCKS // 2
    order = [block_at(plan, place, start + i) for i in range(half)]
    for s in range(LOCAL):
        rows = jnp.concatenate([act_ref[s, b] for b in order])
        down = down_ref[group, s // 2, :, s % 2].reshape(GROUP, FF)
        part = lax.dot_general(
            rows, down, (((1,), (1,)), ((), ())), preferred_element_type=F32
        )
        part_ref[:, s] = part.astype(BF16).reshape(half, CAP, GROUP)

    def back(i):
        b = block_at(plan, place, start + i)
        rows = part_ref[i].reshape(LOCAL * CAP, GROUP)
        out_ref[i] = jnp.dot(spread_ref[b], rows, preferred_element_type=F32).astype(BF16)

    each(half, 4, back)


def experts_kernel(place_ref, packed_hbm, scale_hbm, spread_hbm, weights_hbm, *refs):
    out_refs, act_ref = refs[:GROUPS], refs[GROUPS]
    packed_ref, scale_ref, gate_ref, up_ref, down_ref, spread_ref, part_ref = refs[GROUPS + 1 : -3]
    slot_sems, down_sems, once_sems = refs[-3:]
    blks = 8 // GROUPS
    fetch = pltpu.make_async_copy
    by_slot = [
        [
            fetch(packed_hbm.at[s], packed_ref.at[s], slot_sems.at[s, 0]),
            fetch(weights_hbm.at[s // 2, :, 0, s % 2], gate_ref.at[s], slot_sems.at[s, 1]),
            fetch(weights_hbm.at[s // 2, :, 1, s % 2], up_ref.at[s], slot_sems.at[s, 2]),
        ]
        for s in range(LOCAL)
    ]
    by_group = [
        fetch(weights_hbm.at[:, blks * g : blks * (g + 1), 2], down_ref.at[g], down_sems.at[g])
        for g in range(GROUPS)
    ]
    scales = fetch(scale_hbm, scale_ref, once_sems.at[0])
    spreads = fetch(spread_hbm, spread_ref, once_sems.at[1])
    for copy in (*by_slot[0], scales, *by_slot[1], *by_slot[2], *by_slot[3], *by_group, spreads):
        copy.start()
    for s in range(LOCAL):
        by_slot[s][0].wait()
        by_slot[s][1].wait()
        rows = packed_ref[s].reshape(BLOCKS * CAP, D)
        gate = jnp.dot(rows, gate_ref[s].reshape(D, FF), preferred_element_type=F32)
        by_slot[s][2].wait()
        up = jnp.dot(rows, up_ref[s].reshape(D, FF), preferred_element_type=F32)
        if s == 0:
            scales.wait()
        scale = scale_ref[s].reshape(BLOCKS * CAP, 1)
        act = (gate / (1.0 + jnp.exp(-gate)) * up * scale).astype(BF16)
        act_ref[s] = act.reshape(BLOCKS, CAP, FF)
    spreads.wait()
    for g, plan in enumerate(PLANS):
        by_group[g].wait()
        back_to_rows(
            plan, place_of(place_ref), BLOCKS // 2, g, act_ref, down_ref, spread_ref, part_ref, out_refs[g]
        )


def experts(place, packed, scale, spread, weights):
    half = BLOCKS // 2
    vmem, hbm = pl.BlockSpec(memory_space=pltpu.VMEM), pl.BlockSpec(memory_space=pltpu.HBM)
    return pl.pallas_call(
        experts_kernel,
        in_specs=[pl.BlockSpec(memory_space=pltpu.SMEM), hbm, hbm, hbm, hbm],
        out_specs=[vmem] * (GROUPS + 1),
        out_shape=[jax.ShapeDtypeStruct((half, ROWS, GROUP), BF16)] * GROUPS
        + [jax.ShapeDtypeStruct((LOCAL, BLOCKS, CAP, FF), BF16)],
        scratch_shapes=[
            pltpu.VMEM(packed.shape, BF16),
            pltpu.VMEM(scale.shape, F32),
            pltpu.VMEM((LOCAL, 8, CHUNK, FF), BF16),
            pltpu.VMEM((LOCAL, 8, CHUNK, FF), BF16),
            pltpu.VMEM((GROUPS, 2, 8 // GROUPS, 2, CHUNK, FF), BF16),
            pltpu.VMEM(spread.shape, BF16),
            pltpu.VMEM((half, LOCAL, CAP, GROUP), BF16),
            pltpu.SemaphoreType.DMA((LOCAL, 3)),
            pltpu.SemaphoreType.DMA((GROUPS,)),
            pltpu.SemaphoreType.DMA((2,)),
        ],
        compiler_params=params(48),
        name="experts",
    )(place, packed, scale, spread, weights)


def kept_kernel(place_ref, act_ref, spread_hbm, weights_hbm, *refs):
    out_refs, (down_ref, spread_ref, part_ref, sems) = refs[:GROUPS], refs[GROUPS:]
    blks = 8 // GROUPS
    copies = [
        pltpu.make_async_copy(
            weights_hbm.at[:, blks * g : blks * (g + 1), 2], down_ref.at[g], sems.at[g]
        )
        for g in range(GROUPS)
    ]
    spreads = pltpu.make_async_copy(spread_hbm, spread_ref, sems.at[GROUPS])
    for copy in (copies[0], spreads, *copies[1:]):
        copy.start()
    spreads.wait()
    for g, plan in enumerate(PLANS):
        copies[g].wait()
        back_to_rows(
            plan, place_of(place_ref), 0, g, act_ref, down_ref, spread_ref, part_ref, out_refs[g]
        )


def kept(place, act, spread, weights):
    half = BLOCKS // 2
    vmem, hbm = pl.BlockSpec(memory_space=pltpu.VMEM), pl.BlockSpec(memory_space=pltpu.HBM)
    return pl.pallas_call(
        kept_kernel,
        in_specs=[pl.BlockSpec(memory_space=pltpu.SMEM), vmem, hbm, hbm],
        out_specs=[vmem] * GROUPS,
        out_shape=[jax.ShapeDtypeStruct((half, ROWS, GROUP), BF16)] * GROUPS,
        scratch_shapes=[
            pltpu.VMEM((GROUPS, 2, 8 // GROUPS, 2, CHUNK, FF), BF16),
            pltpu.VMEM(spread.shape, BF16),
            pltpu.VMEM((half, LOCAL, CAP, GROUP), BF16),
            pltpu.SemaphoreType.DMA((GROUPS + 1,)),
        ],
        compiler_params=params(24),
        name="kept",
    )(place, act, spread, weights)


def closing_kernel(hidden_ref, gain_ref, *refs):
    pairs, out_ref = refs[:-1], refs[-1]
    moe = jnp.concatenate(
        [
            pairs[2 * g][...].astype(F32) + pairs[2 * g + 1][...].astype(F32)
            for g in range(GROUPS)
        ],
        axis=1,
    )
    mixed = hidden_ref[...] + moe
    mean_sq = jnp.mean(mixed * mixed, axis=-1, keepdims=True)
    out_ref[...] = (mixed * lax.rsqrt(mean_sq + EPS) * gain_ref[...]).astype(BF16)


def closing(hidden, gain, pairs):
    return pl.pallas_call(
        closing_kernel,
        out_shape=jax.ShapeDtypeStruct((ROWS, D), BF16),
        compiler_params=params(8),
        name="closing",
    )(hidden, gain, *pairs)


def spread_out(rows):
    halves = []
    for group, (first, other) in enumerate(PLANS):
        held = rows[group][None]
        for turn, large in ((other, False), (first, False), (other, True)):
            held = jnp.concatenate([held, turned(held, turn, large)])
        halves += [held, turned(held, first, True)]
    return halves


def add(a, b):
    return (a.astype(F32) + b.astype(F32)).astype(BF16)


def body(
    attn_out, resid, w_o, norm1_gain, router_w, route_slot, slot_expert, keep,
    w_gate, w_up, w_down, norm2_gain,
):
    joined = jnp.stack([w_gate, w_up, w_down])
    weights = lax.all_gather(joined, ("core", "blk"), axis=0, tiled=False)
    weights = weights.reshape(2, 8, 3, 2, CHUNK, FF)
    weights = pltpu.with_memory_space_constraint(weights, pltpu.HBM)

    hidden, outgoing = entry(
        attn_out, resid, w_o, norm1_gain.reshape(1, D), router_w.T, route_slot.T,
        slot_expert.reshape(1, SLOTS), keep.reshape(1, ROWS),
    )
    place = jnp.stack([lax.axis_index(name) for name in ("x", "y", "core")])
    place = place.astype(jnp.int32)
    packed, spread, scale = [
        pltpu.with_memory_space_constraint(array, pltpu.HBM)
        for array in compact(place, spread_out(outgoing))
    ]
    *sends, act = experts(place, packed, scale, spread, weights)
    keeps = kept(place, act, spread, weights)
    pairs = []
    for send, keep, (first, other) in zip(sends, keeps, PLANS):
        got = turned(send, first, True)
        send, keep = add(keep[4:], got[4:]), add(keep[:4], got[:4])
        got = turned(send, other, True)
        send, keep = add(keep[2:], got[2:]), add(keep[:2], got[:2])
        got = turned(send, first, False)
        send, keep = add(keep[1], got[1]), add(keep[0], got[0])
        pairs += [keep, turned(send, other, False)]
    return closing(hidden, norm2_gain.reshape(1, D), pairs)


def solution(mesh):
    fine = Mesh(mesh.devices.reshape(4, 4, 2, 8), ("x", "y", "core", "blk"))
    rows = P(("x", "y", "core", "blk"), None)
    slots = P(("x", "y", "core"), "blk", None)
    placed = (
        rows, rows, P(), P(), P(), rows, P(), P(("x", "y", "core", "blk")),
        slots, slots, slots, P(),
    )
    return jax.shard_map(body, mesh=fine, in_specs=placed, out_specs=rows, check_vma=False)
```

time: 213 us -> 195 us (0.915)
  waiting for transfers between devices: 89.1 us -> 113 us
  starting transfers between devices: 42.5 us -> 20.4 us
  Pallas kernels: 54.1 us -> 36.3 us
    ppermute x32 -> x16, starting transfers between devices: 42.5 us -> 20.4 us  [turned(): return lax.ppermute(rows, ('x', 'y', 'core'), pairs)]
    ppermute x32 -> x16, waiting for transfers between devices: 60.4 us -> 79.8 us  [turned(): return lax.ppermute(rows, ('x', 'y', 'core'), pairs)]
    pallas_call x9 -> x2, Pallas kernels: 38.2 us -> 23.1 us  [the longest x1 17 us: experts(): pl.pallas_call(experts_kernel, in_specs=[pl.BlockSpec(memory_space=pltpu....]
    all_gather x1, waiting for transfers between devices: 28.7 us -> 33.4 us  [body(): weights = lax.all_gather(joined, ('core', 'blk'), axis=0, tiled=False)]
    pallas_call x1, Pallas kernels: 11.5 us -> 8.78 us  [compact(): pl.pallas_call(compact_kernel, in_specs=[pl.BlockSpec(memory_space=pltpu....]
  transfers between devices with their start and end apart: 33 -> 17, of which waited for: 14 -> 14; matrix products, arithmetic and copies ran while one was open for 2% -> 1% of each run, Pallas kernels for 18% -> 9%
where the time goes in v3:
time: 195 us
  waiting for transfers between devices  113 us (58%)
  Pallas kernels  36.3 us (19%)
  starting transfers between devices  20.4 us (10%)
  between operations  13.7 us (7%)
  local copies, waits for them, and re-layouts  6.82 us (3%)
  other arithmetic  4.59 us (2%)
    ppermute x16, waiting for transfers between devices, turned(): return lax.ppermute(rows, ('x', 'y', 'core'), pairs)  79.8 us
    all_gather x1, waiting for transfers between devices, body(): weights = lax.all_gather(joined, ('core', 'blk'), axis=0, tiled=False)  33.4 us
    ppermute x16, starting transfers between devices, turned(): return lax.ppermute(rows, ('x', 'y', 'core'), pairs)  20.4 us
    pallas_call x1, Pallas kernels, experts(): pl.pallas_call(experts_kernel, in_specs=[pl.BlockSpec(memory_space=pltpu....  17 us
    pallas_call x1, Pallas kernels, compact(): pl.pallas_call(compact_kernel, in_specs=[pl.BlockSpec(memory_space=pltpu....  8.78 us
    unnamed x28, local copies, waits for them, and re-layouts  6.78 us
    pallas_call x1, Pallas kernels, kept(): pl.pallas_call(kept_kernel, in_specs=[pl.BlockSpec(memory_space=pltpu.SME...  6.13 us
  transfers between devices with their start and end apart: 17, of which 14 were waited for; matrix products, arithmetic and copies ran while one was open for 1% of the time, Pallas kernels for 9%

profile of v3, /device:TPU:6, one launch (start us, length us, event | category | flops | bytes accessed | tf_op | source)
XLA Modules:
  0.0 194.9 jit_solution(15384958879125330313)
XLA Ops:
  6.6 2.5 %pad_maximum_fusion.2 = bf16[3,2,192,512]{3,2,1,0:T(8,128)(2,1)} fusion(bf16[1,2,192,512]{3,2,1,0:T(8,128)(2,1)} %bitcast.25, bf16[1,2,192,512]{3,2,1,0:T(8,128)(2,1)} %bitcast.26, bf16[1,2,192,512]{3,2,1,0:T(8,128)(2,1)} %bitcast.27), kind=kLoop, calls=%fused_computation.6 | loop fusion | flops 1179648 | bytes 2359296 | tf_op jit(solution)/shard_map/stack | solution.py:379
  9.2 2.3 %copy-done.1 = bf16[1536,1536]{1,0:T(8,128)(2,1)S(1)} copy-done((bf16[1536,1536]{1,0:T(8,128)(2,1)S(1)}, bf16[1536,1536]{1,0:T(8,128)(2,1)}, u32[]{:S(2)}) %copy-start.1) | copy-done | bytes 4718616
  11.5 3.4 %entry.1 = (f32[128,1536]{1,0:T(8,128)S(1)}, bf16[2,144,768]{2,1,0:T(8,128)(2,1)S(1)}) custom-call(bf16[128,1536]{1,0:T(8,128)(2,1)S(1)} %copy-done.6, bf16[128,1536]{1,0:T(8,128)(2,1)S(1)} %copy-done.7, bf16[1536,1536]{1,0:T(8,128)(2,1)S(1)} %copy-done.1, f32[1,1536]{1,0:T(1,128)S(1)} %reshape.31.gain_ref, f32[40,1536]{1,0:T(8,128)S(1)} %bitcast.19, ...), custom_call_target="tpu_custom_call" | custom-call | tf_op jit(solution)/shard_map/entry/pallas_call | solution.py:120
  15.0 1.7 collective-permute-start.4
  16.6 2.2 %collective-permute-start = (bf16[1,144,768]{2,1,0:T(8,128)(2,1)S(1)}, bf16[1,144,768]{2,1,0:T(8,128)(2,1)S(1)}, u32[]{:S(2)}, u32[]{:S(2)}) collective-permute-start(bf16[1,144,768]{2,1,0:T(8,128)(2,1)S(1)} %get-tuple-element.38), channel_id=1, source_target_pairs={{0,48},{8,200},{16,32},{24,216},{32,16},{40,232},{48,0},{56,248},{... | collective-permute-start | bytes 663560 | tf_op jit(solution)/shard_map/ppermute | solution.py:60
  18.8 2.2 %collective-permute-done.4 = bf16[1,144,768]{2,1,0:T(8,128)(2,1)S(1)} collective-permute-done((bf16[1,144,768]{2,1,0:T(8,128)(2,1)S(1)}, bf16[1,144,768]{2,1,0:T(8,128)(2,1)S(1)}, u32[]{:S(2)}, u32[]{:S(2)}) %collective-permute-start.4) | collective-permute-done | bytes 221216 | tf_op jit(solution)/shard_map/ppermute | solution.py:60
  21.0 3.1 %collective-permute-start.5 = (bf16[2,144,768]{2,1,0:T(8,128)(2,1)S(1)}, bf16[2,144,768]{2,1,0:T(8,128)(2,1)S(1)}, u32[]{:S(2)}, u32[]{:S(2)}) collective-permute-start(bf16[2,144,768]{2,1,0:T(8,128)(2,1)S(1)} %pad_maximum_fusion.6), channel_id=1, source_target_pairs={{0,48},{8,200},{16,32},{24,216},{32,16},{40,232},{48,0},{56,248},{... | collective-permute-start | bytes 1327112 | tf_op jit(solution)/shard_map/ppermute | solution.py:60
  24.4 6.2 %collective-permute-done.5 = bf16[2,144,768]{2,1,0:T(8,128)(2,1)S(1)} collective-permute-done((bf16[2,144,768]{2,1,0:T(8,128)(2,1)S(1)}, bf16[2,144,768]{2,1,0:T(8,128)(2,1)S(1)}, u32[]{:S(2)}, u32[]{:S(2)}) %collective-permute-start.5) | collective-permute-done | bytes 442400 | tf_op jit(solution)/shard_map/ppermute | solution.py:60
  30.7 0.9 collective-permute-start.6
  31.6 1.8 collective-permute-done.1
  34.2 9.6 %collective-permute-done.6 = bf16[4,144,768]{2,1,0:T(8,128)(2,1)S(1)} collective-permute-done((bf16[4,144,768]{2,1,0:T(8,128)(2,1)S(1)}, bf16[4,144,768]{2,1,0:T(8,128)(2,1)S(1)}, u32[]{:S(2)}, u32[]{:S(2)}) %collective-permute-start.6) | collective-permute-done | bytes 884768 | tf_op jit(solution)/shard_map/ppermute | solution.py:60
  44.0 2.3 %collective-permute-start.7 = (bf16[8,144,768]{2,1,0:T(8,128)(2,1)S(1)}, bf16[8,144,768]{2,1,0:T(8,128)(2,1)}, u32[]{:S(2)}, u32[]{:S(2)}) collective-permute-start(bf16[8,144,768]{2,1,0:T(8,128)(2,1)S(1)} %pad_maximum_fusion.1.refs_2_), channel_id=1, source_target_pairs={{0,192},{8,56},{16,208},{24,40},{32,224},{40,24},{48,240},{56,8},{... | collective-permute-start | bytes 5308424 | tf_op jit(solution)/shard_map/ppermute | solution.py:60
  46.3 1.5 collective-permute-done.2
  48.0 1.1 collective-permute-start.3
  49.2 18.8 %collective-permute-done.7.refs_3_ = bf16[8,144,768]{2,1,0:T(8,128)(2,1)} collective-permute-done((bf16[8,144,768]{2,1,0:T(8,128)(2,1)S(1)}, bf16[8,144,768]{2,1,0:T(8,128)(2,1)}, u32[]{:S(2)}, u32[]{:S(2)}) %collective-permute-start.7) | collective-permute-done | bytes 1769504 | tf_op jit(solution)/shard_map/ppermute | solution.py:60
  68.0 3.0 %collective-permute-done.3.refs_1_ = bf16[8,144,768]{2,1,0:T(8,128)(2,1)} collective-permute-done((bf16[8,144,768]{2,1,0:T(8,128)(2,1)S(1)}, bf16[8,144,768]{2,1,0:T(8,128)(2,1)}, u32[]{:S(2)}, u32[]{:S(2)}) %collective-permute-start.3) | collective-permute-done | bytes 1769504 | tf_op jit(solution)/shard_map/ppermute | solution.py:60
  70.9 8.8 %compact.1 = (bf16[4,16,32,1536]{3,2,1,0:T(8,128)(2,1)S(1)}, bf16[16,128,128]{2,1,0:T(8,128)(2,1)S(1)}, f32[4,16,32,1]{3,2,1,0:T(8,128)S(1)}) custom-call(s32[3]{0:T(128)S(1)} %pad_add_fusion.place_ref, bf16[8,144,768]{2,1,0:T(8,128)(2,1)S(1)} %pad_maximum_fusion.refs_0_, bf16[8,144,768]{2,1,0:T(8,128)(2,1)} %collective-permute-done.3.refs_1_, ...), custom_call_target="tpu_custom_call" | custom-call | tf_op jit(solution)/shard_map/compact/pallas_call | solution.py:194
  79.7 2.6 %copy-done = bf16[4,16,32,1536]{3,2,1,0:T(8,128)(2,1)} copy-done((bf16[4,16,32,1536]{3,2,1,0:T(8,128)(2,1)}, bf16[4,16,32,1536]{3,2,1,0:T(8,128)(2,1)S(1)}, u32[]{:S(2)}) %copy-start) | copy-done | bytes 6291480
  83.2 1.0 copy-done.3
  84.1 33.4 %all-gather.3.cloned.1.call-done = bf16[48,2,192,512]{3,2,1,0:T(8,128)(2,1)} async-done(((bf16[3,2,192,512]{3,2,1,0:T(8,128)(2,1)}), bf16[48,2,192,512]{3,2,1,0:T(8,128)(2,1)}) %all-gather.3.cloned.1.call-update) | async-done | bytes 18874384 | tf_op jit(solution)/shard_map/all_gather | solution.py:380
  117.5 17.0 %experts.1 = (bf16[8,128,768]{2,1,0:T(8,128)(2,1)S(1)}, bf16[8,128,768]{2,1,0:T(8,128)(2,1)S(1)}, bf16[4,16,32,512]{3,2,1,0:T(8,128)(2,1)S(1)}) custom-call(s32[3]{0:T(128)S(1)} %pad_add_fusion.place_ref, bf16[4,16,32,1536]{3,2,1,0:T(8,128)(2,1)} %copy-done, f32[4,16,32,1]{3,2,1,0:T(8,128)} %copy-done.3, bf16[16,128,128]{2,1,0:T(8,128)(2,1)} %copy-done.2, ...), custom_call_target="tpu_custom_call" | custom-call | tf_op jit(solution)/shard_map/experts/pallas_call | solution.py:276
  135.9 6.1 %kept.1 = (bf16[8,128,768]{2,1,0:T(8,128)(2,1)S(1)}, bf16[8,128,768]{2,1,0:T(8,128)(2,1)S(1)}) custom-call(s32[3]{0:T(128)S(1)} %pad_add_fusion.place_ref, bf16[4,16,32,512]{3,2,1,0:T(8,128)(2,1)S(1)} %get-tuple-element.20.act_ref, bf16[16,128,128]{2,1,0:T(8,128)(2,1)} %copy-done.2, bf16[2,8,3,2,192,512]{5,4,3,2,1,0:T(8,128)(2,1)} %bitcast.24), custom_call_target="tpu_custom_call" | custom-call | tf_op jit(solution)/shard_map/kept/pallas_call | solution.py:322
  142.1 14.1 %collective-permute-done.12 = bf16[8,128,768]{2,1,0:T(8,128)(2,1)S(1)} collective-permute-done((bf16[8,128,768]{2,1,0:T(8,128)(2,1)S(1)}, bf16[8,128,768]{2,1,0:T(8,128)(2,1)S(1)}, u32[]{:S(2)}, u32[]{:S(2)}) %collective-permute-start.12) | collective-permute-done | bytes 1572896 | tf_op jit(solution)/shard_map/ppermute | solution.py:60
  157.3 1.4 collective-permute-start.9
  158.7 10.2 %collective-permute-done.13 = bf16[4,128,768]{2,1,0:T(8,128)(2,1)S(1)} collective-permute-done((bf16[4,128,768]{2,1,0:T(8,128)(2,1)S(1)}, bf16[4,128,768]{2,1,0:T(8,128)(2,1)S(1)}, u32[]{:S(2)}, u32[]{:S(2)}) %collective-permute-start.13) | collective-permute-done | bytes 786464 | tf_op jit(solution)/shard_map/ppermute | solution.py:60
  169.1 2.8 %collective-permute-start.14 = (bf16[2,128,768]{2,1,0:T(8,128)(2,1)S(1)}, bf16[2,128,768]{2,1,0:T(8,128)(2,1)S(1)}, u32[]{:S(2)}, u32[]{:S(2)}) collective-permute-start(bf16[2,128,768]{2,1,0:T(8,128)(2,1)S(1)} %get-tuple-element.30), channel_id=1, source_target_pairs={{0,48},{8,200},{16,32},{24,216},{32,16},{40,232},{48,0},{56,248},{... | collective-permute-start | bytes 1179656 | tf_op jit(solution)/shard_map/ppermute | solution.py:60
  172.5 5.6 %collective-permute-done.14 = bf16[2,128,768]{2,1,0:T(8,128)(2,1)S(1)} collective-permute-done((bf16[2,128,768]{2,1,0:T(8,128)(2,1)S(1)}, bf16[2,128,768]{2,1,0:T(8,128)(2,1)S(1)}, u32[]{:S(2)}, u32[]{:S(2)}) %collective-permute-start.14) | collective-permute-done | bytes 393248 | tf_op jit(solution)/shard_map/ppermute | solution.py:60
  178.6 1.4 collective-permute-done.10
  180.0 1.5 collective-permute-start.11
  181.6 2.4 %collective-permute-done.15.refs_3_ = bf16[128,768]{1,0:T(8,128)(2,1)S(1)} collective-permute-done((bf16[128,768]{1,0:T(8,128)(2,1)S(1)}, bf16[128,768]{1,0:T(8,128)(2,1)S(1)}, u32[]{:S(2)}, u32[]{:S(2)}) %collective-permute-start.15) | collective-permute-done | bytes 196640 | tf_op jit(solution)/shard_map/ppermute | solution.py:60
  184.0 3.0 %collective-permute-done.11.refs_1_ = bf16[128,768]{1,0:T(8,128)(2,1)S(1)} collective-permute-done((bf16[128,768]{1,0:T(8,128)(2,1)S(1)}, bf16[128,768]{1,0:T(8,128)(2,1)S(1)}, u32[]{:S(2)}, u32[]{:S(2)}) %collective-permute-start.11) | collective-permute-done | bytes 196640 | tf_op jit(solution)/shard_map/ppermute | solution.py:60
  187.0 1.0 closing.1
  (53 shorter events, 6.5 us)
Async XLA Ops:
  6.5 111.0 %all-gather.3.cloned.1.call-start = ((), (), s32[]{:S(2)}) async-start(), calls=%async_computation | async-start | bytes 20054016 | tf_op jit(solution)/shard_map/all_gather | solution.py:380
  6.5 2.5 %copy-start.12 = (f32[1536]{0:T(1024)S(1)}, f32[1536]{0:T(1024)}, u32[]{:S(2)}) copy-start(f32[1536]{0:T(1024)} %param.15) | copy-start | bytes 18436
  6.5 2.6 %copy-start.6 = (bf16[128,1536]{1,0:T(8,128)(2,1)S(1)}, bf16[128,1536]{1,0:T(8,128)(2,1)}, u32[]{:S(2)}) copy-start(bf16[128,1536]{1,0:T(8,128)(2,1)} %attn_ref.1) | copy-start | bytes 1179652
  6.5 2.6 %copy-start.7 = (bf16[128,1536]{1,0:T(8,128)(2,1)S(1)}, bf16[128,1536]{1,0:T(8,128)(2,1)}, u32[]{:S(2)}) copy-start(bf16[128,1536]{1,0:T(8,128)(2,1)} %resid_ref.1) | copy-start | bytes 1179652
  6.5 2.6 %copy-start.8 = (f32[1536,40]{0,1:T(8,128)S(1)}, f32[1536,40]{0,1:T(8,128)}, u32[]{:S(2)}) copy-start(f32[1536,40]{0,1:T(8,128)} %param.16) | copy-start | bytes 737284
  6.5 2.6 %copy-start.9 = (s32[128,8]{0,1:T(8,128)S(1)}, s32[128,8]{0,1:T(8,128)}, u32[]{:S(2)}) copy-start(s32[128,8]{0,1:T(8,128)} %param.17) | copy-start | bytes 12292
  6.6 2.6 %copy-start.10 = (s32[64]{0:T(128)S(1)}, s32[64]{0:T(128)}, u32[]{:S(2)}) copy-start(s32[64]{0:T(128)} %param.18) | copy-start | bytes 772
  6.6 2.6 %copy-start.11 = (s32[128]{0:T(128)S(1)}, s32[128]{0:T(128)}, u32[]{:S(2)}) copy-start(s32[128]{0:T(128)} %param.19) | copy-start | bytes 1540
  9.2 2.3 %copy-start.1 = (bf16[1536,1536]{1,0:T(8,128)(2,1)S(1)}, bf16[1536,1536]{1,0:T(8,128)(2,1)}, u32[]{:S(2)}) copy-start(bf16[1536,1536]{1,0:T(8,128)(2,1)} %wo_ref.1) | copy-start | bytes 14155780
  14.9 15.8 %copy-start.4 = (f32[128,1536]{1,0:T(8,128)}, f32[128,1536]{1,0:T(8,128)S(1)}, u32[]{:S(2)}) copy-start(f32[128,1536]{1,0:T(8,128)S(1)} %get-tuple-element.15.hidden_ref) | copy-start | bytes 2359300
  15.0 6.0 %collective-permute-start.4 = (bf16[1,144,768]{2,1,0:T(8,128)(2,1)S(1)}, bf16[1,144,768]{2,1,0:T(8,128)(2,1)S(1)}, u32[]{:S(2)}, u32[]{:S(2)}) collective-permute-start(bf16[1,144,768]{2,1,0:T(8,128)(2,1)S(1)} %get-tuple-element.37), channel_id=1, source_target_pairs={{0,16},{8,72},{16,0},{24,88},{32,48},{40,104},{48,32},{56,120},{64... | collective-permute-start | bytes 663560 | tf_op jit(solution)/shard_map/ppermute | solution.py:60
  16.6 7.5 %collective-permute-start = (bf16[1,144,768]{2,1,0:T(8,128)(2,1)S(1)}, bf16[1,144,768]{2,1,0:T(8,128)(2,1)S(1)}, u32[]{:S(2)}, u32[]{:S(2)}) collective-permute-start(bf16[1,144,768]{2,1,0:T(8,128)(2,1)S(1)} %get-tuple-element.38), channel_id=1, source_target_pairs={{0,48},{8,200},{16,32},{24,216},{32,16},{40,232},{48,0},{56,248},{... | collective-permute-start | bytes 663560 | tf_op jit(solution)/shard_map/ppermute | solution.py:60
  21.0 9.6 %collective-permute-start.5 = (bf16[2,144,768]{2,1,0:T(8,128)(2,1)S(1)}, bf16[2,144,768]{2,1,0:T(8,128)(2,1)S(1)}, u32[]{:S(2)}, u32[]{:S(2)}) collective-permute-start(bf16[2,144,768]{2,1,0:T(8,128)(2,1)S(1)} %pad_maximum_fusion.6), channel_id=1, source_target_pairs={{0,48},{8,200},{16,32},{24,216},{32,16},{40,232},{48,0},{56,248},{... | collective-permute-start | bytes 1327112 | tf_op jit(solution)/shard_map/ppermute | solution.py:60
  24.2 9.3 %collective-permute-start.1 = (bf16[2,144,768]{2,1,0:T(8,128)(2,1)S(1)}, bf16[2,144,768]{2,1,0:T(8,128)(2,1)S(1)}, u32[]{:S(2)}, u32[]{:S(2)}) collective-permute-start(bf16[2,144,768]{2,1,0:T(8,128)(2,1)S(1)} %pad_maximum_fusion.5), channel_id=1, source_target_pairs={{0,16},{8,72},{16,0},{24,88},{32,48},{40,104},{48,32},{56,120},{64... | collective-permute-start | bytes 1327112 | tf_op jit(solution)/shard_map/ppermute | solution.py:60
  30.7 13.1 %collective-permute-start.6 = (bf16[4,144,768]{2,1,0:T(8,128)(2,1)S(1)}, bf16[4,144,768]{2,1,0:T(8,128)(2,1)S(1)}, u32[]{:S(2)}, u32[]{:S(2)}) collective-permute-start(bf16[4,144,768]{2,1,0:T(8,128)(2,1)S(1)} %pad_maximum_fusion.4), channel_id=1, source_target_pairs={{0,64},{8,24},{16,80},{24,8},{32,96},{40,56},{48,112},{56,40},{64,... | collective-permute-start | bytes 2654216 | tf_op jit(solution)/shard_map/ppermute | solution.py:60
  33.5 14.3 %collective-permute-start.2 = (bf16[4,144,768]{2,1,0:T(8,128)(2,1)S(1)}, bf16[4,144,768]{2,1,0:T(8,128)(2,1)S(1)}, u32[]{:S(2)}, u32[]{:S(2)}) collective-permute-start(bf16[4,144,768]{2,1,0:T(8,128)(2,1)S(1)} %pad_maximum_fusion.3), channel_id=1, source_target_pairs={{0,192},{8,56},{16,208},{24,40},{32,224},{40,24},{48,240},{56,8},{... | collective-permute-start | bytes 2654216 | tf_op jit(solution)/shard_map/ppermute | solution.py:60
  44.0 23.9 %collective-permute-start.7 = (bf16[8,144,768]{2,1,0:T(8,128)(2,1)S(1)}, bf16[8,144,768]{2,1,0:T(8,128)(2,1)}, u32[]{:S(2)}, u32[]{:S(2)}) collective-permute-start(bf16[8,144,768]{2,1,0:T(8,128)(2,1)S(1)} %pad_maximum_fusion.1.refs_2_), channel_id=1, source_target_pairs={{0,192},{8,56},{16,208},{24,40},{32,224},{40,24},{48,240},{56,8},{... | collective-permute-start | bytes 5308424 | tf_op jit(solution)/shard_map/ppermute | solution.py:60
  48.0 22.9 %collective-permute-start.3 = (bf16[8,144,768]{2,1,0:T(8,128)(2,1)S(1)}, bf16[8,144,768]{2,1,0:T(8,128)(2,1)}, u32[]{:S(2)}, u32[]{:S(2)}) collective-permute-start(bf16[8,144,768]{2,1,0:T(8,128)(2,1)S(1)} %pad_maximum_fusion.refs_0_), channel_id=1, source_target_pairs={{0,64},{8,24},{16,80},{24,8},{32,96},{40,56},{48,112},{56,40},{64,... | collective-permute-start | bytes 5308424 | tf_op jit(solution)/shard_map/ppermute | solution.py:60
  79.7 2.7 %copy-start = (bf16[4,16,32,1536]{3,2,1,0:T(8,128)(2,1)}, bf16[4,16,32,1536]{3,2,1,0:T(8,128)(2,1)S(1)}, u32[]{:S(2)}) copy-start(bf16[4,16,32,1536]{3,2,1,0:T(8,128)(2,1)S(1)} %get-tuple-element.17.packed_hbm) | copy-start | bytes 18874372
  82.4 0.8 copy-start.2
  83.2 1.0 copy-start.3
  134.5 21.7 %collective-permute-start.12 = (bf16[8,128,768]{2,1,0:T(8,128)(2,1)S(1)}, bf16[8,128,768]{2,1,0:T(8,128)(2,1)S(1)}, u32[]{:S(2)}, u32[]{:S(2)}) collective-permute-start(bf16[8,128,768]{2,1,0:T(8,128)(2,1)S(1)} %get-tuple-element.24), channel_id=1, source_target_pairs={{0,192},{8,56},{16,208},{24,40},{32,224},{40,24},{48,240},{56,8},{... | collective-permute-start | bytes 4718600 | tf_op jit(solution)/shard_map/ppermute | solution.py:60
  135.0 21.9 %collective-permute-start.8 = (bf16[8,128,768]{2,1,0:T(8,128)(2,1)S(1)}, bf16[8,128,768]{2,1,0:T(8,128)(2,1)S(1)}, u32[]{:S(2)}, u32[]{:S(2)}) collective-permute-start(bf16[8,128,768]{2,1,0:T(8,128)(2,1)S(1)} %get-tuple-element.22), channel_id=1, source_target_pairs={{0,64},{8,24},{16,80},{24,8},{32,96},{40,56},{48,112},{56,40},{64,... | collective-permute-start | bytes 4718600 | tf_op jit(solution)/shard_map/ppermute | solution.py:60
  156.6 12.3 %collective-permute-start.13 = (bf16[4,128,768]{2,1,0:T(8,128)(2,1)S(1)}, bf16[4,128,768]{2,1,0:T(8,128)(2,1)S(1)}, u32[]{:S(2)}, u32[]{:S(2)}) collective-permute-start(bf16[4,128,768]{2,1,0:T(8,128)(2,1)S(1)} %get-tuple-element.26), channel_id=1, source_target_pairs={{0,64},{8,24},{16,80},{24,8},{32,96},{40,56},{48,112},{56,40},{64,... | collective-permute-start | bytes 2359304 | tf_op jit(solution)/shard_map/ppermute | solution.py:60
  157.3 14.5 %collective-permute-start.9 = (bf16[4,128,768]{2,1,0:T(8,128)(2,1)S(1)}, bf16[4,128,768]{2,1,0:T(8,128)(2,1)S(1)}, u32[]{:S(2)}, u32[]{:S(2)}) collective-permute-start(bf16[4,128,768]{2,1,0:T(8,128)(2,1)S(1)} %get-tuple-element.28), channel_id=1, source_target_pairs={{0,192},{8,56},{16,208},{24,40},{32,224},{40,24},{48,240},{56,8},{... | collective-permute-start | bytes 2359304 | tf_op jit(solution)/shard_map/ppermute | solution.py:60
  169.1 9.1 %collective-permute-start.14 = (bf16[2,128,768]{2,1,0:T(8,128)(2,1)S(1)}, bf16[2,128,768]{2,1,0:T(8,128)(2,1)S(1)}, u32[]{:S(2)}, u32[]{:S(2)}) collective-permute-start(bf16[2,128,768]{2,1,0:T(8,128)(2,1)S(1)} %get-tuple-element.30), channel_id=1, source_target_pairs={{0,48},{8,200},{16,32},{24,216},{32,16},{40,232},{48,0},{56,248},{... | collective-permute-start | bytes 1179656 | tf_op jit(solution)/shard_map/ppermute | solution.py:60
  172.1 9.5 %copy-start.13 = (f32[1536]{0:T(1024)S(1)}, f32[1536]{0:T(1024)}, u32[]{:S(2)}) copy-start(f32[1536]{0:T(1024)} %param.23) | copy-start | bytes 18436
  172.1 14.9 %copy-start.5 = (f32[128,1536]{1,0:T(8,128)S(1)}, f32[128,1536]{1,0:T(8,128)}, u32[]{:S(2)}) copy-start(f32[128,1536]{1,0:T(8,128)} %copy-done.4) | copy-start | bytes 2359300
  172.1 7.9 %collective-permute-start.10 = (bf16[2,128,768]{2,1,0:T(8,128)(2,1)S(1)}, bf16[2,128,768]{2,1,0:T(8,128)(2,1)S(1)}, u32[]{:S(2)}, u32[]{:S(2)}) collective-permute-start(bf16[2,128,768]{2,1,0:T(8,128)(2,1)S(1)} %get-tuple-element.32), channel_id=1, source_target_pairs={{0,16},{8,72},{16,0},{24,88},{32,48},{40,104},{48,32},{56,120},{64... | collective-permute-start | bytes 1179656 | tf_op jit(solution)/shard_map/ppermute | solution.py:60
  178.3 5.8 %collective-permute-start.15 = (bf16[128,768]{1,0:T(8,128)(2,1)S(1)}, bf16[128,768]{1,0:T(8,128)(2,1)S(1)}, u32[]{:S(2)}, u32[]{:S(2)}) collective-permute-start(bf16[128,768]{1,0:T(8,128)(2,1)S(1)} %get-tuple-element.33), channel_id=1, source_target_pairs={{0,16},{8,72},{16,0},{24,88},{32,48},{40,104},{48,32},{56,120},{64... | collective-permute-start | bytes 589832 | tf_op jit(solution)/shard_map/ppermute | solution.py:60
  180.0 7.0 %collective-permute-start.11 = (bf16[128,768]{1,0:T(8,128)(2,1)S(1)}, bf16[128,768]{1,0:T(8,128)(2,1)S(1)}, u32[]{:S(2)}, u32[]{:S(2)}) collective-permute-start(bf16[128,768]{1,0:T(8,128)(2,1)S(1)} %get-tuple-element.35), channel_id=1, source_target_pairs={{0,48},{8,200},{16,32},{24,216},{32,16},{40,232},{48,0},{56,248},{... | collective-permute-start | bytes 589832 | tf_op jit(solution)/shard_map/ppermute | solution.py:60
Sparse Core Ops, SparseCore 0:
  9.2 108.2 all-gather.2

commit v4 on v3

--- a/solution.py
+++ b/solution.py
@@ -66,6 +66,29 @@
         return carry
 
     lax.fori_loop(0, count, run, 0, unroll=unroll)
+
+
+def join_kernel(*refs):
+    shards, joined, sems = refs[:-2], refs[-2], refs[-1]
+    copies = [
+        pltpu.make_async_copy(shard, joined.at[n], sems.at[n]) for n, shard in enumerate(shards)
+    ]
+    for copy in copies:
+        copy.start()
+    for copy in copies:
+        copy.wait()
+
+
+def join(*shards):
+    hbm = pl.BlockSpec(memory_space=pltpu.HBM)
+    return pl.pallas_call(
+        join_kernel,
+        in_specs=[hbm] * len(shards),
+        out_specs=hbm,
+        out_shape=jax.ShapeDtypeStruct((len(shards), *shards[0].shape), BF16),
+        scratch_shapes=[pltpu.SemaphoreType.DMA((len(shards),))],
+        name="join",
+    )(*shards)
 
 
 def entry_kernel(
@@ -209,7 +232,7 @@
     )(place, *rows)
 
 
-def back_to_rows(plan, place, start, group, act_ref, down_ref, spread_ref, part_ref, out_ref):
+def back_to_rows(plan, place, start, group, act_ref, down_ref, spread_ref, part_ref, out_refs):
     half = BLOCKS // 2
     order = [block_at(plan, place, start + i) for i in range(half)]
     for s in range(LOCAL):
@@ -220,17 +243,18 @@
         )
         part_ref[:, s] = part.astype(BF16).reshape(half, CAP, GROUP)
 
-    def back(i):
-        b = block_at(plan, place, start + i)
-        rows = part_ref[i].reshape(LOCAL * CAP, GROUP)
+    def back(out_ref, first, i):
+        b = block_at(plan, place, start + first + i)
+        rows = part_ref[first + i].reshape(LOCAL * CAP, GROUP)
         out_ref[i] = jnp.dot(spread_ref[b], rows, preferred_element_type=F32).astype(BF16)
 
-    each(half, 4, back)
+    for n, out_ref in enumerate(out_refs):
+        each(half // 2, 4, functools.partial(back, out_ref, n * half // 2))
 
 
 def experts_kernel(place_ref, packed_hbm, scale_hbm, spread_hbm, weights_hbm, *refs):
-    out_refs, act_ref = refs[:GROUPS], refs[GROUPS]
-    packed_ref, scale_ref, gate_ref, up_ref, down_ref, spread_ref, part_ref = refs[GROUPS + 1 : -3]
+    out_refs, act_ref = refs[: 2 * GROUPS], refs[2 * GROUPS]
+    packed_ref, scale_ref, gate_ref, up_ref, down_ref, spread_ref, part_ref = refs[2 * GROUPS + 1 : -3]
     slot_sems, down_sems, once_sems = refs[-3:]
     blks = 8 // GROUPS
     fetch = pltpu.make_async_copy
@@ -266,7 +290,8 @@
     for g, plan in enumerate(PLANS):
         by_group[g].wait()
         back_to_rows(
-            plan, place_of(place_ref), BLOCKS // 2, g, act_ref, down_ref, spread_ref, part_ref, out_refs[g]
+            plan, place_of(place_ref), BLOCKS // 2, g, act_ref, down_ref, spread_ref, part_ref,
+            out_refs[2 * g : 2 * g + 2],
         )
 
 
@@ -276,8 +301,8 @@
     return pl.pallas_call(
         experts_kernel,
         in_specs=[pl.BlockSpec(memory_space=pltpu.SMEM), hbm, hbm, hbm, hbm],
-        out_specs=[vmem] * (GROUPS + 1),
-        out_shape=[jax.ShapeDtypeStruct((half, ROWS, GROUP), BF16)] * GROUPS
+        out_specs=[vmem] * (2 * GROUPS + 1),
+        out_shape=[jax.ShapeDtypeStruct((half // 2, ROWS, GROUP), BF16)] * (2 * GROUPS)
         + [jax.ShapeDtypeStruct((LOCAL, BLOCKS, CAP, FF), BF16)],
         scratch_shapes=[
             pltpu.VMEM(packed.shape, BF16),
@@ -297,7 +322,7 @@
 
 
 def kept_kernel(place_ref, act_ref, spread_hbm, weights_hbm, *refs):
-    out_refs, (down_ref, spread_ref, part_ref, sems) = refs[:GROUPS], refs[GROUPS:]
+    out_refs, (down_ref, spread_ref, part_ref, sems) = refs[: 2 * GROUPS], refs[2 * GROUPS :]
     blks = 8 // GROUPS
     copies = [
         pltpu.make_async_copy(
@@ -312,7 +337,8 @@
     for g, plan in enumerate(PLANS):
         copies[g].wait()
         back_to_rows(
-            plan, place_of(place_ref), 0, g, act_ref, down_ref, spread_ref, part_ref, out_refs[g]
+            plan, place_of(place_ref), 0, g, act_ref, down_ref, spread_ref, part_ref,
+            out_refs[2 * g : 2 * g + 2],
         )
 
 
@@ -322,8 +348,8 @@
     return pl.pallas_call(
         kept_kernel,
         in_specs=[pl.BlockSpec(memory_space=pltpu.SMEM), vmem, hbm, hbm],
-        out_specs=[vmem] * GROUPS,
-        out_shape=[jax.ShapeDtypeStruct((half, ROWS, GROUP), BF16)] * GROUPS,
+        out_specs=[vmem] * (2 * GROUPS),
+        out_shape=[jax.ShapeDtypeStruct((half // 2, ROWS, GROUP), BF16)] * (2 * GROUPS),
         scratch_shapes=[
             pltpu.VMEM((GROUPS, 2, 8 // GROUPS, 2, CHUNK, FF), BF16),
             pltpu.VMEM(spread.shape, BF16),
@@ -336,12 +362,9 @@
 
 
 def closing_kernel(hidden_ref, gain_ref, *refs):
-    pairs, out_ref = refs[:-1], refs[-1]
+    parts, out_ref = refs[:-1], refs[-1]
     moe = jnp.concatenate(
-        [
-            pairs[2 * g][...].astype(F32) + pairs[2 * g + 1][...].astype(F32)
-            for g in range(GROUPS)
-        ],
+        [sum(ref[...].astype(F32) for ref in parts[4 * g : 4 * g + 4]) for g in range(GROUPS)],
         axis=1,
     )
     mixed = hidden_ref[...] + moe
@@ -349,13 +372,13 @@
     out_ref[...] = (mixed * lax.rsqrt(mean_sq + EPS) * gain_ref[...]).astype(BF16)
 
 
-def closing(hidden, gain, pairs):
+def closing(hidden, gain, parts):
     return pl.pallas_call(
         closing_kernel,
         out_shape=jax.ShapeDtypeStruct((ROWS, D), BF16),
         compiler_params=params(8),
         name="closing",
-    )(hidden, gain, *pairs)
+    )(hidden, gain, *parts)
 
 
 def spread_out(rows):
@@ -376,7 +399,7 @@
     attn_out, resid, w_o, norm1_gain, router_w, route_slot, slot_expert, keep,
     w_gate, w_up, w_down, norm2_gain,
 ):
-    joined = jnp.stack([w_gate, w_up, w_down])
+    joined = join(w_gate, w_up, w_down)
     weights = lax.all_gather(joined, ("core", "blk"), axis=0, tiled=False)
     weights = weights.reshape(2, 8, 3, 2, CHUNK, FF)
     weights = pltpu.with_memory_space_constraint(weights, pltpu.HBM)
@@ -393,16 +416,17 @@
     ]
     *sends, act = experts(place, packed, scale, spread, weights)
     keeps = kept(place, act, spread, weights)
-    pairs = []
-    for send, keep, (first, other) in zip(sends, keeps, PLANS):
-        got = turned(send, first, True)
-        send, keep = add(keep[4:], got[4:]), add(keep[:4], got[:4])
-        got = turned(send, other, True)
-        send, keep = add(keep[2:], got[2:]), add(keep[:2], got[:2])
-        got = turned(send, first, False)
-        send, keep = add(keep[1], got[1]), add(keep[0], got[0])
-        pairs += [keep, turned(send, other, False)]
-    return closing(hidden, norm2_gain.reshape(1, D), pairs)
+    parts = []
+    for group, (first, other) in enumerate(PLANS):
+        last, soon = sends[2 * group : 2 * group + 2]
+        held, passed = keeps[2 * group : 2 * group + 2]
+        passed = add(passed, turned(soon, first, True))
+        held = add(held, turned(last, first, True))
+        got = turned(passed, other, True)
+        sums = [add(held[i], got[i]) for i in range(4)]
+        turns = (other, first, first ^ other)
+        parts += [sums[0]] + [turned(sums[i + 1], turn, False) for i, turn in enumerate(turns)]
+    return closing(hidden, norm2_gain.reshape(1, D), parts)
 
 
 def solution(mesh):

time: 195 us -> 223 us (1.14)
  Pallas kernels: 36.3 us -> 72.1 us
  waiting for transfers between devices: 113 us -> 98.7 us
  starting transfers between devices: 20.4 us -> 28 us
  other arithmetic: 4.59 us -> 1.82 us
    pallas_call x0 -> x1, Pallas kernels: none -> 36.9 us  [join(): pl.pallas_call(join_kernel, in_specs=[hbm] * len(shards), out_specs=hbm,...]
    ppermute x16 -> x20, waiting for transfers between devices: 79.8 us -> 65.3 us  [turned(): return lax.ppermute(rows, ('x', 'y', 'core'), pairs)]
    ppermute x16 -> x20, starting transfers between devices: 20.4 us -> 27.9 us  [turned(): return lax.ppermute(rows, ('x', 'y', 'core'), pairs)]
    another operation x1 -> x0, other arithmetic: 2.47 us -> none  [body(): joined = jnp.stack([w_gate, w_up, w_down])]
  transfers between devices with their start and end apart: 17 -> 21, of which waited for: 14 -> 14; matrix products, arithmetic and copies ran while one was open for 1% -> 1% of each run, Pallas kernels for 9% -> 8%
where the time goes in v4:
time: 223 us; the launch traced here: 221 us
  waiting for transfers between devices  98.7 us (44%)
  Pallas kernels  72.1 us (32%)
  starting transfers between devices  28 us (13%)
  between operations  13.7 us (6%)
  local copies, waits for them, and re-layouts  6.82 us (3%)
    ppermute x20, waiting for transfers between devices, turned(): return lax.ppermute(rows, ('x', 'y', 'core'), pairs)  65.3 us
    pallas_call x1, Pallas kernels, join(): pl.pallas_call(join_kernel, in_specs=[hbm] * len(shards), out_specs=hbm,...  36.9 us
    all_gather x1, waiting for transfers between devices, body(): weights = lax.all_gather(joined, ('core', 'blk'), axis=0, tiled=False)  33.4 us
    ppermute x20, starting transfers between devices, turned(): return lax.ppermute(rows, ('x', 'y', 'core'), pairs)  27.9 us
    pallas_call x1, Pallas kernels, experts(): pl.pallas_call(experts_kernel, in_specs=[pl.BlockSpec(memory_space=pltpu....  16.4 us
    pallas_call x1, Pallas kernels, compact(): pl.pallas_call(compact_kernel, in_specs=[pl.BlockSpec(memory_space=pltpu....  8.78 us
    unnamed x28, local copies, waits for them, and re-layouts  6.78 us
    pallas_call x1, Pallas kernels, kept(): pl.pallas_call(kept_kernel, in_specs=[pl.BlockSpec(memory_space=pltpu.SME...  5.58 us
  transfers between devices with their start and end apart: 21, of which 14 were waited for; matrix products, arithmetic and copies ran while one was open for 1% of the time, Pallas kernels for 8%

profile of v4, /device:TPU:6, one launch (start us, length us, event | category | flops | bytes accessed | tf_op | source)
XLA Modules:
  0.0 221.2 jit_solution(13359635095130514061)
XLA Ops:
  6.6 36.9 %join.1 = bf16[3,2,192,512]{3,2,1,0:T(8,128)(2,1)} custom-call(bf16[2,192,512]{2,1,0:T(8,128)(2,1)} %refs_0_.1, bf16[2,192,512]{2,1,0:T(8,128)(2,1)} %refs_1_.1, bf16[2,192,512]{2,1,0:T(8,128)(2,1)} %refs_2_.1), custom_call_target="tpu_custom_call" | custom-call | tf_op jit(solution)/shard_map/join/pallas_call | solution.py:84
  43.6 2.3 %copy-done.1 = bf16[1536,1536]{1,0:T(8,128)(2,1)S(1)} copy-done((bf16[1536,1536]{1,0:T(8,128)(2,1)S(1)}, bf16[1536,1536]{1,0:T(8,128)(2,1)}, u32[]{:S(2)}) %copy-start.1) | copy-done | bytes 4718616
  45.9 3.4 %entry.1 = (f32[128,1536]{1,0:T(8,128)S(1)}, bf16[2,144,768]{2,1,0:T(8,128)(2,1)S(1)}) custom-call(bf16[128,1536]{1,0:T(8,128)(2,1)S(1)} %copy-done.6, bf16[128,1536]{1,0:T(8,128)(2,1)S(1)} %copy-done.7, bf16[1536,1536]{1,0:T(8,128)(2,1)S(1)} %copy-done.1, f32[1,1536]{1,0:T(1,128)S(1)} %reshape.47.gain_ref, f32[40,1536]{1,0:T(8,128)S(1)} %bitcast.24, ...), custom_call_target="tpu_custom_call" | custom-call | tf_op jit(solution)/shard_map/entry/pallas_call | solution.py:143
  49.4 1.7 collective-permute-start.4
  51.0 2.2 collective-permute-start
  53.2 2.2 collective-permute-done.4
  55.5 3.1 %collective-permute-start.5 = (bf16[2,144,768]{2,1,0:T(8,128)(2,1)S(1)}, bf16[2,144,768]{2,1,0:T(8,128)(2,1)S(1)}, u32[]{:S(2)}, u32[]{:S(2)}) collective-permute-start(bf16[2,144,768]{2,1,0:T(8,128)(2,1)S(1)} %pad_maximum_fusion.5), channel_id=1, source_target_pairs={{0,48},{8,200},{16,32},{24,216},{32,16},{40,232},{48,0},{56,248},{... | collective-permute-start | bytes 1327112 | tf_op jit(solution)/shard_map/ppermute | solution.py:60
  58.8 6.2 %collective-permute-done.5 = bf16[2,144,768]{2,1,0:T(8,128)(2,1)S(1)} collective-permute-done((bf16[2,144,768]{2,1,0:T(8,128)(2,1)S(1)}, bf16[2,144,768]{2,1,0:T(8,128)(2,1)S(1)}, u32[]{:S(2)}, u32[]{:S(2)}) %collective-permute-start.5) | collective-permute-done | bytes 442400 | tf_op jit(solution)/shard_map/ppermute | solution.py:60
  66.1 1.8 collective-permute-done.1
  68.7 9.6 %collective-permute-done.6 = bf16[4,144,768]{2,1,0:T(8,128)(2,1)S(1)} collective-permute-done((bf16[4,144,768]{2,1,0:T(8,128)(2,1)S(1)}, bf16[4,144,768]{2,1,0:T(8,128)(2,1)S(1)}, u32[]{:S(2)}, u32[]{:S(2)}) %collective-permute-start.6) | collective-permute-done | bytes 884768 | tf_op jit(solution)/shard_map/ppermute | solution.py:60
  78.5 2.3 %collective-permute-start.7 = (bf16[8,144,768]{2,1,0:T(8,128)(2,1)S(1)}, bf16[8,144,768]{2,1,0:T(8,128)(2,1)}, u32[]{:S(2)}, u32[]{:S(2)}) collective-permute-start(bf16[8,144,768]{2,1,0:T(8,128)(2,1)S(1)} %pad_maximum_fusion.1.refs_2_), channel_id=1, source_target_pairs={{0,192},{8,56},{16,208},{24,40},{32,224},{40,24},{48,240},{56,8},{... | collective-permute-start | bytes 5308424 | tf_op jit(solution)/shard_map/ppermute | solution.py:60
  80.8 1.5 collective-permute-done.2
  83.6 18.8 %collective-permute-done.7.refs_3_ = bf16[8,144,768]{2,1,0:T(8,128)(2,1)} collective-permute-done((bf16[8,144,768]{2,1,0:T(8,128)(2,1)S(1)}, bf16[8,144,768]{2,1,0:T(8,128)(2,1)}, u32[]{:S(2)}, u32[]{:S(2)}) %collective-permute-start.7) | collective-permute-done | bytes 1769504 | tf_op jit(solution)/shard_map/ppermute | solution.py:60
  102.4 3.0 %collective-permute-done.3.refs_1_ = bf16[8,144,768]{2,1,0:T(8,128)(2,1)} collective-permute-done((bf16[8,144,768]{2,1,0:T(8,128)(2,1)S(1)}, bf16[8,144,768]{2,1,0:T(8,128)(2,1)}, u32[]{:S(2)}, u32[]{:S(2)}) %collective-permute-start.3) | collective-permute-done | bytes 1769504 | tf_op jit(solution)/shard_map/ppermute | solution.py:60
  105.4 8.8 %compact.1 = (bf16[4,16,32,1536]{3,2,1,0:T(8,128)(2,1)S(1)}, bf16[16,128,128]{2,1,0:T(8,128)(2,1)S(1)}, f32[4,16,32,1]{3,2,1,0:T(8,128)S(1)}) custom-call(s32[3]{0:T(128)S(1)} %pad_add_fusion.place_ref, bf16[8,144,768]{2,1,0:T(8,128)(2,1)S(1)} %pad_maximum_fusion.refs_0_, bf16[8,144,768]{2,1,0:T(8,128)(2,1)} %collective-permute-done.3.refs_1_, ...), custom_call_target="tpu_custom_call" | custom-call | tf_op jit(solution)/shard_map/compact/pallas_call | solution.py:217
  114.1 2.6 %copy-done = bf16[4,16,32,1536]{3,2,1,0:T(8,128)(2,1)} copy-done((bf16[4,16,32,1536]{3,2,1,0:T(8,128)(2,1)}, bf16[4,16,32,1536]{3,2,1,0:T(8,128)(2,1)S(1)}, u32[]{:S(2)}) %copy-start) | copy-done | bytes 6291480
  118.6 33.4 %all-gather.3.cloned.1.call-done = bf16[48,2,192,512]{3,2,1,0:T(8,128)(2,1)} async-done(((bf16[3,2,192,512]{3,2,1,0:T(8,128)(2,1)}), bf16[48,2,192,512]{3,2,1,0:T(8,128)(2,1)}) %all-gather.3.cloned.1.call-update) | async-done | bytes 18874384 | tf_op jit(solution)/shard_map/all_gather | solution.py:403
  151.9 16.4 %experts.1 = (bf16[4,128,768]{2,1,0:T(8,128)(2,1)S(1)}, bf16[4,128,768]{2,1,0:T(8,128)(2,1)S(1)}, bf16[4,128,768]{2,1,0:T(8,128)(2,1)S(1)}, bf16[4,128,768]{2,1,0:T(8,128)(2,1)S(1)}, bf16[4,16,32,512]{3,2,1,0:T(8,128)(2,1)S(1)}) custom-call(s32[3]{0:T(128)S(1)} %pad_add_fusion.place_ref, bf16[4,16,32,1536]{3,2,1,0:T(8,128)(2,1)} %copy-done, ...), custom_call_target="tpu_custom_call" | custom-call | tf_op jit(solution)/shard_map/experts/pallas_call | solution.py:301
  169.8 2.1 collective-permute-start.14
  171.9 5.6 %kept.1 = (bf16[4,128,768]{2,1,0:T(8,128)(2,1)S(1)}, bf16[4,128,768]{2,1,0:T(8,128)(2,1)S(1)}, bf16[4,128,768]{2,1,0:T(8,128)(2,1)S(1)}, bf16[4,128,768]{2,1,0:T(8,128)(2,1)S(1)}) custom-call(s32[3]{0:T(128)S(1)} %pad_add_fusion.place_ref, bf16[4,16,32,512]{3,2,1,0:T(8,128)(2,1)S(1)} %get-tuple-element.24.act_ref, bf16[16,128,128]{2,1,0:T(8,128)(2,1)} %copy-done.2, ...), custom_call_target="tpu_custom_call" | custom-call | tf_op jit(solution)/shard_map/kept/pallas_call | solution.py:348
  177.5 1.3 collective-permute-start.8
  178.8 2.9 %collective-permute-done.15 = bf16[4,128,768]{2,1,0:T(8,128)(2,1)S(1)} collective-permute-done((bf16[4,128,768]{2,1,0:T(8,128)(2,1)S(1)}, bf16[4,128,768]{2,1,0:T(8,128)(2,1)S(1)}, u32[]{:S(2)}, u32[]{:S(2)}) %collective-permute-start.15) | collective-permute-done | bytes 786464 | tf_op jit(solution)/shard_map/ppermute | solution.py:60
  182.1 1.8 collective-permute-start.10
  183.9 6.1 %collective-permute-done.14 = bf16[4,128,768]{2,1,0:T(8,128)(2,1)S(1)} collective-permute-done((bf16[4,128,768]{2,1,0:T(8,128)(2,1)S(1)}, bf16[4,128,768]{2,1,0:T(8,128)(2,1)S(1)}, u32[]{:S(2)}, u32[]{:S(2)}) %collective-permute-start.14) | collective-permute-done | bytes 786464 | tf_op jit(solution)/shard_map/ppermute | solution.py:60
  190.5 7.5 %collective-permute-done.16 = bf16[4,128,768]{2,1,0:T(8,128)(2,1)S(1)} collective-permute-done((bf16[4,128,768]{2,1,0:T(8,128)(2,1)S(1)}, bf16[4,128,768]{2,1,0:T(8,128)(2,1)S(1)}, u32[]{:S(2)}, u32[]{:S(2)}) %collective-permute-start.16) | collective-permute-done | bytes 786464 | tf_op jit(solution)/shard_map/ppermute | solution.py:60
  198.2 1.5 collective-permute-start.17
  199.7 2.1 collective-permute-start.18
  202.6 2.7 %collective-permute-start.11 = (bf16[128,768]{1,0:T(8,128)(2,1)S(1)}, bf16[128,768]{1,0:T(8,128)(2,1)S(1)}, u32[]{:S(2)}, u32[]{:S(2)}) collective-permute-start(bf16[128,768]{1,0:T(8,128)(2,1)S(1)} %get-tuple-element.39), channel_id=1, source_target_pairs={{0,48},{8,200},{16,32},{24,216},{32,16},{40,232},{48,0},{56,248},{... | collective-permute-start | bytes 589832 | tf_op jit(solution)/shard_map/ppermute | solution.py:60
  205.6 1.8 collective-permute-start.13
  207.4 1.7 collective-permute-done.19.refs_7_
  209.1 2.0 collective-permute-done.11.refs_1_
  211.1 2.1 collective-permute-done.13.refs_3_
  (61 shorter events, 10.2 us)
Async XLA Ops:
  6.5 37.0 %copy-start.12 = (f32[1536]{0:T(1024)S(1)}, f32[1536]{0:T(1024)}, u32[]{:S(2)}) copy-start(f32[1536]{0:T(1024)} %param.15) | copy-start | bytes 18436
  6.5 37.0 %copy-start.8 = (f32[1536,40]{0,1:T(8,128)S(1)}, f32[1536,40]{0,1:T(8,128)}, u32[]{:S(2)}) copy-start(f32[1536,40]{0,1:T(8,128)} %param.16) | copy-start | bytes 737284
  6.5 37.0 %copy-start.9 = (s32[128,8]{0,1:T(8,128)S(1)}, s32[128,8]{0,1:T(8,128)}, u32[]{:S(2)}) copy-start(s32[128,8]{0,1:T(8,128)} %param.17) | copy-start | bytes 12292
  6.5 37.0 %copy-start.10 = (s32[64]{0:T(128)S(1)}, s32[64]{0:T(128)}, u32[]{:S(2)}) copy-start(s32[64]{0:T(128)} %param.18) | copy-start | bytes 772
  6.5 37.0 %copy-start.11 = (s32[128]{0:T(128)S(1)}, s32[128]{0:T(128)}, u32[]{:S(2)}) copy-start(s32[128]{0:T(128)} %param.19) | copy-start | bytes 1540
  6.5 37.0 %copy-start.6 = (bf16[128,1536]{1,0:T(8,128)(2,1)S(1)}, bf16[128,1536]{1,0:T(8,128)(2,1)}, u32[]{:S(2)}) copy-start(bf16[128,1536]{1,0:T(8,128)(2,1)} %attn_ref.1) | copy-start | bytes 1179652
  6.6 37.0 %copy-start.7 = (bf16[128,1536]{1,0:T(8,128)(2,1)S(1)}, bf16[128,1536]{1,0:T(8,128)(2,1)}, u32[]{:S(2)}) copy-start(bf16[128,1536]{1,0:T(8,128)(2,1)} %resid_ref.1) | copy-start | bytes 1179652
  6.6 145.4 %all-gather.3.cloned.1.call-start = ((), (), s32[]{:S(2)}) async-start(), calls=%async_computation | async-start | bytes 20054016 | tf_op jit(solution)/shard_map/all_gather | solution.py:403
  49.3 15.8 %copy-start.4 = (f32[128,1536]{1,0:T(8,128)}, f32[128,1536]{1,0:T(8,128)S(1)}, u32[]{:S(2)}) copy-start(f32[128,1536]{1,0:T(8,128)S(1)} %get-tuple-element.19.hidden_ref) | copy-start | bytes 2359300
  49.4 6.0 %collective-permute-start.4 = (bf16[1,144,768]{2,1,0:T(8,128)(2,1)S(1)}, bf16[1,144,768]{2,1,0:T(8,128)(2,1)S(1)}, u32[]{:S(2)}, u32[]{:S(2)}) collective-permute-start(bf16[1,144,768]{2,1,0:T(8,128)(2,1)S(1)} %get-tuple-element.41), channel_id=1, source_target_pairs={{0,16},{8,72},{16,0},{24,88},{32,48},{40,104},{48,32},{56,120},{64... | collective-permute-start | bytes 663560 | tf_op jit(solution)/shard_map/ppermute | solution.py:60
  51.0 7.5 %collective-permute-start = (bf16[1,144,768]{2,1,0:T(8,128)(2,1)S(1)}, bf16[1,144,768]{2,1,0:T(8,128)(2,1)S(1)}, u32[]{:S(2)}, u32[]{:S(2)}) collective-permute-start(bf16[1,144,768]{2,1,0:T(8,128)(2,1)S(1)} %get-tuple-element.42), channel_id=1, source_target_pairs={{0,48},{8,200},{16,32},{24,216},{32,16},{40,232},{48,0},{56,248},{... | collective-permute-start | bytes 663560 | tf_op jit(solution)/shard_map/ppermute | solution.py:60
  55.5 9.6 %collective-permute-start.5 = (bf16[2,144,768]{2,1,0:T(8,128)(2,1)S(1)}, bf16[2,144,768]{2,1,0:T(8,128)(2,1)S(1)}, u32[]{:S(2)}, u32[]{:S(2)}) collective-permute-start(bf16[2,144,768]{2,1,0:T(8,128)(2,1)S(1)} %pad_maximum_fusion.5), channel_id=1, source_target_pairs={{0,48},{8,200},{16,32},{24,216},{32,16},{40,232},{48,0},{56,248},{... | collective-permute-start | bytes 1327112 | tf_op jit(solution)/shard_map/ppermute | solution.py:60
  58.6 9.3 %collective-permute-start.1 = (bf16[2,144,768]{2,1,0:T(8,128)(2,1)S(1)}, bf16[2,144,768]{2,1,0:T(8,128)(2,1)S(1)}, u32[]{:S(2)}, u32[]{:S(2)}) collective-permute-start(bf16[2,144,768]{2,1,0:T(8,128)(2,1)S(1)} %pad_maximum_fusion.4), channel_id=1, source_target_pairs={{0,16},{8,72},{16,0},{24,88},{32,48},{40,104},{48,32},{56,120},{64... | collective-permute-start | bytes 1327112 | tf_op jit(solution)/shard_map/ppermute | solution.py:60
  65.2 13.1 %collective-permute-start.6 = (bf16[4,144,768]{2,1,0:T(8,128)(2,1)S(1)}, bf16[4,144,768]{2,1,0:T(8,128)(2,1)S(1)}, u32[]{:S(2)}, u32[]{:S(2)}) collective-permute-start(bf16[4,144,768]{2,1,0:T(8,128)(2,1)S(1)} %pad_maximum_fusion.3), channel_id=1, source_target_pairs={{0,64},{8,24},{16,80},{24,8},{32,96},{40,56},{48,112},{56,40},{64,... | collective-permute-start | bytes 2654216 | tf_op jit(solution)/shard_map/ppermute | solution.py:60
  67.9 14.3 %collective-permute-start.2 = (bf16[4,144,768]{2,1,0:T(8,128)(2,1)S(1)}, bf16[4,144,768]{2,1,0:T(8,128)(2,1)S(1)}, u32[]{:S(2)}, u32[]{:S(2)}) collective-permute-start(bf16[4,144,768]{2,1,0:T(8,128)(2,1)S(1)} %pad_maximum_fusion.2), channel_id=1, source_target_pairs={{0,192},{8,56},{16,208},{24,40},{32,224},{40,24},{48,240},{56,8},{... | collective-permute-start | bytes 2654216 | tf_op jit(solution)/shard_map/ppermute | solution.py:60
  78.5 23.9 %collective-permute-start.7 = (bf16[8,144,768]{2,1,0:T(8,128)(2,1)S(1)}, bf16[8,144,768]{2,1,0:T(8,128)(2,1)}, u32[]{:S(2)}, u32[]{:S(2)}) collective-permute-start(bf16[8,144,768]{2,1,0:T(8,128)(2,1)S(1)} %pad_maximum_fusion.1.refs_2_), channel_id=1, source_target_pairs={{0,192},{8,56},{16,208},{24,40},{32,224},{40,24},{48,240},{56,8},{... | collective-permute-start | bytes 5308424 | tf_op jit(solution)/shard_map/ppermute | solution.py:60
  82.5 22.9 %collective-permute-start.3 = (bf16[8,144,768]{2,1,0:T(8,128)(2,1)S(1)}, bf16[8,144,768]{2,1,0:T(8,128)(2,1)}, u32[]{:S(2)}, u32[]{:S(2)}) collective-permute-start(bf16[8,144,768]{2,1,0:T(8,128)(2,1)S(1)} %pad_maximum_fusion.refs_0_), channel_id=1, source_target_pairs={{0,64},{8,24},{16,80},{24,8},{32,96},{40,56},{48,112},{56,40},{64,... | collective-permute-start | bytes 5308424 | tf_op jit(solution)/shard_map/ppermute | solution.py:60
  114.1 2.7 %copy-start = (bf16[4,16,32,1536]{3,2,1,0:T(8,128)(2,1)}, bf16[4,16,32,1536]{3,2,1,0:T(8,128)(2,1)S(1)}, u32[]{:S(2)}) copy-start(bf16[4,16,32,1536]{3,2,1,0:T(8,128)(2,1)S(1)} %get-tuple-element.21.packed_hbm) | copy-start | bytes 18874372
  168.3 13.3 %collective-permute-start.15 = (bf16[4,128,768]{2,1,0:T(8,128)(2,1)S(1)}, bf16[4,128,768]{2,1,0:T(8,128)(2,1)S(1)}, u32[]{:S(2)}, u32[]{:S(2)}) collective-permute-start(bf16[4,128,768]{2,1,0:T(8,128)(2,1)S(1)} %get-tuple-element.32), channel_id=1, source_target_pairs={{0,192},{8,56},{16,208},{24,40},{32,224},{40,24},{48,240},{56,8},{... | collective-permute-start | bytes 2359304 | tf_op jit(solution)/shard_map/ppermute | solution.py:60
  168.9 13.0 %collective-permute-start.9 = (bf16[4,128,768]{2,1,0:T(8,128)(2,1)S(1)}, bf16[4,128,768]{2,1,0:T(8,128)(2,1)S(1)}, u32[]{:S(2)}, u32[]{:S(2)}) collective-permute-start(bf16[4,128,768]{2,1,0:T(8,128)(2,1)S(1)} %get-tuple-element.28), channel_id=1, source_target_pairs={{0,64},{8,24},{16,80},{24,8},{32,96},{40,56},{48,112},{56,40},{64,... | collective-permute-start | bytes 2359304 | tf_op jit(solution)/shard_map/ppermute | solution.py:60
  169.8 20.3 %collective-permute-start.14 = (bf16[4,128,768]{2,1,0:T(8,128)(2,1)S(1)}, bf16[4,128,768]{2,1,0:T(8,128)(2,1)S(1)}, u32[]{:S(2)}, u32[]{:S(2)}) collective-permute-start(bf16[4,128,768]{2,1,0:T(8,128)(2,1)S(1)} %get-tuple-element.30), channel_id=1, source_target_pairs={{0,192},{8,56},{16,208},{24,40},{32,224},{40,24},{48,240},{56,8},{... | collective-permute-start | bytes 2359304 | tf_op jit(solution)/shard_map/ppermute | solution.py:60
  177.5 12.8 %collective-permute-start.8 = (bf16[4,128,768]{2,1,0:T(8,128)(2,1)S(1)}, bf16[4,128,768]{2,1,0:T(8,128)(2,1)S(1)}, u32[]{:S(2)}, u32[]{:S(2)}) collective-permute-start(bf16[4,128,768]{2,1,0:T(8,128)(2,1)S(1)} %get-tuple-element.26), channel_id=1, source_target_pairs={{0,64},{8,24},{16,80},{24,8},{32,96},{40,56},{48,112},{56,40},{64,... | collective-permute-start | bytes 2359304 | tf_op jit(solution)/shard_map/ppermute | solution.py:60
  181.8 16.2 %collective-permute-start.16 = (bf16[4,128,768]{2,1,0:T(8,128)(2,1)S(1)}, bf16[4,128,768]{2,1,0:T(8,128)(2,1)S(1)}, u32[]{:S(2)}, u32[]{:S(2)}) collective-permute-start(bf16[4,128,768]{2,1,0:T(8,128)(2,1)S(1)} %add_convert_fusion), channel_id=1, source_target_pairs={{0,64},{8,24},{16,80},{24,8},{32,96},{40,56},{48,112},{56,40},{64,... | collective-permute-start | bytes 2359304 | tf_op jit(solution)/shard_map/ppermute | solution.py:60
  182.1 20.3 %collective-permute-start.10 = (bf16[4,128,768]{2,1,0:T(8,128)(2,1)S(1)}, bf16[4,128,768]{2,1,0:T(8,128)(2,1)S(1)}, u32[]{:S(2)}, u32[]{:S(2)}) collective-permute-start(bf16[4,128,768]{2,1,0:T(8,128)(2,1)S(1)} %add_convert_fusion.2), channel_id=1, source_target_pairs={{0,192},{8,56},{16,208},{24,40},{32,224},{40,24},{48,240},{56,8},{... | collective-permute-start | bytes 2359304 | tf_op jit(solution)/shard_map/ppermute | solution.py:60
  198.2 9.2 %copy-start.13 = (f32[1536]{0:T(1024)S(1)}, f32[1536]{0:T(1024)}, u32[]{:S(2)}) copy-start(f32[1536]{0:T(1024)} %param.23) | copy-start | bytes 18436
  198.2 15.0 %copy-start.5 = (f32[128,1536]{1,0:T(8,128)S(1)}, f32[128,1536]{1,0:T(8,128)}, u32[]{:S(2)}) copy-start(f32[128,1536]{1,0:T(8,128)} %copy-done.4) | copy-start | bytes 2359300
  198.2 7.4 %collective-permute-start.17 = (bf16[128,768]{1,0:T(8,128)(2,1)S(1)}, bf16[128,768]{1,0:T(8,128)(2,1)S(1)}, u32[]{:S(2)}, u32[]{:S(2)}) collective-permute-start(bf16[128,768]{1,0:T(8,128)(2,1)S(1)} %get-tuple-element.35), channel_id=1, source_target_pairs={{0,16},{8,72},{16,0},{24,88},{32,48},{40,104},{48,32},{56,120},{64... | collective-permute-start | bytes 589832 | tf_op jit(solution)/shard_map/ppermute | solution.py:60
  199.7 7.7 %collective-permute-start.18 = (bf16[128,768]{1,0:T(8,128)(2,1)S(1)}, bf16[128,768]{1,0:T(8,128)(2,1)S(1)}, u32[]{:S(2)}, u32[]{:S(2)}) collective-permute-start(bf16[128,768]{1,0:T(8,128)(2,1)S(1)} %get-tuple-element.34), channel_id=1, source_target_pairs={{0,48},{8,200},{16,32},{24,216},{32,16},{40,232},{48,0},{56,248},{... | collective-permute-start | bytes 589832 | tf_op jit(solution)/shard_map/ppermute | solution.py:60
  201.8 7.3 %collective-permute-start.19 = (bf16[128,768]{1,0:T(8,128)(2,1)S(1)}, bf16[128,768]{1,0:T(8,128)(2,1)S(1)}, u32[]{:S(2)}, u32[]{:S(2)}) collective-permute-start(bf16[128,768]{1,0:T(8,128)(2,1)S(1)} %get-tuple-element.33), channel_id=1, source_target_pairs={{0,32},{8,136},{16,48},{24,152},{32,0},{40,168},{48,16},{56,184},{... | collective-permute-start | bytes 589832 | tf_op jit(solution)/shard_map/ppermute | solution.py:60
  202.6 8.5 %collective-permute-start.11 = (bf16[128,768]{1,0:T(8,128)(2,1)S(1)}, bf16[128,768]{1,0:T(8,128)(2,1)S(1)}, u32[]{:S(2)}, u32[]{:S(2)}) collective-permute-start(bf16[128,768]{1,0:T(8,128)(2,1)S(1)} %get-tuple-element.39), channel_id=1, source_target_pairs={{0,48},{8,200},{16,32},{24,216},{32,16},{40,232},{48,0},{56,248},{... | collective-permute-start | bytes 589832 | tf_op jit(solution)/shard_map/ppermute | solution.py:60
  205.3 5.8 %collective-permute-start.12 = (bf16[128,768]{1,0:T(8,128)(2,1)S(1)}, bf16[128,768]{1,0:T(8,128)(2,1)S(1)}, u32[]{:S(2)}, u32[]{:S(2)}) collective-permute-start(bf16[128,768]{1,0:T(8,128)(2,1)S(1)} %get-tuple-element.38), channel_id=1, source_target_pairs={{0,16},{8,72},{16,0},{24,88},{32,48},{40,104},{48,32},{56,120},{64... | collective-permute-start | bytes 589832 | tf_op jit(solution)/shard_map/ppermute | solution.py:60
  205.6 7.6 %collective-permute-start.13 = (bf16[128,768]{1,0:T(8,128)(2,1)S(1)}, bf16[128,768]{1,0:T(8,128)(2,1)S(1)}, u32[]{:S(2)}, u32[]{:S(2)}) collective-permute-start(bf16[128,768]{1,0:T(8,128)(2,1)S(1)} %get-tuple-element.37), channel_id=1, source_target_pairs={{0,32},{8,136},{16,48},{24,152},{32,0},{40,168},{48,16},{56,184},{... | collective-permute-start | bytes 589832 | tf_op jit(solution)/shard_map/ppermute | solution.py:60
  (3 other events, 4.1 us)
Sparse Core Ops, SparseCore 0:
  43.6 108.2 all-gather.2

commit v5 on v4

--- a/solution.py
+++ b/solution.py
@@ -69,24 +69,32 @@
 
 
 def join_kernel(*refs):
-    shards, joined, sems = refs[:-2], refs[-2], refs[-1]
-    copies = [
-        pltpu.make_async_copy(shard, joined.at[n], sems.at[n]) for n, shard in enumerate(shards)
-    ]
-    for copy in copies:
+    count = len(refs) - 3
+    shards, joined, held, sems = refs[:count], refs[count], refs[count + 1], refs[count + 2]
+    inward = [
+        pltpu.make_async_copy(shard, held.at[n], sems.at[0, n]) for n, shard in enumerate(shards)
+    ]
+    outward = [
+        pltpu.make_async_copy(held.at[n], joined.at[n], sems.at[1, n]) for n in range(count)
+    ]
+    for copy in inward:
         copy.start()
-    for copy in copies:
+    for n in range(count):
+        inward[n].wait()
+        outward[n].start()
+    for copy in outward:
         copy.wait()
 
 
 def join(*shards):
     hbm = pl.BlockSpec(memory_space=pltpu.HBM)
+    shape = (len(shards), *shards[0].shape)
     return pl.pallas_call(
         join_kernel,
         in_specs=[hbm] * len(shards),
         out_specs=hbm,
-        out_shape=jax.ShapeDtypeStruct((len(shards), *shards[0].shape), BF16),
-        scratch_shapes=[pltpu.SemaphoreType.DMA((len(shards),))],
+        out_shape=jax.ShapeDtypeStruct(shape, BF16),
+        scratch_shapes=[pltpu.VMEM(shape, BF16), pltpu.SemaphoreType.DMA((2, len(shards)))],
         name="join",
     )(*shards)
 
@@ -363,10 +371,7 @@
 
 def closing_kernel(hidden_ref, gain_ref, *refs):
     parts, out_ref = refs[:-1], refs[-1]
-    moe = jnp.concatenate(
-        [sum(ref[...].astype(F32) for ref in parts[4 * g : 4 * g + 4]) for g in range(GROUPS)],
-        axis=1,
-    )
+    moe = sum(ref[...].astype(F32) for ref in parts)
     mixed = hidden_ref[...] + moe
     mean_sq = jnp.mean(mixed * mixed, axis=-1, keepdims=True)
     out_ref[...] = (mixed * lax.rsqrt(mean_sq + EPS) * gain_ref[...]).astype(BF16)
@@ -416,16 +421,17 @@
     ]
     *sends, act = experts(place, packed, scale, spread, weights)
     keeps = kept(place, act, spread, weights)
-    parts = []
+    sums = []
     for group, (first, other) in enumerate(PLANS):
         last, soon = sends[2 * group : 2 * group + 2]
         held, passed = keeps[2 * group : 2 * group + 2]
         passed = add(passed, turned(soon, first, True))
         held = add(held, turned(last, first, True))
         got = turned(passed, other, True)
-        sums = [add(held[i], got[i]) for i in range(4)]
-        turns = (other, first, first ^ other)
-        parts += [sums[0]] + [turned(sums[i + 1], turn, False) for i, turn in enumerate(turns)]
+        at = {0: 0, other: 1, first: 2, first ^ other: 3}
+        sums.append([add(held[at[turn]], got[at[turn]]) for turn in range(4)])
+    parts = [jnp.concatenate(both, axis=1) for both in zip(*sums)]
+    parts = parts[:1] + [turned(parts[turn], turn, False) for turn in (2, 1, 3)]
     return closing(hidden, norm2_gain.reshape(1, D), parts)
 
 

time: 223 us -> 189 us (0.85)
  Pallas kernels: 72.1 us -> 37.4 us
  waiting for transfers between devices: 98.7 us -> 106 us
  starting transfers between devices: 28 us -> 22.7 us
    pallas_call x1, Pallas kernels: 36.9 us -> 2.22 us  [join(): pl.pallas_call(join_kernel, in_specs=[hbm] * len(shards), out_specs=hbm,...]
    ppermute x20 -> x17, waiting for transfers between devices: 65.3 us -> 71.9 us  [turned(): return lax.ppermute(rows, ('x', 'y', 'core'), pairs)]
    ppermute x20 -> x17, starting transfers between devices: 27.9 us -> 22.7 us  [turned(): return lax.ppermute(rows, ('x', 'y', 'core'), pairs)]
  transfers between devices with their start and end apart: 21 -> 18, of which waited for: 14 -> 16; matrix products, arithmetic and copies ran while one was open for 1% -> 1% of each run, Pallas kernels for 8% -> 9%
where the time goes in v5:
time: 189 us; the launch traced here: 188 us
  waiting for transfers between devices  106 us (56%)
  Pallas kernels  37.4 us (20%)
  starting transfers between devices  22.7 us (12%)
  between operations  13.7 us (7%)
  local copies, waits for them, and re-layouts  6.84 us (4%)
  other arithmetic  1.93 us (1%)
    ppermute x17, waiting for transfers between devices, turned(): return lax.ppermute(rows, ('x', 'y', 'core'), pairs)  71.9 us
    all_gather x1, waiting for transfers between devices, body(): weights = lax.all_gather(joined, ('core', 'blk'), axis=0, tiled=False)  33.6 us
    ppermute x17, starting transfers between devices, turned(): return lax.ppermute(rows, ('x', 'y', 'core'), pairs)  22.7 us
    pallas_call x1, Pallas kernels, experts(): pl.pallas_call(experts_kernel, in_specs=[pl.BlockSpec(memory_space=pltpu....  16.4 us
    pallas_call x1, Pallas kernels, compact(): pl.pallas_call(compact_kernel, in_specs=[pl.BlockSpec(memory_space=pltpu....  8.71 us
    unnamed x28, local copies, waits for them, and re-layouts  6.8 us
    pallas_call x1, Pallas kernels, kept(): pl.pallas_call(kept_kernel, in_specs=[pl.BlockSpec(memory_space=pltpu.SME...  5.58 us
  transfers between devices with their start and end apart: 18, of which 16 were waited for; matrix products, arithmetic and copies ran while one was open for 1% of the time, Pallas kernels for 9%

profile of v5, /device:TPU:6, one launch (start us, length us, event | category | flops | bytes accessed | tf_op | source)
XLA Modules:
  0.0 188.1 jit_solution(10087472549802693548)
XLA Ops:
  6.6 2.2 %join.1 = bf16[3,2,192,512]{3,2,1,0:T(8,128)(2,1)} custom-call(bf16[2,192,512]{2,1,0:T(8,128)(2,1)} %refs_0_.1, bf16[2,192,512]{2,1,0:T(8,128)(2,1)} %refs_1_.1, bf16[2,192,512]{2,1,0:T(8,128)(2,1)} %refs_2_.1), custom_call_target="tpu_custom_call" | custom-call | tf_op jit(solution)/shard_map/join/pallas_call | solution.py:92
  9.0 2.3 %copy-done.1 = bf16[1536,1536]{1,0:T(8,128)(2,1)S(1)} copy-done((bf16[1536,1536]{1,0:T(8,128)(2,1)S(1)}, bf16[1536,1536]{1,0:T(8,128)(2,1)}, u32[]{:S(2)}) %copy-start.1) | copy-done | bytes 4718616
  11.3 3.4 %entry.1 = (f32[128,1536]{1,0:T(8,128)S(1)}, bf16[2,144,768]{2,1,0:T(8,128)(2,1)S(1)}) custom-call(bf16[128,1536]{1,0:T(8,128)(2,1)S(1)} %copy-done.6, bf16[128,1536]{1,0:T(8,128)(2,1)S(1)} %copy-done.7, bf16[1536,1536]{1,0:T(8,128)(2,1)S(1)} %copy-done.1, f32[1,1536]{1,0:T(1,128)S(1)} %reshape.47.gain_ref, f32[40,1536]{1,0:T(8,128)S(1)} %bitcast.24, ...), custom_call_target="tpu_custom_call" | custom-call | tf_op jit(solution)/shard_map/entry/pallas_call | solution.py:151
  14.7 1.7 collective-permute-start.4
  16.4 2.2 %collective-permute-start = (bf16[1,144,768]{2,1,0:T(8,128)(2,1)S(1)}, bf16[1,144,768]{2,1,0:T(8,128)(2,1)S(1)}, u32[]{:S(2)}, u32[]{:S(2)}) collective-permute-start(bf16[1,144,768]{2,1,0:T(8,128)(2,1)S(1)} %get-tuple-element.42), channel_id=1, source_target_pairs={{0,48},{8,200},{16,32},{24,216},{32,16},{40,232},{48,0},{56,248},{... | collective-permute-start | bytes 663560 | tf_op jit(solution)/shard_map/ppermute | solution.py:60
  18.6 2.2 %collective-permute-done.4 = bf16[1,144,768]{2,1,0:T(8,128)(2,1)S(1)} collective-permute-done((bf16[1,144,768]{2,1,0:T(8,128)(2,1)S(1)}, bf16[1,144,768]{2,1,0:T(8,128)(2,1)S(1)}, u32[]{:S(2)}, u32[]{:S(2)}) %collective-permute-start.4) | collective-permute-done | bytes 221216 | tf_op jit(solution)/shard_map/ppermute | solution.py:60
  20.8 3.1 %collective-permute-start.5 = (bf16[2,144,768]{2,1,0:T(8,128)(2,1)S(1)}, bf16[2,144,768]{2,1,0:T(8,128)(2,1)S(1)}, u32[]{:S(2)}, u32[]{:S(2)}) collective-permute-start(bf16[2,144,768]{2,1,0:T(8,128)(2,1)S(1)} %pad_maximum_fusion.5), channel_id=1, source_target_pairs={{0,48},{8,200},{16,32},{24,216},{32,16},{40,232},{48,0},{56,248},{... | collective-permute-start | bytes 1327112 | tf_op jit(solution)/shard_map/ppermute | solution.py:60
  24.2 6.2 %collective-permute-done.5 = bf16[2,144,768]{2,1,0:T(8,128)(2,1)S(1)} collective-permute-done((bf16[2,144,768]{2,1,0:T(8,128)(2,1)S(1)}, bf16[2,144,768]{2,1,0:T(8,128)(2,1)S(1)}, u32[]{:S(2)}, u32[]{:S(2)}) %collective-permute-start.5) | collective-permute-done | bytes 442400 | tf_op jit(solution)/shard_map/ppermute | solution.py:60
  31.4 1.8 collective-permute-done.1
  34.0 9.6 %collective-permute-done.6 = bf16[4,144,768]{2,1,0:T(8,128)(2,1)S(1)} collective-permute-done((bf16[4,144,768]{2,1,0:T(8,128)(2,1)S(1)}, bf16[4,144,768]{2,1,0:T(8,128)(2,1)S(1)}, u32[]{:S(2)}, u32[]{:S(2)}) %collective-permute-start.6) | collective-permute-done | bytes 884768 | tf_op jit(solution)/shard_map/ppermute | solution.py:60
  43.8 2.3 %collective-permute-start.7 = (bf16[8,144,768]{2,1,0:T(8,128)(2,1)S(1)}, bf16[8,144,768]{2,1,0:T(8,128)(2,1)}, u32[]{:S(2)}, u32[]{:S(2)}) collective-permute-start(bf16[8,144,768]{2,1,0:T(8,128)(2,1)S(1)} %pad_maximum_fusion.1.refs_2_), channel_id=1, source_target_pairs={{0,192},{8,56},{16,208},{24,40},{32,224},{40,24},{48,240},{56,8},{... | collective-permute-start | bytes 5308424 | tf_op jit(solution)/shard_map/ppermute | solution.py:60
  46.1 1.5 collective-permute-done.2
  49.0 18.8 %collective-permute-done.7.refs_3_ = bf16[8,144,768]{2,1,0:T(8,128)(2,1)} collective-permute-done((bf16[8,144,768]{2,1,0:T(8,128)(2,1)S(1)}, bf16[8,144,768]{2,1,0:T(8,128)(2,1)}, u32[]{:S(2)}, u32[]{:S(2)}) %collective-permute-start.7) | collective-permute-done | bytes 1769504 | tf_op jit(solution)/shard_map/ppermute | solution.py:60
  67.7 3.0 %collective-permute-done.3.refs_1_ = bf16[8,144,768]{2,1,0:T(8,128)(2,1)} collective-permute-done((bf16[8,144,768]{2,1,0:T(8,128)(2,1)S(1)}, bf16[8,144,768]{2,1,0:T(8,128)(2,1)}, u32[]{:S(2)}, u32[]{:S(2)}) %collective-permute-start.3) | collective-permute-done | bytes 1769504 | tf_op jit(solution)/shard_map/ppermute | solution.py:60
  70.7 8.7 %compact.1 = (bf16[4,16,32,1536]{3,2,1,0:T(8,128)(2,1)S(1)}, bf16[16,128,128]{2,1,0:T(8,128)(2,1)S(1)}, f32[4,16,32,1]{3,2,1,0:T(8,128)S(1)}) custom-call(s32[3]{0:T(128)S(1)} %pad_add_fusion.place_ref, bf16[8,144,768]{2,1,0:T(8,128)(2,1)S(1)} %pad_maximum_fusion.refs_0_, bf16[8,144,768]{2,1,0:T(8,128)(2,1)} %collective-permute-done.3.refs_1_, ...), custom_call_target="tpu_custom_call" | custom-call | tf_op jit(solution)/shard_map/compact/pallas_call | solution.py:225
  79.4 2.6 %copy-done = bf16[4,16,32,1536]{3,2,1,0:T(8,128)(2,1)} copy-done((bf16[4,16,32,1536]{3,2,1,0:T(8,128)(2,1)}, bf16[4,16,32,1536]{3,2,1,0:T(8,128)(2,1)S(1)}, u32[]{:S(2)}) %copy-start) | copy-done | bytes 6291480
  83.9 33.6 %all-gather.3.cloned.1.call-done = bf16[48,2,192,512]{3,2,1,0:T(8,128)(2,1)} async-done(((bf16[3,2,192,512]{3,2,1,0:T(8,128)(2,1)}), bf16[48,2,192,512]{3,2,1,0:T(8,128)(2,1)}) %all-gather.3.cloned.1.call-update) | async-done | bytes 18874384 | tf_op jit(solution)/shard_map/all_gather | solution.py:408
  117.5 16.4 %experts.1 = (bf16[4,128,768]{2,1,0:T(8,128)(2,1)S(1)}, bf16[4,128,768]{2,1,0:T(8,128)(2,1)S(1)}, bf16[4,128,768]{2,1,0:T(8,128)(2,1)S(1)}, bf16[4,128,768]{2,1,0:T(8,128)(2,1)S(1)}, bf16[4,16,32,512]{3,2,1,0:T(8,128)(2,1)S(1)}) custom-call(s32[3]{0:T(128)S(1)} %pad_add_fusion.place_ref, bf16[4,16,32,1536]{3,2,1,0:T(8,128)(2,1)} %copy-done, ...), custom_call_target="tpu_custom_call" | custom-call | tf_op jit(solution)/shard_map/experts/pallas_call | solution.py:309
  134.8 1.2 collective-permute-start.12
  136.0 5.6 %kept.1 = (bf16[4,128,768]{2,1,0:T(8,128)(2,1)S(1)}, bf16[4,128,768]{2,1,0:T(8,128)(2,1)S(1)}, bf16[4,128,768]{2,1,0:T(8,128)(2,1)S(1)}, bf16[4,128,768]{2,1,0:T(8,128)(2,1)S(1)}) custom-call(s32[3]{0:T(128)S(1)} %pad_add_fusion.place_ref, bf16[4,16,32,512]{3,2,1,0:T(8,128)(2,1)S(1)} %get-tuple-element.24.act_ref, bf16[16,128,128]{2,1,0:T(8,128)(2,1)} %copy-done.2, ...), custom_call_target="tpu_custom_call" | custom-call | tf_op jit(solution)/shard_map/kept/pallas_call | solution.py:356
  141.6 2.7 %collective-permute-start.11 = (bf16[4,128,768]{2,1,0:T(8,128)(2,1)S(1)}, bf16[4,128,768]{2,1,0:T(8,128)(2,1)S(1)}, u32[]{:S(2)}, u32[]{:S(2)}) collective-permute-start(bf16[4,128,768]{2,1,0:T(8,128)(2,1)S(1)} %get-tuple-element.30), channel_id=1, source_target_pairs={{0,192},{8,56},{16,208},{24,40},{32,224},{40,24},{48,240},{56,8},{... | collective-permute-start | bytes 2359304 | tf_op jit(solution)/shard_map/ppermute | solution.py:60
  144.3 1.6 collective-permute-done.9
  146.8 1.2 collective-permute-done.12
  148.3 6.1 %collective-permute-done.8 = bf16[4,128,768]{2,1,0:T(8,128)(2,1)S(1)} collective-permute-done((bf16[4,128,768]{2,1,0:T(8,128)(2,1)S(1)}, bf16[4,128,768]{2,1,0:T(8,128)(2,1)S(1)}, u32[]{:S(2)}, u32[]{:S(2)}) %collective-permute-start.8) | collective-permute-done | bytes 786464 | tf_op jit(solution)/shard_map/ppermute | solution.py:60
  154.5 1.9 collective-permute-done.11
  156.6 8.2 %collective-permute-done.10 = bf16[4,128,768]{2,1,0:T(8,128)(2,1)S(1)} collective-permute-done((bf16[4,128,768]{2,1,0:T(8,128)(2,1)S(1)}, bf16[4,128,768]{2,1,0:T(8,128)(2,1)S(1)}, u32[]{:S(2)}, u32[]{:S(2)}) %collective-permute-start.10) | collective-permute-done | bytes 786464 | tf_op jit(solution)/shard_map/ppermute | solution.py:60
  165.3 2.9 %collective-permute-start.16 = (bf16[128,1536]{1,0:T(8,128)(2,1)S(1)}, bf16[128,1536]{1,0:T(8,128)(2,1)S(1)}, u32[]{:S(2)}, u32[]{:S(2)}) collective-permute-start(bf16[128,1536]{1,0:T(8,128)(2,1)S(1)} %pad_maximum_fusion.9), channel_id=1, source_target_pairs={{0,48},{8,200},{16,32},{24,216},{32,16},{40,232},{48,0},{56,248},{... | collective-permute-start | bytes 1179656 | tf_op jit(solution)/shard_map/ppermute | solution.py:60
  168.5 1.8 collective-permute-start.14
  170.4 4.0 %collective-permute-done.16.refs_3_ = bf16[128,1536]{1,0:T(8,128)(2,1)S(1)} collective-permute-done((bf16[128,1536]{1,0:T(8,128)(2,1)S(1)}, bf16[128,1536]{1,0:T(8,128)(2,1)S(1)}, u32[]{:S(2)}, u32[]{:S(2)}) %collective-permute-start.16) | collective-permute-done | bytes 393248 | tf_op jit(solution)/shard_map/ppermute | solution.py:60
  174.4 1.7 collective-permute-done.15.refs_2_
  176.1 4.1 %collective-permute-done.14.refs_1_ = bf16[128,1536]{1,0:T(8,128)(2,1)S(1)} collective-permute-done((bf16[128,1536]{1,0:T(8,128)(2,1)S(1)}, bf16[128,1536]{1,0:T(8,128)(2,1)S(1)}, u32[]{:S(2)}, u32[]{:S(2)}) %collective-permute-start.14) | collective-permute-done | bytes 393248 | tf_op jit(solution)/shard_map/ppermute | solution.py:60
  180.2 1.1 closing.1
  (59 shorter events, 8.7 us)
Async XLA Ops:
  6.5 2.3 %copy-start.12 = (f32[1536]{0:T(1024)S(1)}, f32[1536]{0:T(1024)}, u32[]{:S(2)}) copy-start(f32[1536]{0:T(1024)} %param.15) | copy-start | bytes 18436
  6.5 2.4 %copy-start.8 = (f32[1536,40]{0,1:T(8,128)S(1)}, f32[1536,40]{0,1:T(8,128)}, u32[]{:S(2)}) copy-start(f32[1536,40]{0,1:T(8,128)} %param.16) | copy-start | bytes 737284
  6.5 2.4 %copy-start.9 = (s32[128,8]{0,1:T(8,128)S(1)}, s32[128,8]{0,1:T(8,128)}, u32[]{:S(2)}) copy-start(s32[128,8]{0,1:T(8,128)} %param.17) | copy-start | bytes 12292
  6.5 2.4 %copy-start.10 = (s32[64]{0:T(128)S(1)}, s32[64]{0:T(128)}, u32[]{:S(2)}) copy-start(s32[64]{0:T(128)} %param.18) | copy-start | bytes 772
  6.5 2.4 %copy-start.11 = (s32[128]{0:T(128)S(1)}, s32[128]{0:T(128)}, u32[]{:S(2)}) copy-start(s32[128]{0:T(128)} %param.19) | copy-start | bytes 1540
  6.5 2.4 %copy-start.6 = (bf16[128,1536]{1,0:T(8,128)(2,1)S(1)}, bf16[128,1536]{1,0:T(8,128)(2,1)}, u32[]{:S(2)}) copy-start(bf16[128,1536]{1,0:T(8,128)(2,1)} %attn_ref.1) | copy-start | bytes 1179652
  6.6 2.4 %copy-start.7 = (bf16[128,1536]{1,0:T(8,128)(2,1)S(1)}, bf16[128,1536]{1,0:T(8,128)(2,1)}, u32[]{:S(2)}) copy-start(bf16[128,1536]{1,0:T(8,128)(2,1)} %resid_ref.1) | copy-start | bytes 1179652
  6.6 110.9 %all-gather.3.cloned.1.call-start = ((), (), s32[]{:S(2)}) async-start(), calls=%async_computation | async-start | bytes 20054016 | tf_op jit(solution)/shard_map/all_gather | solution.py:408
  9.0 2.3 %copy-start.1 = (bf16[1536,1536]{1,0:T(8,128)(2,1)S(1)}, bf16[1536,1536]{1,0:T(8,128)(2,1)}, u32[]{:S(2)}) copy-start(bf16[1536,1536]{1,0:T(8,128)(2,1)} %wo_ref.1) | copy-start | bytes 14155780
  14.7 15.8 %copy-start.4 = (f32[128,1536]{1,0:T(8,128)}, f32[128,1536]{1,0:T(8,128)S(1)}, u32[]{:S(2)}) copy-start(f32[128,1536]{1,0:T(8,128)S(1)} %get-tuple-element.19.hidden_ref) | copy-start | bytes 2359300
  14.7 6.0 %collective-permute-start.4 = (bf16[1,144,768]{2,1,0:T(8,128)(2,1)S(1)}, bf16[1,144,768]{2,1,0:T(8,128)(2,1)S(1)}, u32[]{:S(2)}, u32[]{:S(2)}) collective-permute-start(bf16[1,144,768]{2,1,0:T(8,128)(2,1)S(1)} %get-tuple-element.41), channel_id=1, source_target_pairs={{0,16},{8,72},{16,0},{24,88},{32,48},{40,104},{48,32},{56,120},{64... | collective-permute-start | bytes 663560 | tf_op jit(solution)/shard_map/ppermute | solution.py:60
  16.4 7.5 %collective-permute-start = (bf16[1,144,768]{2,1,0:T(8,128)(2,1)S(1)}, bf16[1,144,768]{2,1,0:T(8,128)(2,1)S(1)}, u32[]{:S(2)}, u32[]{:S(2)}) collective-permute-start(bf16[1,144,768]{2,1,0:T(8,128)(2,1)S(1)} %get-tuple-element.42), channel_id=1, source_target_pairs={{0,48},{8,200},{16,32},{24,216},{32,16},{40,232},{48,0},{56,248},{... | collective-permute-start | bytes 663560 | tf_op jit(solution)/shard_map/ppermute | solution.py:60
  20.8 9.6 %collective-permute-start.5 = (bf16[2,144,768]{2,1,0:T(8,128)(2,1)S(1)}, bf16[2,144,768]{2,1,0:T(8,128)(2,1)S(1)}, u32[]{:S(2)}, u32[]{:S(2)}) collective-permute-start(bf16[2,144,768]{2,1,0:T(8,128)(2,1)S(1)} %pad_maximum_fusion.5), channel_id=1, source_target_pairs={{0,48},{8,200},{16,32},{24,216},{32,16},{40,232},{48,0},{56,248},{... | collective-permute-start | bytes 1327112 | tf_op jit(solution)/shard_map/ppermute | solution.py:60
  24.0 9.3 %collective-permute-start.1 = (bf16[2,144,768]{2,1,0:T(8,128)(2,1)S(1)}, bf16[2,144,768]{2,1,0:T(8,128)(2,1)S(1)}, u32[]{:S(2)}, u32[]{:S(2)}) collective-permute-start(bf16[2,144,768]{2,1,0:T(8,128)(2,1)S(1)} %pad_maximum_fusion.4), channel_id=1, source_target_pairs={{0,16},{8,72},{16,0},{24,88},{32,48},{40,104},{48,32},{56,120},{64... | collective-permute-start | bytes 1327112 | tf_op jit(solution)/shard_map/ppermute | solution.py:60
  30.5 13.1 %collective-permute-start.6 = (bf16[4,144,768]{2,1,0:T(8,128)(2,1)S(1)}, bf16[4,144,768]{2,1,0:T(8,128)(2,1)S(1)}, u32[]{:S(2)}, u32[]{:S(2)}) collective-permute-start(bf16[4,144,768]{2,1,0:T(8,128)(2,1)S(1)} %pad_maximum_fusion.3), channel_id=1, source_target_pairs={{0,64},{8,24},{16,80},{24,8},{32,96},{40,56},{48,112},{56,40},{64,... | collective-permute-start | bytes 2654216 | tf_op jit(solution)/shard_map/ppermute | solution.py:60
  33.3 14.3 %collective-permute-start.2 = (bf16[4,144,768]{2,1,0:T(8,128)(2,1)S(1)}, bf16[4,144,768]{2,1,0:T(8,128)(2,1)S(1)}, u32[]{:S(2)}, u32[]{:S(2)}) collective-permute-start(bf16[4,144,768]{2,1,0:T(8,128)(2,1)S(1)} %pad_maximum_fusion.2), channel_id=1, source_target_pairs={{0,192},{8,56},{16,208},{24,40},{32,224},{40,24},{48,240},{56,8},{... | collective-permute-start | bytes 2654216 | tf_op jit(solution)/shard_map/ppermute | solution.py:60
  43.8 23.9 %collective-permute-start.7 = (bf16[8,144,768]{2,1,0:T(8,128)(2,1)S(1)}, bf16[8,144,768]{2,1,0:T(8,128)(2,1)}, u32[]{:S(2)}, u32[]{:S(2)}) collective-permute-start(bf16[8,144,768]{2,1,0:T(8,128)(2,1)S(1)} %pad_maximum_fusion.1.refs_2_), channel_id=1, source_target_pairs={{0,192},{8,56},{16,208},{24,40},{32,224},{40,24},{48,240},{56,8},{... | collective-permute-start | bytes 5308424 | tf_op jit(solution)/shard_map/ppermute | solution.py:60
  47.8 22.9 %collective-permute-start.3 = (bf16[8,144,768]{2,1,0:T(8,128)(2,1)S(1)}, bf16[8,144,768]{2,1,0:T(8,128)(2,1)}, u32[]{:S(2)}, u32[]{:S(2)}) collective-permute-start(bf16[8,144,768]{2,1,0:T(8,128)(2,1)S(1)} %pad_maximum_fusion.refs_0_), channel_id=1, source_target_pairs={{0,64},{8,24},{16,80},{24,8},{32,96},{40,56},{48,112},{56,40},{64,... | collective-permute-start | bytes 5308424 | tf_op jit(solution)/shard_map/ppermute | solution.py:60
  79.4 2.7 %copy-start = (bf16[4,16,32,1536]{3,2,1,0:T(8,128)(2,1)}, bf16[4,16,32,1536]{3,2,1,0:T(8,128)(2,1)S(1)}, u32[]{:S(2)}) copy-start(bf16[4,16,32,1536]{3,2,1,0:T(8,128)(2,1)S(1)} %get-tuple-element.21.packed_hbm) | copy-start | bytes 18874372
  82.1 0.8 copy-start.2
  82.9 1.0 copy-start.3
  133.9 12.1 %collective-permute-start.9 = (bf16[4,128,768]{2,1,0:T(8,128)(2,1)S(1)}, bf16[4,128,768]{2,1,0:T(8,128)(2,1)S(1)}, u32[]{:S(2)}, u32[]{:S(2)}) collective-permute-start(bf16[4,128,768]{2,1,0:T(8,128)(2,1)S(1)} %get-tuple-element.28), channel_id=1, source_target_pairs={{0,64},{8,24},{16,80},{24,8},{32,96},{40,56},{48,112},{56,40},{64,... | collective-permute-start | bytes 2359304 | tf_op jit(solution)/shard_map/ppermute | solution.py:60
  134.8 13.2 %collective-permute-start.12 = (bf16[4,128,768]{2,1,0:T(8,128)(2,1)S(1)}, bf16[4,128,768]{2,1,0:T(8,128)(2,1)S(1)}, u32[]{:S(2)}, u32[]{:S(2)}) collective-permute-start(bf16[4,128,768]{2,1,0:T(8,128)(2,1)S(1)} %get-tuple-element.32), channel_id=1, source_target_pairs={{0,192},{8,56},{16,208},{24,40},{32,224},{40,24},{48,240},{56,8},{... | collective-permute-start | bytes 2359304 | tf_op jit(solution)/shard_map/ppermute | solution.py:60
  136.0 18.4 %collective-permute-start.8 = (bf16[4,128,768]{2,1,0:T(8,128)(2,1)S(1)}, bf16[4,128,768]{2,1,0:T(8,128)(2,1)S(1)}, u32[]{:S(2)}, u32[]{:S(2)}) collective-permute-start(bf16[4,128,768]{2,1,0:T(8,128)(2,1)S(1)} %get-tuple-element.26), channel_id=1, source_target_pairs={{0,64},{8,24},{16,80},{24,8},{32,96},{40,56},{48,112},{56,40},{64,... | collective-permute-start | bytes 2359304 | tf_op jit(solution)/shard_map/ppermute | solution.py:60
  141.6 14.9 %collective-permute-start.11 = (bf16[4,128,768]{2,1,0:T(8,128)(2,1)S(1)}, bf16[4,128,768]{2,1,0:T(8,128)(2,1)S(1)}, u32[]{:S(2)}, u32[]{:S(2)}) collective-permute-start(bf16[4,128,768]{2,1,0:T(8,128)(2,1)S(1)} %get-tuple-element.30), channel_id=1, source_target_pairs={{0,192},{8,56},{16,208},{24,40},{32,224},{40,24},{48,240},{56,8},{... | collective-permute-start | bytes 2359304 | tf_op jit(solution)/shard_map/ppermute | solution.py:60
  146.1 18.7 %collective-permute-start.10 = (bf16[4,128,768]{2,1,0:T(8,128)(2,1)S(1)}, bf16[4,128,768]{2,1,0:T(8,128)(2,1)S(1)}, u32[]{:S(2)}, u32[]{:S(2)}) collective-permute-start(bf16[4,128,768]{2,1,0:T(8,128)(2,1)S(1)} %add_convert_fusion.2), channel_id=1, source_target_pairs={{0,192},{8,56},{16,208},{24,40},{32,224},{40,24},{48,240},{56,8},{... | collective-permute-start | bytes 2359304 | tf_op jit(solution)/shard_map/ppermute | solution.py:60
  148.2 16.9 %collective-permute-start.13 = (bf16[4,128,768]{2,1,0:T(8,128)(2,1)S(1)}, bf16[4,128,768]{2,1,0:T(8,128)(2,1)S(1)}, u32[]{:S(2)}, u32[]{:S(2)}) collective-permute-start(bf16[4,128,768]{2,1,0:T(8,128)(2,1)S(1)} %add_convert_fusion), channel_id=1, source_target_pairs={{0,64},{8,24},{16,80},{24,8},{32,96},{40,56},{48,112},{56,40},{64,... | collective-permute-start | bytes 2359304 | tf_op jit(solution)/shard_map/ppermute | solution.py:60
  165.2 5.1 %copy-start.13 = (f32[1536]{0:T(1024)S(1)}, f32[1536]{0:T(1024)}, u32[]{:S(2)}) copy-start(f32[1536]{0:T(1024)} %param.23) | copy-start | bytes 18436
  165.2 14.9 %copy-start.5 = (f32[128,1536]{1,0:T(8,128)S(1)}, f32[128,1536]{1,0:T(8,128)}, u32[]{:S(2)}) copy-start(f32[128,1536]{1,0:T(8,128)} %copy-done.4) | copy-start | bytes 2359300
  165.3 9.1 %collective-permute-start.16 = (bf16[128,1536]{1,0:T(8,128)(2,1)S(1)}, bf16[128,1536]{1,0:T(8,128)(2,1)S(1)}, u32[]{:S(2)}, u32[]{:S(2)}) collective-permute-start(bf16[128,1536]{1,0:T(8,128)(2,1)S(1)} %pad_maximum_fusion.9), channel_id=1, source_target_pairs={{0,48},{8,200},{16,32},{24,216},{32,16},{40,232},{48,0},{56,248},{... | collective-permute-start | bytes 1179656 | tf_op jit(solution)/shard_map/ppermute | solution.py:60
  168.2 7.9 %collective-permute-start.15 = (bf16[128,1536]{1,0:T(8,128)(2,1)S(1)}, bf16[128,1536]{1,0:T(8,128)(2,1)S(1)}, u32[]{:S(2)}, u32[]{:S(2)}) collective-permute-start(bf16[128,1536]{1,0:T(8,128)(2,1)S(1)} %pad_maximum_fusion.8), channel_id=1, source_target_pairs={{0,16},{8,72},{16,0},{24,88},{32,48},{40,104},{48,32},{56,120},{64... | collective-permute-start | bytes 1179656 | tf_op jit(solution)/shard_map/ppermute | solution.py:60
  168.5 11.7 %collective-permute-start.14 = (bf16[128,1536]{1,0:T(8,128)(2,1)S(1)}, bf16[128,1536]{1,0:T(8,128)(2,1)S(1)}, u32[]{:S(2)}, u32[]{:S(2)}) collective-permute-start(bf16[128,1536]{1,0:T(8,128)(2,1)S(1)} %pad_maximum_fusion.7), channel_id=1, source_target_pairs={{0,32},{8,136},{16,48},{24,152},{32,0},{40,168},{48,16},{56,184},{... | collective-permute-start | bytes 1179656 | tf_op jit(solution)/shard_map/ppermute | solution.py:60
Sparse Core Ops, SparseCore 0:
  9.2 108.1 all-gather.2

commit v6 on v5

--- a/solution.py
+++ b/solution.py
@@ -280,11 +280,14 @@
     ]
     scales = fetch(scale_hbm, scale_ref, once_sems.at[0])
     spreads = fetch(spread_hbm, spread_ref, once_sems.at[1])
-    for copy in (*by_slot[0], scales, *by_slot[1], *by_slot[2], *by_slot[3], *by_group, spreads):
+    queue = [by_slot[0], [scales, *by_slot[1]], by_slot[2], by_slot[3], [*by_group, spreads]]
+    for copy in (*queue[0], *queue[1]):
         copy.start()
     for s in range(LOCAL):
         by_slot[s][0].wait()
         by_slot[s][1].wait()
+        for copy in queue[s + 2] if s + 2 < len(queue) else ():
+            copy.start()
         rows = packed_ref[s].reshape(BLOCKS * CAP, D)
         gate = jnp.dot(rows, gate_ref[s].reshape(D, FF), preferred_element_type=F32)
         by_slot[s][2].wait()

time: 189 us -> 186 us (0.984)
  Pallas kernels: 37.4 us -> 35 us
    pallas_call x1, Pallas kernels: 16.4 us -> 14 us  [experts(): pl.pallas_call(experts_kernel, in_specs=[pl.BlockSpec(memory_space=pltpu....]
  transfers between devices with their start and end apart: 18 -> 18, of which waited for: 16 -> 16; matrix products, arithmetic and copies ran while one was open for 1% -> 1% of each run, Pallas kernels for 9% -> 10%
where the time goes in v6:
time: 186 us
  waiting for transfers between devices  106 us (57%)
  Pallas kernels  35 us (19%)
  starting transfers between devices  22.7 us (12%)
  between operations  13.7 us (7%)
  local copies, waits for them, and re-layouts  6.84 us (4%)
  other arithmetic  1.93 us (1%)
    ppermute x17, waiting for transfers between devices, turned(): return lax.ppermute(rows, ('x', 'y', 'core'), pairs)  71.9 us
    all_gather x1, waiting for transfers between devices, body(): weights = lax.all_gather(joined, ('core', 'blk'), axis=0, tiled=False)  33.6 us
    ppermute x17, starting transfers between devices, turned(): return lax.ppermute(rows, ('x', 'y', 'core'), pairs)  22.7 us
    pallas_call x1, Pallas kernels, experts(): pl.pallas_call(experts_kernel, in_specs=[pl.BlockSpec(memory_space=pltpu....  14 us
    pallas_call x1, Pallas kernels, compact(): pl.pallas_call(compact_kernel, in_specs=[pl.BlockSpec(memory_space=pltpu....  8.71 us
    unnamed x28, local copies, waits for them, and re-layouts  6.8 us
    pallas_call x1, Pallas kernels, kept(): pl.pallas_call(kept_kernel, in_specs=[pl.BlockSpec(memory_space=pltpu.SME...  5.58 us
  transfers between devices with their start and end apart: 18, of which 16 were waited for; matrix products, arithmetic and copies ran while one was open for 1% of the time, Pallas kernels for 10%

profile of v6, /device:TPU:6, one launch (start us, length us, event | category | flops | bytes accessed | tf_op | source)
XLA Modules:
  0.0 185.7 jit_solution(7215584992150853308)
XLA Ops:
  6.6 2.2 %join.1 = bf16[3,2,192,512]{3,2,1,0:T(8,128)(2,1)} custom-call(bf16[2,192,512]{2,1,0:T(8,128)(2,1)} %refs_0_.1, bf16[2,192,512]{2,1,0:T(8,128)(2,1)} %refs_1_.1, bf16[2,192,512]{2,1,0:T(8,128)(2,1)} %refs_2_.1), custom_call_target="tpu_custom_call" | custom-call | tf_op jit(solution)/shard_map/join/pallas_call | solution.py:92
  9.0 2.3 %copy-done.1 = bf16[1536,1536]{1,0:T(8,128)(2,1)S(1)} copy-done((bf16[1536,1536]{1,0:T(8,128)(2,1)S(1)}, bf16[1536,1536]{1,0:T(8,128)(2,1)}, u32[]{:S(2)}) %copy-start.1) | copy-done | bytes 4718616
  11.3 3.4 %entry.1 = (f32[128,1536]{1,0:T(8,128)S(1)}, bf16[2,144,768]{2,1,0:T(8,128)(2,1)S(1)}) custom-call(bf16[128,1536]{1,0:T(8,128)(2,1)S(1)} %copy-done.6, bf16[128,1536]{1,0:T(8,128)(2,1)S(1)} %copy-done.7, bf16[1536,1536]{1,0:T(8,128)(2,1)S(1)} %copy-done.1, f32[1,1536]{1,0:T(1,128)S(1)} %reshape.47.gain_ref, f32[40,1536]{1,0:T(8,128)S(1)} %bitcast.24, ...), custom_call_target="tpu_custom_call" | custom-call | tf_op jit(solution)/shard_map/entry/pallas_call | solution.py:151
  14.7 1.7 collective-permute-start.4
  16.4 2.2 %collective-permute-start = (bf16[1,144,768]{2,1,0:T(8,128)(2,1)S(1)}, bf16[1,144,768]{2,1,0:T(8,128)(2,1)S(1)}, u32[]{:S(2)}, u32[]{:S(2)}) collective-permute-start(bf16[1,144,768]{2,1,0:T(8,128)(2,1)S(1)} %get-tuple-element.42), channel_id=1, source_target_pairs={{0,48},{8,200},{16,32},{24,216},{32,16},{40,232},{48,0},{56,248},{... | collective-permute-start | bytes 663560 | tf_op jit(solution)/shard_map/ppermute | solution.py:60
  18.6 2.2 %collective-permute-done.4 = bf16[1,144,768]{2,1,0:T(8,128)(2,1)S(1)} collective-permute-done((bf16[1,144,768]{2,1,0:T(8,128)(2,1)S(1)}, bf16[1,144,768]{2,1,0:T(8,128)(2,1)S(1)}, u32[]{:S(2)}, u32[]{:S(2)}) %collective-permute-start.4) | collective-permute-done | bytes 221216 | tf_op jit(solution)/shard_map/ppermute | solution.py:60
  20.8 3.1 %collective-permute-start.5 = (bf16[2,144,768]{2,1,0:T(8,128)(2,1)S(1)}, bf16[2,144,768]{2,1,0:T(8,128)(2,1)S(1)}, u32[]{:S(2)}, u32[]{:S(2)}) collective-permute-start(bf16[2,144,768]{2,1,0:T(8,128)(2,1)S(1)} %pad_maximum_fusion.5), channel_id=1, source_target_pairs={{0,48},{8,200},{16,32},{24,216},{32,16},{40,232},{48,0},{56,248},{... | collective-permute-start | bytes 1327112 | tf_op jit(solution)/shard_map/ppermute | solution.py:60
  24.2 6.2 %collective-permute-done.5 = bf16[2,144,768]{2,1,0:T(8,128)(2,1)S(1)} collective-permute-done((bf16[2,144,768]{2,1,0:T(8,128)(2,1)S(1)}, bf16[2,144,768]{2,1,0:T(8,128)(2,1)S(1)}, u32[]{:S(2)}, u32[]{:S(2)}) %collective-permute-start.5) | collective-permute-done | bytes 442400 | tf_op jit(solution)/shard_map/ppermute | solution.py:60
  31.4 1.8 collective-permute-done.1
  34.0 9.6 %collective-permute-done.6 = bf16[4,144,768]{2,1,0:T(8,128)(2,1)S(1)} collective-permute-done((bf16[4,144,768]{2,1,0:T(8,128)(2,1)S(1)}, bf16[4,144,768]{2,1,0:T(8,128)(2,1)S(1)}, u32[]{:S(2)}, u32[]{:S(2)}) %collective-permute-start.6) | collective-permute-done | bytes 884768 | tf_op jit(solution)/shard_map/ppermute | solution.py:60
  43.8 2.3 %collective-permute-start.7 = (bf16[8,144,768]{2,1,0:T(8,128)(2,1)S(1)}, bf16[8,144,768]{2,1,0:T(8,128)(2,1)}, u32[]{:S(2)}, u32[]{:S(2)}) collective-permute-start(bf16[8,144,768]{2,1,0:T(8,128)(2,1)S(1)} %pad_maximum_fusion.1.refs_2_), channel_id=1, source_target_pairs={{0,192},{8,56},{16,208},{24,40},{32,224},{40,24},{48,240},{56,8},{... | collective-permute-start | bytes 5308424 | tf_op jit(solution)/shard_map/ppermute | solution.py:60
  46.1 1.5 collective-permute-done.2
  49.0 18.8 %collective-permute-done.7.refs_3_ = bf16[8,144,768]{2,1,0:T(8,128)(2,1)} collective-permute-done((bf16[8,144,768]{2,1,0:T(8,128)(2,1)S(1)}, bf16[8,144,768]{2,1,0:T(8,128)(2,1)}, u32[]{:S(2)}, u32[]{:S(2)}) %collective-permute-start.7) | collective-permute-done | bytes 1769504 | tf_op jit(solution)/shard_map/ppermute | solution.py:60
  67.7 3.0 %collective-permute-done.3.refs_1_ = bf16[8,144,768]{2,1,0:T(8,128)(2,1)} collective-permute-done((bf16[8,144,768]{2,1,0:T(8,128)(2,1)S(1)}, bf16[8,144,768]{2,1,0:T(8,128)(2,1)}, u32[]{:S(2)}, u32[]{:S(2)}) %collective-permute-start.3) | collective-permute-done | bytes 1769504 | tf_op jit(solution)/shard_map/ppermute | solution.py:60
  70.7 8.7 %compact.1 = (bf16[4,16,32,1536]{3,2,1,0:T(8,128)(2,1)S(1)}, bf16[16,128,128]{2,1,0:T(8,128)(2,1)S(1)}, f32[4,16,32,1]{3,2,1,0:T(8,128)S(1)}) custom-call(s32[3]{0:T(128)S(1)} %pad_add_fusion.place_ref, bf16[8,144,768]{2,1,0:T(8,128)(2,1)S(1)} %pad_maximum_fusion.refs_0_, bf16[8,144,768]{2,1,0:T(8,128)(2,1)} %collective-permute-done.3.refs_1_, ...), custom_call_target="tpu_custom_call" | custom-call | tf_op jit(solution)/shard_map/compact/pallas_call | solution.py:225
  79.4 2.6 %copy-done = bf16[4,16,32,1536]{3,2,1,0:T(8,128)(2,1)} copy-done((bf16[4,16,32,1536]{3,2,1,0:T(8,128)(2,1)}, bf16[4,16,32,1536]{3,2,1,0:T(8,128)(2,1)S(1)}, u32[]{:S(2)}) %copy-start) | copy-done | bytes 6291480
  83.9 33.6 %all-gather.3.cloned.1.call-done = bf16[48,2,192,512]{3,2,1,0:T(8,128)(2,1)} async-done(((bf16[3,2,192,512]{3,2,1,0:T(8,128)(2,1)}), bf16[48,2,192,512]{3,2,1,0:T(8,128)(2,1)}) %all-gather.3.cloned.1.call-update) | async-done | bytes 18874384 | tf_op jit(solution)/shard_map/all_gather | solution.py:411
  117.5 14.0 %experts.1 = (bf16[4,128,768]{2,1,0:T(8,128)(2,1)S(1)}, bf16[4,128,768]{2,1,0:T(8,128)(2,1)S(1)}, bf16[4,128,768]{2,1,0:T(8,128)(2,1)S(1)}, bf16[4,128,768]{2,1,0:T(8,128)(2,1)S(1)}, bf16[4,16,32,512]{3,2,1,0:T(8,128)(2,1)S(1)}) custom-call(s32[3]{0:T(128)S(1)} %pad_add_fusion.place_ref, bf16[4,16,32,1536]{3,2,1,0:T(8,128)(2,1)} %copy-done, ...), custom_call_target="tpu_custom_call" | custom-call | tf_op jit(solution)/shard_map/experts/pallas_call | solution.py:312
  132.4 1.2 collective-permute-start.12
  133.6 5.6 %kept.1 = (bf16[4,128,768]{2,1,0:T(8,128)(2,1)S(1)}, bf16[4,128,768]{2,1,0:T(8,128)(2,1)S(1)}, bf16[4,128,768]{2,1,0:T(8,128)(2,1)S(1)}, bf16[4,128,768]{2,1,0:T(8,128)(2,1)S(1)}) custom-call(s32[3]{0:T(128)S(1)} %pad_add_fusion.place_ref, bf16[4,16,32,512]{3,2,1,0:T(8,128)(2,1)S(1)} %get-tuple-element.24.act_ref, bf16[16,128,128]{2,1,0:T(8,128)(2,1)} %copy-done.2, ...), custom_call_target="tpu_custom_call" | custom-call | tf_op jit(solution)/shard_map/kept/pallas_call | solution.py:359
  139.2 2.7 %collective-permute-start.11 = (bf16[4,128,768]{2,1,0:T(8,128)(2,1)S(1)}, bf16[4,128,768]{2,1,0:T(8,128)(2,1)S(1)}, u32[]{:S(2)}, u32[]{:S(2)}) collective-permute-start(bf16[4,128,768]{2,1,0:T(8,128)(2,1)S(1)} %get-tuple-element.30), channel_id=1, source_target_pairs={{0,192},{8,56},{16,208},{24,40},{32,224},{40,24},{48,240},{56,8},{... | collective-permute-start | bytes 2359304 | tf_op jit(solution)/shard_map/ppermute | solution.py:60
  141.9 1.6 collective-permute-done.9
  144.4 1.2 collective-permute-done.12
  145.9 6.1 %collective-permute-done.8 = bf16[4,128,768]{2,1,0:T(8,128)(2,1)S(1)} collective-permute-done((bf16[4,128,768]{2,1,0:T(8,128)(2,1)S(1)}, bf16[4,128,768]{2,1,0:T(8,128)(2,1)S(1)}, u32[]{:S(2)}, u32[]{:S(2)}) %collective-permute-start.8) | collective-permute-done | bytes 786464 | tf_op jit(solution)/shard_map/ppermute | solution.py:60
  152.2 1.9 %collective-permute-done.11 = bf16[4,128,768]{2,1,0:T(8,128)(2,1)S(1)} collective-permute-done((bf16[4,128,768]{2,1,0:T(8,128)(2,1)S(1)}, bf16[4,128,768]{2,1,0:T(8,128)(2,1)S(1)}, u32[]{:S(2)}, u32[]{:S(2)}) %collective-permute-start.11) | collective-permute-done | bytes 786464 | tf_op jit(solution)/shard_map/ppermute | solution.py:60
  154.2 8.2 %collective-permute-done.10 = bf16[4,128,768]{2,1,0:T(8,128)(2,1)S(1)} collective-permute-done((bf16[4,128,768]{2,1,0:T(8,128)(2,1)S(1)}, bf16[4,128,768]{2,1,0:T(8,128)(2,1)S(1)}, u32[]{:S(2)}, u32[]{:S(2)}) %collective-permute-start.10) | collective-permute-done | bytes 786464 | tf_op jit(solution)/shard_map/ppermute | solution.py:60
  162.9 2.9 %collective-permute-start.16 = (bf16[128,1536]{1,0:T(8,128)(2,1)S(1)}, bf16[128,1536]{1,0:T(8,128)(2,1)S(1)}, u32[]{:S(2)}, u32[]{:S(2)}) collective-permute-start(bf16[128,1536]{1,0:T(8,128)(2,1)S(1)} %pad_maximum_fusion.9), channel_id=1, source_target_pairs={{0,48},{8,200},{16,32},{24,216},{32,16},{40,232},{48,0},{56,248},{... | collective-permute-start | bytes 1179656 | tf_op jit(solution)/shard_map/ppermute | solution.py:60
  166.1 1.8 collective-permute-start.14
  168.0 4.0 %collective-permute-done.16.refs_3_ = bf16[128,1536]{1,0:T(8,128)(2,1)S(1)} collective-permute-done((bf16[128,1536]{1,0:T(8,128)(2,1)S(1)}, bf16[128,1536]{1,0:T(8,128)(2,1)S(1)}, u32[]{:S(2)}, u32[]{:S(2)}) %collective-permute-start.16) | collective-permute-done | bytes 393248 | tf_op jit(solution)/shard_map/ppermute | solution.py:60
  172.0 1.7 collective-permute-done.15.refs_2_
  173.7 4.1 %collective-permute-done.14.refs_1_ = bf16[128,1536]{1,0:T(8,128)(2,1)S(1)} collective-permute-done((bf16[128,1536]{1,0:T(8,128)(2,1)S(1)}, bf16[128,1536]{1,0:T(8,128)(2,1)S(1)}, u32[]{:S(2)}, u32[]{:S(2)}) %collective-permute-start.14) | collective-permute-done | bytes 393248 | tf_op jit(solution)/shard_map/ppermute | solution.py:60
  177.8 1.1 closing.1
  (59 shorter events, 8.7 us)
Async XLA Ops:
  6.5 2.3 %copy-start.12 = (f32[1536]{0:T(1024)S(1)}, f32[1536]{0:T(1024)}, u32[]{:S(2)}) copy-start(f32[1536]{0:T(1024)} %param.15) | copy-start | bytes 18436
  6.5 2.4 %copy-start.8 = (f32[1536,40]{0,1:T(8,128)S(1)}, f32[1536,40]{0,1:T(8,128)}, u32[]{:S(2)}) copy-start(f32[1536,40]{0,1:T(8,128)} %param.16) | copy-start | bytes 737284
  6.5 2.4 %copy-start.9 = (s32[128,8]{0,1:T(8,128)S(1)}, s32[128,8]{0,1:T(8,128)}, u32[]{:S(2)}) copy-start(s32[128,8]{0,1:T(8,128)} %param.17) | copy-start | bytes 12292
  6.5 2.4 %copy-start.10 = (s32[64]{0:T(128)S(1)}, s32[64]{0:T(128)}, u32[]{:S(2)}) copy-start(s32[64]{0:T(128)} %param.18) | copy-start | bytes 772
  6.5 2.4 %copy-start.11 = (s32[128]{0:T(128)S(1)}, s32[128]{0:T(128)}, u32[]{:S(2)}) copy-start(s32[128]{0:T(128)} %param.19) | copy-start | bytes 1540
  6.5 2.4 %copy-start.6 = (bf16[128,1536]{1,0:T(8,128)(2,1)S(1)}, bf16[128,1536]{1,0:T(8,128)(2,1)}, u32[]{:S(2)}) copy-start(bf16[128,1536]{1,0:T(8,128)(2,1)} %attn_ref.1) | copy-start | bytes 1179652
  6.6 2.4 %copy-start.7 = (bf16[128,1536]{1,0:T(8,128)(2,1)S(1)}, bf16[128,1536]{1,0:T(8,128)(2,1)}, u32[]{:S(2)}) copy-start(bf16[128,1536]{1,0:T(8,128)(2,1)} %resid_ref.1) | copy-start | bytes 1179652
  6.6 110.9 %all-gather.3.cloned.1.call-start = ((), (), s32[]{:S(2)}) async-start(), calls=%async_computation | async-start | bytes 20054016 | tf_op jit(solution)/shard_map/all_gather | solution.py:411
  9.0 2.3 %copy-start.1 = (bf16[1536,1536]{1,0:T(8,128)(2,1)S(1)}, bf16[1536,1536]{1,0:T(8,128)(2,1)}, u32[]{:S(2)}) copy-start(bf16[1536,1536]{1,0:T(8,128)(2,1)} %wo_ref.1) | copy-start | bytes 14155780
  14.7 15.8 %copy-start.4 = (f32[128,1536]{1,0:T(8,128)}, f32[128,1536]{1,0:T(8,128)S(1)}, u32[]{:S(2)}) copy-start(f32[128,1536]{1,0:T(8,128)S(1)} %get-tuple-element.19.hidden_ref) | copy-start | bytes 2359300
  14.7 6.0 %collective-permute-start.4 = (bf16[1,144,768]{2,1,0:T(8,128)(2,1)S(1)}, bf16[1,144,768]{2,1,0:T(8,128)(2,1)S(1)}, u32[]{:S(2)}, u32[]{:S(2)}) collective-permute-start(bf16[1,144,768]{2,1,0:T(8,128)(2,1)S(1)} %get-tuple-element.41), channel_id=1, source_target_pairs={{0,16},{8,72},{16,0},{24,88},{32,48},{40,104},{48,32},{56,120},{64... | collective-permute-start | bytes 663560 | tf_op jit(solution)/shard_map/ppermute | solution.py:60
  16.4 7.5 %collective-permute-start = (bf16[1,144,768]{2,1,0:T(8,128)(2,1)S(1)}, bf16[1,144,768]{2,1,0:T(8,128)(2,1)S(1)}, u32[]{:S(2)}, u32[]{:S(2)}) collective-permute-start(bf16[1,144,768]{2,1,0:T(8,128)(2,1)S(1)} %get-tuple-element.42), channel_id=1, source_target_pairs={{0,48},{8,200},{16,32},{24,216},{32,16},{40,232},{48,0},{56,248},{... | collective-permute-start | bytes 663560 | tf_op jit(solution)/shard_map/ppermute | solution.py:60
  20.8 9.6 %collective-permute-start.5 = (bf16[2,144,768]{2,1,0:T(8,128)(2,1)S(1)}, bf16[2,144,768]{2,1,0:T(8,128)(2,1)S(1)}, u32[]{:S(2)}, u32[]{:S(2)}) collective-permute-start(bf16[2,144,768]{2,1,0:T(8,128)(2,1)S(1)} %pad_maximum_fusion.5), channel_id=1, source_target_pairs={{0,48},{8,200},{16,32},{24,216},{32,16},{40,232},{48,0},{56,248},{... | collective-permute-start | bytes 1327112 | tf_op jit(solution)/shard_map/ppermute | solution.py:60
  24.0 9.3 %collective-permute-start.1 = (bf16[2,144,768]{2,1,0:T(8,128)(2,1)S(1)}, bf16[2,144,768]{2,1,0:T(8,128)(2,1)S(1)}, u32[]{:S(2)}, u32[]{:S(2)}) collective-permute-start(bf16[2,144,768]{2,1,0:T(8,128)(2,1)S(1)} %pad_maximum_fusion.4), channel_id=1, source_target_pairs={{0,16},{8,72},{16,0},{24,88},{32,48},{40,104},{48,32},{56,120},{64... | collective-permute-start | bytes 1327112 | tf_op jit(solution)/shard_map/ppermute | solution.py:60
  30.5 13.1 %collective-permute-start.6 = (bf16[4,144,768]{2,1,0:T(8,128)(2,1)S(1)}, bf16[4,144,768]{2,1,0:T(8,128)(2,1)S(1)}, u32[]{:S(2)}, u32[]{:S(2)}) collective-permute-start(bf16[4,144,768]{2,1,0:T(8,128)(2,1)S(1)} %pad_maximum_fusion.3), channel_id=1, source_target_pairs={{0,64},{8,24},{16,80},{24,8},{32,96},{40,56},{48,112},{56,40},{64,... | collective-permute-start | bytes 2654216 | tf_op jit(solution)/shard_map/ppermute | solution.py:60
  33.3 14.3 %collective-permute-start.2 = (bf16[4,144,768]{2,1,0:T(8,128)(2,1)S(1)}, bf16[4,144,768]{2,1,0:T(8,128)(2,1)S(1)}, u32[]{:S(2)}, u32[]{:S(2)}) collective-permute-start(bf16[4,144,768]{2,1,0:T(8,128)(2,1)S(1)} %pad_maximum_fusion.2), channel_id=1, source_target_pairs={{0,192},{8,56},{16,208},{24,40},{32,224},{40,24},{48,240},{56,8},{... | collective-permute-start | bytes 2654216 | tf_op jit(solution)/shard_map/ppermute | solution.py:60
  43.8 23.9 %collective-permute-start.7 = (bf16[8,144,768]{2,1,0:T(8,128)(2,1)S(1)}, bf16[8,144,768]{2,1,0:T(8,128)(2,1)}, u32[]{:S(2)}, u32[]{:S(2)}) collective-permute-start(bf16[8,144,768]{2,1,0:T(8,128)(2,1)S(1)} %pad_maximum_fusion.1.refs_2_), channel_id=1, source_target_pairs={{0,192},{8,56},{16,208},{24,40},{32,224},{40,24},{48,240},{56,8},{... | collective-permute-start | bytes 5308424 | tf_op jit(solution)/shard_map/ppermute | solution.py:60
  47.8 22.9 %collective-permute-start.3 = (bf16[8,144,768]{2,1,0:T(8,128)(2,1)S(1)}, bf16[8,144,768]{2,1,0:T(8,128)(2,1)}, u32[]{:S(2)}, u32[]{:S(2)}) collective-permute-start(bf16[8,144,768]{2,1,0:T(8,128)(2,1)S(1)} %pad_maximum_fusion.refs_0_), channel_id=1, source_target_pairs={{0,64},{8,24},{16,80},{24,8},{32,96},{40,56},{48,112},{56,40},{64,... | collective-permute-start | bytes 5308424 | tf_op jit(solution)/shard_map/ppermute | solution.py:60
  79.4 2.7 %copy-start = (bf16[4,16,32,1536]{3,2,1,0:T(8,128)(2,1)}, bf16[4,16,32,1536]{3,2,1,0:T(8,128)(2,1)S(1)}, u32[]{:S(2)}) copy-start(bf16[4,16,32,1536]{3,2,1,0:T(8,128)(2,1)S(1)} %get-tuple-element.21.packed_hbm) | copy-start | bytes 18874372
  82.1 0.8 copy-start.2
  82.9 1.0 copy-start.3
  131.5 12.1 %collective-permute-start.9 = (bf16[4,128,768]{2,1,0:T(8,128)(2,1)S(1)}, bf16[4,128,768]{2,1,0:T(8,128)(2,1)S(1)}, u32[]{:S(2)}, u32[]{:S(2)}) collective-permute-start(bf16[4,128,768]{2,1,0:T(8,128)(2,1)S(1)} %get-tuple-element.28), channel_id=1, source_target_pairs={{0,64},{8,24},{16,80},{24,8},{32,96},{40,56},{48,112},{56,40},{64,... | collective-permute-start | bytes 2359304 | tf_op jit(solution)/shard_map/ppermute | solution.py:60
  132.4 13.2 %collective-permute-start.12 = (bf16[4,128,768]{2,1,0:T(8,128)(2,1)S(1)}, bf16[4,128,768]{2,1,0:T(8,128)(2,1)S(1)}, u32[]{:S(2)}, u32[]{:S(2)}) collective-permute-start(bf16[4,128,768]{2,1,0:T(8,128)(2,1)S(1)} %get-tuple-element.32), channel_id=1, source_target_pairs={{0,192},{8,56},{16,208},{24,40},{32,224},{40,24},{48,240},{56,8},{... | collective-permute-start | bytes 2359304 | tf_op jit(solution)/shard_map/ppermute | solution.py:60
  133.6 18.4 %collective-permute-start.8 = (bf16[4,128,768]{2,1,0:T(8,128)(2,1)S(1)}, bf16[4,128,768]{2,1,0:T(8,128)(2,1)S(1)}, u32[]{:S(2)}, u32[]{:S(2)}) collective-permute-start(bf16[4,128,768]{2,1,0:T(8,128)(2,1)S(1)} %get-tuple-element.26), channel_id=1, source_target_pairs={{0,64},{8,24},{16,80},{24,8},{32,96},{40,56},{48,112},{56,40},{64,... | collective-permute-start | bytes 2359304 | tf_op jit(solution)/shard_map/ppermute | solution.py:60
  139.2 14.9 %collective-permute-start.11 = (bf16[4,128,768]{2,1,0:T(8,128)(2,1)S(1)}, bf16[4,128,768]{2,1,0:T(8,128)(2,1)S(1)}, u32[]{:S(2)}, u32[]{:S(2)}) collective-permute-start(bf16[4,128,768]{2,1,0:T(8,128)(2,1)S(1)} %get-tuple-element.30), channel_id=1, source_target_pairs={{0,192},{8,56},{16,208},{24,40},{32,224},{40,24},{48,240},{56,8},{... | collective-permute-start | bytes 2359304 | tf_op jit(solution)/shard_map/ppermute | solution.py:60
  143.7 18.7 %collective-permute-start.10 = (bf16[4,128,768]{2,1,0:T(8,128)(2,1)S(1)}, bf16[4,128,768]{2,1,0:T(8,128)(2,1)S(1)}, u32[]{:S(2)}, u32[]{:S(2)}) collective-permute-start(bf16[4,128,768]{2,1,0:T(8,128)(2,1)S(1)} %add_convert_fusion.2), channel_id=1, source_target_pairs={{0,192},{8,56},{16,208},{24,40},{32,224},{40,24},{48,240},{56,8},{... | collective-permute-start | bytes 2359304 | tf_op jit(solution)/shard_map/ppermute | solution.py:60
  145.8 16.9 %collective-permute-start.13 = (bf16[4,128,768]{2,1,0:T(8,128)(2,1)S(1)}, bf16[4,128,768]{2,1,0:T(8,128)(2,1)S(1)}, u32[]{:S(2)}, u32[]{:S(2)}) collective-permute-start(bf16[4,128,768]{2,1,0:T(8,128)(2,1)S(1)} %add_convert_fusion), channel_id=1, source_target_pairs={{0,64},{8,24},{16,80},{24,8},{32,96},{40,56},{48,112},{56,40},{64,... | collective-permute-start | bytes 2359304 | tf_op jit(solution)/shard_map/ppermute | solution.py:60
  162.8 5.1 %copy-start.13 = (f32[1536]{0:T(1024)S(1)}, f32[1536]{0:T(1024)}, u32[]{:S(2)}) copy-start(f32[1536]{0:T(1024)} %param.23) | copy-start | bytes 18436
  162.9 14.9 %copy-start.5 = (f32[128,1536]{1,0:T(8,128)S(1)}, f32[128,1536]{1,0:T(8,128)}, u32[]{:S(2)}) copy-start(f32[128,1536]{1,0:T(8,128)} %copy-done.4) | copy-start | bytes 2359300
  162.9 9.1 %collective-permute-start.16 = (bf16[128,1536]{1,0:T(8,128)(2,1)S(1)}, bf16[128,1536]{1,0:T(8,128)(2,1)S(1)}, u32[]{:S(2)}, u32[]{:S(2)}) collective-permute-start(bf16[128,1536]{1,0:T(8,128)(2,1)S(1)} %pad_maximum_fusion.9), channel_id=1, source_target_pairs={{0,48},{8,200},{16,32},{24,216},{32,16},{40,232},{48,0},{56,248},{... | collective-permute-start | bytes 1179656 | tf_op jit(solution)/shard_map/ppermute | solution.py:60
  165.8 7.9 %collective-permute-start.15 = (bf16[128,1536]{1,0:T(8,128)(2,1)S(1)}, bf16[128,1536]{1,0:T(8,128)(2,1)S(1)}, u32[]{:S(2)}, u32[]{:S(2)}) collective-permute-start(bf16[128,1536]{1,0:T(8,128)(2,1)S(1)} %pad_maximum_fusion.8), channel_id=1, source_target_pairs={{0,16},{8,72},{16,0},{24,88},{32,48},{40,104},{48,32},{56,120},{64... | collective-permute-start | bytes 1179656 | tf_op jit(solution)/shard_map/ppermute | solution.py:60
  166.1 11.7 %collective-permute-start.14 = (bf16[128,1536]{1,0:T(8,128)(2,1)S(1)}, bf16[128,1536]{1,0:T(8,128)(2,1)S(1)}, u32[]{:S(2)}, u32[]{:S(2)}) collective-permute-start(bf16[128,1536]{1,0:T(8,128)(2,1)S(1)} %pad_maximum_fusion.7), channel_id=1, source_target_pairs={{0,32},{8,136},{16,48},{24,152},{32,0},{40,168},{48,16},{56,184},{... | collective-permute-start | bytes 1179656 | tf_op jit(solution)/shard_map/ppermute | solution.py:60
Sparse Core Ops, SparseCore 0:
  9.2 108.1 all-gather.2
